TPU v7x, 32 devices: a whole 2x2x4 slice. The times are simulated.
32 devices in a mesh: rows: 8 (over z, y), mk: 4 (over x, core).
Axes of the slice: x: 2, y: 2, z: 4, core: 2. Of those that a mesh axis runs over, the one named last changes fastest.
Arguments:
- solution_animal: float32 [6, 131072], P(None, ('rows', 'mk')), may hold values from -6 to 6
- solution_marker: float32 [6, 49152], P(None, 'mk'), may hold values from -6 to 6
- residual_animal: float32 [6, 131072], P(None, ('rows', 'mk')), may hold values from -6 to 6
- residual_marker: float32 [6, 49152], P(None, 'mk'), may hold values from -6 to 6
- direction_animal: float32 [6, 131072], P(None, ('rows', 'mk')), may hold values from -6 to 6
- direction_marker: float32 [6, 49152], P(None, 'mk'), may hold values from -6 to 6
- scaling_animal: float32 [6, 131072], P(None, ('rows', 'mk')), may hold values from 0.3 to 9, as said below
- scaling_marker: float32 [6, 49152], P(None, 'mk'), may hold values from 0.3 to 3
- previous_product: float32 [], replicated, may hold values from 943718.4 to 3932160
- genotypes: bfloat16 [3072, 49152], P('rows', 'mk'), may hold values from -0.0390625 to 0.0390625
- genetic_inverse: float32 [6, 6], replicated, may hold values from -0.28 to 4, as said below
- genomic_inverse: float32 [6, 6], replicated, may hold values from -0.28 to 4, as said below
- marker_inverse: float32 [6, 6], replicated, may hold values from -0.28 to 4, as said below
- residual_table: float32 [64, 6, 6], replicated, may hold values from -0.28 to 4, as said below
- pattern: int32 [131072], P(('rows', 'mk')), may hold values from 0 to 63
- sire_slot: int32 [131072], P(('rows', 'mk')), may hold values from 0 to 2048, as said below
- dam_slot: int32 [131072], P(('rows', 'mk')), may hold values from 0 to 2048, as said below
- genotype_row: int32 [131072], P(('rows', 'mk')), may hold values from 0 to 384, as said below
- send_list: int32 [8, 4, 8, 256], P('rows', 'mk'), may hold values from 0 to 4096, as said below
Outputs:
- next_solution_animal: float32 [6, 131072], P(None, ('rows', 'mk'))
- next_solution_marker: float32 [6, 49152], P(None, 'mk')
- next_residual_animal: float32 [6, 131072], P(None, ('rows', 'mk'))
- next_residual_marker: float32 [6, 49152], P(None, 'mk')
- reduction: float32 [], replicated
Inputs may be any that keep to these rules, and one draw needn't show every extreme that they name: `send_list`: used entries are distinct local animal indices of the owner; 4096 marks an empty slot, and empty slots only follow used ones. Every device's list to itself is full, and in every column some receiving row gets full lists from all owners. `sire_slot`: points at a used slot of the parent lists sent to the animal's device, or is 8 * 256 for an unknown sire. `dam_slot`: points at a used slot of the parent lists sent to the animal's device, or is 8 * 256 for an unknown dam. `genotype_row`: within the animals of one rows block, each value below 384 occurs exactly once; 384 marks an animal without genotypes. `scaling_animal`: Positive. `genetic_inverse`: symmetric and strictly diagonally dominant with positive diagonal. `genomic_inverse`: symmetric and strictly diagonally dominant with positive diagonal. `marker_inverse`: symmetric and strictly diagonally dominant with positive diagonal. `residual_table`: entry p is symmetric, zero in the rows and columns of traits whose bit of p is 0, and strictly diagonally dominant on the others.
All inputs are finite; a program needn't handle non-finite values.
Results may differ from a plain program's by a relative error of at most 0.00045.
Values sent between devices are 32-bit elements; how exact they have to be, the bound alone decides.
No kernel may reach another device: no remote copies, remote signals or barrier semaphores. Data moves between devices by JAX's collectives and lax.ppermute only.
A program may use at most 128 MiB of HBM per device.

v0:
```python
import jax
import jax.numpy as jnp
from jax import lax
from jax.sharding import PartitionSpec as P

precise = lax.Precision.HIGHEST


def local(
    solution_animal,
    solution_marker,
    residual_animal,
    residual_marker,
    direction_animal,
    direction_marker,
    scaling_animal,
    scaling_marker,
    previous_product,
    genotypes,
    genetic_inverse,
    genomic_inverse,
    marker_inverse,
    residual_table,
    pattern,
    sire_slot,
    dam_slot,
    genotype_row,
    send_list,
):
    traits = residual_animal.shape[0]
    animal_count = residual_animal.shape[1]
    row_count = lax.axis_size("rows")
    share_width = residual_marker.shape[1] // row_count
    share_start = lax.axis_index("rows") * share_width

    def marker_share_of(values):
        return lax.dynamic_slice_in_dim(values, share_start, share_width, 1)

    search_animal = scaling_animal * residual_animal
    search_marker = scaling_marker * residual_marker
    product_now, norm_before = lax.psum(
        (
            jnp.sum(residual_animal * search_animal)
            + jnp.sum(marker_share_of(residual_marker) * marker_share_of(search_marker)),
            jnp.sum(residual_animal * residual_animal)
            + jnp.sum(marker_share_of(residual_marker) ** 2),
        ),
        ("rows", "mk"),
    )
    conjugacy = product_now / previous_product
    new_animal = search_animal + conjugacy * direction_animal
    new_marker = search_marker + conjugacy * direction_marker
    capacity = send_list.shape[3]
    slot_total = row_count * capacity
    outgoing_index = send_list[0, 0]
    zero_column = jnp.zeros((traits, 1), jnp.float32)
    padded = jnp.concatenate([new_animal, zero_column], axis=1)
    outgoing = padded[:, outgoing_index]
    parents = lax.all_to_all(outgoing, "rows", split_axis=1, concat_axis=1, tiled=True).reshape(
        traits, slot_total
    )
    parents = jnp.concatenate([parents, zero_column], axis=1)
    known = (sire_slot < slot_total).astype(jnp.float32) + (dam_slot < slot_total).astype(
        jnp.float32
    )
    mendel = 1.0 / (1.0 - 0.25 * known)
    sampling = mendel[None, :] * (
        new_animal - 0.5 * parents[:, sire_slot] - 0.5 * parents[:, dam_slot]
    )
    backward = jnp.zeros((traits, slot_total + 1), jnp.float32)
    backward = backward.at[:, sire_slot].add(-0.5 * sampling).at[:, dam_slot].add(-0.5 * sampling)
    returned = lax.all_to_all(
        backward[:, :slot_total].reshape(traits, row_count, capacity),
        "rows",
        split_axis=1,
        concat_axis=1,
        tiled=True,
    )
    gathered_terms = (
        jnp.zeros((traits, animal_count + 1), jnp.float32)
        .at[:, outgoing_index.reshape(-1)]
        .add(returned.reshape(traits, slot_total))
    )
    pedigree = sampling + gathered_terms[:, :animal_count]
    genotyped = genotypes.shape[0]
    placed = (
        jnp.zeros((traits, genotyped + 1), jnp.float32)
        .at[:, genotype_row]
        .add(new_animal)[:, :genotyped]
    )
    predicted = lax.dot_general(
        new_marker.astype(jnp.bfloat16),
        genotypes,
        (((1,), (1,)), ((), ())),
        preferred_element_type=jnp.float32,
    )
    difference = lax.psum(placed - predicted, "mk")
    deviation = jnp.dot(genomic_inverse, difference, precision=precise)
    genomic_term = jnp.concatenate([deviation, zero_column], axis=1)[:, genotype_row]
    patterns = residual_table.shape[0]
    one_hot = (pattern[None, :] == jnp.arange(patterns, dtype=jnp.int32)[:, None]).astype(
        jnp.float32
    )
    blocks = jnp.dot(
        residual_table.reshape(patterns, traits * traits).T, one_hot, precision=precise
    ).reshape(traits, traits, animal_count)
    record_term = jnp.sum(blocks * new_animal[None, :, :], axis=1)
    image_animal = (
        jnp.dot(genetic_inverse, pedigree, precision=precise) + record_term + genomic_term
    )
    marker_terms = lax.dot_general(
        deviation.astype(jnp.bfloat16),
        genotypes,
        (((1,), (0,)), ((), ())),
        preferred_element_type=jnp.float32,
    )
    new_share = marker_share_of(new_marker)
    residual_share = marker_share_of(residual_marker)
    summed_terms = lax.psum(marker_terms, "rows")
    image_marker = jnp.dot(marker_inverse, new_marker, precision=precise) - summed_terms
    image_share = marker_share_of(image_marker)
    curvature = lax.psum(
        jnp.sum(new_animal * image_animal) + jnp.sum(new_share * image_share), ("rows", "mk")
    )
    step_size = product_now / curvature
    next_residual_animal = residual_animal - step_size * image_animal
    next_share = residual_share - step_size * image_share
    norm_after = lax.psum(
        jnp.sum(next_residual_animal * next_residual_animal) + jnp.sum(next_share * next_share),
        ("rows", "mk"),
    )
    reduction = norm_after / norm_before
    next_residual_marker = residual_marker - step_size * image_marker
    next_solution_animal = solution_animal + step_size * new_animal
    next_solution_marker = solution_marker + step_size * new_marker
    return (
        next_solution_animal,
        next_solution_marker,
        next_residual_animal,
        next_residual_marker,
        reduction,
    )


def solution(mesh):
    return jax.shard_map(
        local,
        mesh=mesh,
        in_specs=(
            P(None, ("rows", "mk")),
            P(None, "mk"),
            P(None, ("rows", "mk")),
            P(None, "mk"),
            P(None, ("rows", "mk")),
            P(None, "mk"),
            P(None, ("rows", "mk")),
            P(None, "mk"),
            P(),
            P("rows", "mk"),
            P(),
            P(),
            P(),
            P(),
            P(("rows", "mk")),
            P(("rows", "mk")),
            P(("rows", "mk")),
            P(("rows", "mk")),
            P("rows", "mk", None, None),
        ),
        out_specs=(
            P(None, ("rows", "mk")),
            P(None, "mk"),
            P(None, ("rows", "mk")),
            P(None, "mk"),
            P(),
        ),
        check_vma=False,
    )
```

profile of v0, /device:TPU:0, one launch (start us, length us, event | category | flops | bytes accessed | tf_op | source)
XLA Modules:
  0.0 349.5 jit_solution(8003247312584046191)
XLA Ops:
  7.2 1.2 mul.103
  8.4 1.4 multiply_reduce_fusion.8
  9.8 1.6 multiply_reduce_fusion.1
  12.7 42.0 %psum.42 = f32[]{:T(128)} all-reduce(f32[]{:T(128)S(6)} %add.109), channel_id=1, replica_groups=mesh['rows'=8,'mk'=4] {'rows','mk'}, use_global_device_ids=true, to_apply=%region_2.0 | all-reduce | flops 1 | bytes 8 | tf_op jit(solution)/shard_map/psum | solution.py:41
  56.0 0.9 multiply_add_fusion.3
  56.9 0.6 copy.61
  57.6 1.5 concatenate.9.clone
  59.1 7.1 %gather_fusion = f32[2048,6]{1,0:T(8,128)S(1)} fusion(f32[6,4097]{0,1:T(8,128)} %concatenate.9.clone, s32[2048]{0:T(1024)S(1)} %broadcast_clamp_fusion.3), kind=kCustom, calls=%fused_computation | custom fusion | bytes 106496 | tf_op jit(solution)/shard_map/gather | solution.py:58
  66.2 1.0 copy.46
  67.2 5.5 %all-to-all-start = ((f32[6,8,256]{2,0,1:T(8,128)}), f32[6,8,256]{2,0,1:T(8,128)S(1)}, u32[]{:S(2)}, u32[]{:S(2)}) async-start(f32[6,8,256]{2,0,1:T(8,128)} %bitcast.2), calls=%async_computation | async-start | bytes 131072 | tf_op jit(solution)/shard_map/all_to_all | solution.py:59
  72.7 0.6 copy.55
  73.4 0.6 broadcast_clamp_fusion
  74.0 28.3 %scatter_custom_fusion.3 = f32[6,385]{0,1:T(8,128)S(1)} fusion(s32[4096]{0:T(1024)S(1)} %get-tuple-element.21, f32[4096,6]{1,0:T(8,128)S(1)} %copy.55, f32[]{:T(128)} %constant.14.clone.1), kind=kCustom, calls=%fused_computation.39 | custom fusion | flops 24576 | bytes 9244 | tf_op jit(solution)/shard_map/scatter-add | solution.py:89
  102.5 6.2 %convolution_subtract_fusion = f32[6,384]{1,0:T(8,128)S(1)} fusion(f32[6,384]{1,0:T(8,128)S(1)} %copy.60, bf16[384,12288]{1,0:T(8,128)(2,1)} %param.28, f32[6,12288]{1,0:T(8,128)S(1)} %multiply_add_fusion.1), kind=kOutput, calls=%fused_computation.15 | convolution fusion | flops 56699136 | bytes 9750528 | tf_op jit(solution)/shard_map/dot_general | solution.py:91
  108.7 10.3 %psum.43 = f32[6,384]{1,0:T(8,128)S(1)} all-reduce(f32[6,384]{1,0:T(8,128)S(1)} %convolution_subtract_fusion), channel_id=1, replica_groups=mesh['rows'=8,'mk'=4] {'mk'}, use_global_device_ids=true, to_apply=%region_8.0 | all-reduce | flops 2304 | bytes 18432 | tf_op jit(solution)/shard_map/psum | solution.py:97
  119.0 0.1 convolution_bitcast_fusion.3
  119.2 5.8 %fusion.14 = f32[6,12288]{1,0:T(8,128)} fusion(bf16[384,12288]{1,0:T(8,128)(2,1)} %param.28, f32[6,384]{1,0:T(8,128)S(1)} %convolution_bitcast_fusion.3), kind=kOutput, calls=%fused_computation.55 | convolution fusion | flops 56625408 | bytes 9741312 | tf_op jit(solution)/shard_map/dot_general | solution.py:111
  125.0 0.6 compare_select_fusion.3
  125.6 0.6 compare_select_fusion.2
  126.3 0.5 convolution_bitcast_fusion.1
  126.8 0.6 subtract_divide_fusion
  127.5 0.4 copy.47
  127.9 14.1 %gather_fusion.1 = f32[4096,6]{1,0:T(8,128)} fusion(f32[6,2049]{0,1:T(8,128)S(1)} %concatenate.10, s32[4096]{0:T(1024)S(1)} %get-tuple-element.19), kind=kCustom, calls=%fused_computation.1 | custom fusion | bytes 212992 | tf_op jit(solution)/shard_map/gather | solution.py:68
  142.0 2.2 copy.48
  144.3 14.1 %gather_fusion.2 = f32[4096,6]{1,0:T(8,128)} fusion(f32[6,2049]{0,1:T(8,128)S(1)} %concatenate.10, s32[4096]{0:T(1024)S(1)} %get-tuple-element.17), kind=kCustom, calls=%fused_computation.2 | custom fusion | bytes 212992 | tf_op jit(solution)/shard_map/gather | solution.py:68
  158.4 2.2 copy.49
  160.6 2.0 copy.50
  162.6 22.9 %scatter_custom_fusion = f32[6,2049]{0,1:T(8,128)S(1)} fusion(s32[4096]{0:T(1024)} %get-tuple-element.18, f32[4096,6]{1,0:T(8,128)} %copy.50, f32[]{:T(128)} %constant.14.clone.1), kind=kCustom, calls=%fused_computation.20 | custom fusion | flops 24576 | bytes 49688 | tf_op jit(solution)/shard_map/scatter-add | solution.py:71
  185.5 23.0 %scatter_fusion = f32[6,2049]{0,1:T(8,128)S(1)} fusion(f32[6,2049]{0,1:T(8,128)S(1)} %scatter_custom_fusion, s32[4096]{0:T(1024)S(1)} %copy-done.8, f32[4096,6]{1,0:T(8,128)} %copy.50), kind=kCustom, calls=%fused_computation.5 | custom fusion | flops 24576 | bytes 311296 | tf_op jit(solution)/shard_map/scatter-add | solution.py:71
  208.6 1.0 copy.52
  209.6 5.9 %all-to-all-start.1 = ((f32[6,8,256]{2,0,1:T(8,128)}), f32[6,8,256]{2,0,1:T(8,128)S(1)}, u32[]{:S(2)}, u32[]{:S(2)}) async-start(f32[6,8,256]{2,0,1:T(8,128)} %copy.52), calls=%async_computation.1 | async-start | bytes 131072 | tf_op jit(solution)/shard_map/all_to_all | solution.py:72
  215.4 0.3 multiply_reduce_fusion
  215.7 0.1 copy.62
  215.9 12.7 %gather_fusion.3 = f32[4096,6]{1,0:T(8,128)S(1)} fusion(f32[6,385]{0,1:T(8,128)S(1)} %concatenate.11.clone, s32[4096]{0:T(1024)} %get-tuple-element.20), kind=kCustom, calls=%fused_computation.3 | custom fusion | bytes 212992 | tf_op jit(solution)/shard_map/gather | solution.py:99
  228.6 0.6 copy.58
  229.3 1.4 copy.53
  230.6 13.5 %scatter_custom_fusion.2 = f32[6,4097]{0,1:T(8,128)S(1)} fusion(s32[2048]{0:T(1024)S(1)} %bitcast.64, f32[2048,6]{1,0:T(8,128)} %copy.53, f32[]{:T(128)} %constant.14.clone.1), kind=kCustom, calls=%fused_computation.16 | custom fusion | flops 12288 | bytes 98840 | tf_op jit(solution)/shard_map/scatter-add | solution.py:82
  244.1 1.5 slice.21
  245.6 2.3 copy.59
  247.9 0.9 multiply_reduce_fusion.3
  248.8 1.5 fusion
  250.3 0.6 multiply_reduce_fusion.7
  252.2 40.0 %psum.45 = f32[]{:T(128)} all-reduce(f32[]{:T(128)S(6)} %add.123), channel_id=1, replica_groups=mesh['rows'=8,'mk'=4] {'rows','mk'}, use_global_device_ids=true, to_apply=%region_12.0 | all-reduce | flops 1 | bytes 8 | tf_op jit(solution)/shard_map/psum | solution.py:122
  293.6 0.7 multiply_reduce_fusion.5
  294.3 1.3 multiply_reduce_fusion.2
  295.5 1.0 multiply_subtract_fusion
  299.1 0.7 multiply_add_fusion.2
  299.7 40.4 %all-reduce.3 = (f32[]{:T(128)}, f32[]{:T(128)}) all-reduce(f32[]{:T(128)S(6)} %add.126, f32[]{:T(128)S(6)} %add.127), channel_id=1, replica_groups=mesh['rows'=8,'mk'=4] {'rows','mk'}, use_global_device_ids=true, to_apply=%region_15.0 | all-reduce | flops 2 | bytes 16 | tf_op jit(solution)/shard_map/psum | solution.py:128
  (55 shorter events, 0.6 us)
Async XLA Ops:
  7.2 241.6 %copy-start = (f32[6,6]{1,0:T(8,128)S(1)}, f32[6,6]{1,0:T(8,128)}, u32[]{:S(2)}) copy-start(f32[6,6]{1,0:T(8,128)} %param.31) | copy-start | bytes 436
  7.2 50.4 %copy-start.12 = (s32[1,1,8,256]{3,2,1,0:T(8,128)S(1)}, s32[1,1,8,256]{3,2,1,0:T(8,128)}, u32[]{:S(2)}) copy-start(s32[1,1,8,256]{3,2,1,0:T(8,128)} %param.37) | copy-start | bytes 24580
  59.1 14.3 %copy-start.14 = (s32[4096]{0:T(1024)S(1)}, s32[4096]{0:T(1024)}, u32[]{:S(2)}) copy-start(s32[4096]{0:T(1024)} %param.36) | copy-start | bytes 49156
  66.2 36.2 %copy-start.4 = (f32[6,12288]{1,0:T(8,128)S(1)}, f32[6,12288]{1,0:T(8,128)}, u32[]{:S(2)}) copy-start(f32[6,12288]{1,0:T(8,128)} %param.24) | copy-start | bytes 884740
  67.2 60.3 %all-to-all-start = ((f32[6,8,256]{2,0,1:T(8,128)}), f32[6,8,256]{2,0,1:T(8,128)S(1)}, u32[]{:S(2)}, u32[]{:S(2)}) async-start(f32[6,8,256]{2,0,1:T(8,128)} %bitcast.2), calls=%async_computation | async-start | bytes 131072 | tf_op jit(solution)/shard_map/all_to_all | solution.py:59
  72.7 176.1 %all-reduce.6.cloned.1.call-start = ((), (), s32[]{:S(2)}) async-start(), calls=%async_computation.2 | async-start | bytes 786432 | tf_op jit(solution)/shard_map/psum | solution.py:119
  102.5 16.5 %copy-start.17 = (f32[6,6]{1,0:T(8,128)S(1)}, f32[6,6]{1,0:T(8,128)}, u32[]{:S(2)}) copy-start(f32[6,6]{1,0:T(8,128)} %param.30) | copy-start | bytes 436
  119.1 5.8 %copy-start.5 = (f32[6,384]{1,0:T(8,128)}, f32[6,384]{1,0:T(8,128)S(1)}, u32[]{:S(2)}) copy-start(f32[6,384]{1,0:T(8,128)S(1)} %convolution_bitcast_fusion.3) | copy-start | bytes 27652
  119.1 5.9 %copy-start.10 = (s32[4096]{0:T(1024)S(1)}, s32[4096]{0:T(1024)}, u32[]{:S(2)}) copy-start(s32[4096]{0:T(1024)} %param.34) | copy-start | bytes 49156
  119.1 6.5 %copy-start.9 = (s32[4096]{0:T(1024)S(1)}, s32[4096]{0:T(1024)}, u32[]{:S(2)}) copy-start(s32[4096]{0:T(1024)} %param.35) | copy-start | bytes 49156
  119.2 7.1 %copy-start.13 = (f32[64,6,6]{0,2,1:T(8,128)S(1)}, f32[64,6,6]{0,2,1:T(8,128)}, u32[]{:S(2)}) copy-start(f32[64,6,6]{0,2,1:T(8,128)} %param.32) | copy-start | bytes 27652
  119.2 7.1 %copy-start.15 = (s32[4096]{0:T(1024)S(1)}, s32[4096]{0:T(1024)}, u32[]{:S(2)}) copy-start(s32[4096]{0:T(1024)} %param.33) | copy-start | bytes 49156
  144.3 16.3 %copy-start.11 = (f32[4096]{0:T(1024)S(1)}, f32[4096]{0:T(1024)}, u32[]{:S(2)}) copy-start(f32[4096]{0:T(1024)} %subtract_divide_fusion) | copy-start | bytes 49156
  160.6 24.9 %copy-start.8 = (s32[4096]{0:T(1024)S(1)}, s32[4096]{0:T(1024)}, u32[]{:S(2)}) copy-start(s32[4096]{0:T(1024)} %get-tuple-element.16) | copy-start | bytes 49156
  208.6 7.1 %copy-start.6 = (f32[6,384]{1,0:T(8,128)S(1)}, f32[6,384]{1,0:T(8,128)}, u32[]{:S(2)}) copy-start(f32[6,384]{1,0:T(8,128)} %copy-done.5) | copy-start | bytes 27652
  209.6 19.7 %all-to-all-start.1 = ((f32[6,8,256]{2,0,1:T(8,128)}), f32[6,8,256]{2,0,1:T(8,128)S(1)}, u32[]{:S(2)}, u32[]{:S(2)}) async-start(f32[6,8,256]{2,0,1:T(8,128)} %copy.52), calls=%async_computation.1 | async-start | bytes 131072 | tf_op jit(solution)/shard_map/all_to_all | solution.py:72
  245.6 2.3 copy-start.16
  245.6 48.0 %copy-start.1 = (f32[6,12288]{1,0:T(8,128)S(1)}, f32[6,12288]{1,0:T(8,128)}, u32[]{:S(2)}) copy-start(f32[6,12288]{1,0:T(8,128)} %param.22) | copy-start | bytes 884740
  245.6 48.7 %copy-start.2 = (f32[6,4096]{1,0:T(8,128)S(1)}, f32[6,4096]{1,0:T(8,128)}, u32[]{:S(2)}) copy-start(f32[6,4096]{1,0:T(8,128)} %param.21) | copy-start | bytes 294916
  245.6 50.0 %copy-start.3 = (f32[6,12288]{1,0:T(8,128)S(1)}, f32[6,12288]{1,0:T(8,128)}, u32[]{:S(2)}) copy-start(f32[6,12288]{1,0:T(8,128)} %param.20) | copy-start | bytes 884740
  248.8 50.3 %copy-start.7 = (f32[6,4096]{1,0:T(8,128)S(1)}, f32[6,4096]{1,0:T(8,128)}, u32[]{:S(2)}) copy-start(f32[6,4096]{1,0:T(8,128)} %param.19) | copy-start | bytes 294916
Sparse Core Ops, SparseCore 0:
  125.1 72.1 all-reduce.5
where the time goes:
time: 351 us; the launch traced here: 349 us
  blocking collectives  133 us (38%)
  other arithmetic  99.8 us (28%)
  local copies, waits for them, and re-layouts  65.8 us (19%)
  between operations  24.7 us (7%)
  matrix products  15 us (4%)
  starting transfers between devices  11.4 us (3%)
    scatter-add x2, other arithmetic, local(): backward.at[:, sire_slot].add(-0.5 * sampling).at[:, dam_slot]  45.9 us
    psum x1, blocking collectives, local(): lax.psum((jnp.sum(residual_animal * search_animal) + jnp.sum(marker_share...  42 us
    psum x1, blocking collectives, local(): lax.psum(jnp.sum(next_residual_animal * next_residual_animal) + jnp.sum(n...  40.4 us
    psum x1, blocking collectives, local(): lax.psum(jnp.sum(new_animal * image_animal) + jnp.sum(new_share * image_s...  40 us
    scatter-add x1, other arithmetic, local(): placed = jnp.zeros((traits, genotyped + 1), jnp.float32).at[:, genotype_r...  28.3 us
    gather x2, local copies, waits for them, and re-layouts, local(): parents[:, dam_slot]  16.3 us
    gather x2, local copies, waits for them, and re-layouts, local(): parents[:, sire_slot]  16.3 us
    scatter-add x1, other arithmetic, local(): gathered_terms = jnp.zeros((traits, animal_count + 1), jnp.float32).at[:,...  13.5 us
  transfers between devices with their start and end apart: 3, of which 0 were waited for; matrix products, arithmetic and copies ran while one was open for 46% of the time, Pallas kernels for 0%

commit v1 on v0

v1 whole, which is shorter than its diff:
```python
import functools

import jax
import jax.numpy as jnp
from jax import lax
from jax.experimental import pallas as pl
from jax.experimental.pallas import tpu as pltpu
from jax.sharding import PartitionSpec as P

F32 = jnp.float32
BF16 = jnp.bfloat16
PAD = 8
LANES = 128


def shape_of(*dims, dtype=F32):
    return jax.ShapeDtypeStruct(dims, dtype)


def call(kernel, out_shape, scratch=(), **options):
    return pl.pallas_call(kernel, out_shape=out_shape, scratch_shapes=list(scratch), **options)


def parts_of(values):
    high = values.astype(BF16).astype(F32)
    rest = values - high
    middle = rest.astype(BF16).astype(F32)
    return jnp.concatenate([high, middle, rest - middle], axis=0)


def add_parts(stacked):
    return stacked[:PAD] + stacked[PAD : 2 * PAD] + stacked[2 * PAD :]


ROWS_EACH = 3 * PAD


def one_hot(low, base):
    wanted = lax.broadcasted_iota(jnp.int32, (base, low.shape[1]), 0)
    return jnp.where(wanted == low, 1.0, 0.0).astype(BF16)


def dot(left, right):
    return lax.dot_general(left, right, (((1,), (0,)), ((), ())), preferred_element_type=F32)


def dot_t(left, right):
    return lax.dot_general(left, right, (((1,), (1,)), ((), ())), preferred_element_type=F32)


def select_blocks(products, high, first, count):
    total = None
    for h in range(count):
        block = add_parts(products[h * ROWS_EACH : (h + 1) * ROWS_EACH])
        block = jnp.where(high == first + h, block, 0.0)
        total = block if total is None else total + block
    return total


def masked_blocks(stacked, high, first, count):
    return jnp.concatenate(
        [jnp.where(high == first + h, stacked, 0.0) for h in range(count)], axis=0
    ).astype(BF16)


def fold(values):
    total = values[:, :LANES]
    for start in range(LANES, values.shape[1], LANES):
        total = total + values[:, start : start + LANES]
    return total


def load_matrix(matrix_ref, padded_ref):
    padded_ref[...] = jnp.zeros_like(padded_ref)
    size = matrix_ref.shape[0]
    padded_ref[:size, :size] = matrix_ref[...]


def apply_matrix(padded_ref, values, count):
    total = None
    for s in range(count):
        term = padded_ref[:, s : s + 1] * values[s : s + 1, :]
        total = term if total is None else total + term
    return total


def total_of(tile):
    return jnp.sum(jnp.sum(tile, axis=0, keepdims=True), axis=1, keepdims=True)


def sums_of(received_ref):
    tile = received_ref[0]
    for i in range(1, received_ref.shape[0]):
        tile = tile + received_ref[i]
    return tile


def product_of(sums_ref):
    return jnp.sum(sums_of(sums_ref)[0:1], axis=1, keepdims=True)


def norm_of(sums_ref):
    return jnp.sum(sums_of(sums_ref)[1:2], axis=1, keepdims=True)


def totals_kernel(marker_weight, res_a, scal_a, res_m, scal_m, out):
    def pair(res_ref, scal_ref):
        res = res_ref[...]
        square = res * res
        return (
            jnp.sum(fold(square * scal_ref[...]), axis=0, keepdims=True),
            jnp.sum(fold(square), axis=0, keepdims=True),
        )

    product_a, norm_a = pair(res_a, scal_a)
    product_m, norm_m = pair(res_m, scal_m)
    row = lax.broadcasted_iota(jnp.int32, (PAD, LANES), 0)
    product = product_a + marker_weight * product_m
    norm = norm_a + marker_weight * norm_m
    tile = jnp.where(row == 0, product, jnp.where(row == 1, norm, 0.0))
    out[...] = jnp.broadcast_to(tile[None], out.shape)


def animal_kernel(bits, sums, previous, res, scal, direction, send, new_ref, out):
    traits, animals = res.shape
    base = 1 << bits
    conjugacy = product_of(sums) / previous[...]
    new_ref[...] = jnp.zeros_like(new_ref)
    new_ref[:traits] = scal[...] * res[...] + conjugacy * direction[...]
    blocks = animals // base
    table = jnp.concatenate(
        [parts_of(new_ref[:, h * base : (h + 1) * base]) for h in range(blocks)], axis=0
    ).astype(BF16)

    def one(r):
        index = send[pl.ds(r, 1), :]
        products = dot(table, one_hot(index & (base - 1), base))
        out[r] = select_blocks(products, index >> bits, 0, blocks)

    if send.shape[0] <= 8:
        for r in range(send.shape[0]):
            one(r)
    else:
        pl.loop(0, send.shape[0])(one)


def predict_kernel(
    bits,
    sums,
    previous,
    res,
    scal,
    direction,
    genotypes,
    new_a,
    row_index,
    new_m,
    placed_ref,
    out,
    conjugacy_ref,
    total_ref,
):
    step = pl.program_id(0)
    traits = res.shape[0]
    genotyped = genotypes.shape[0]
    base = 1 << bits

    @pl.when(step == 0)
    def _():
        conjugacy_ref[...] = jnp.broadcast_to(product_of(sums) / previous[...], (PAD, LANES))
        total_ref[...] = jnp.zeros_like(total_ref)
        blocks = -(-genotyped // base)
        width = 1024
        total = jnp.zeros((blocks * ROWS_EACH, base), F32)
        for start in range(0, new_a.shape[1], width):
            index = row_index[:, start : start + width]
            stacked = parts_of(new_a[:, start : start + width])
            total = total + dot_t(
                masked_blocks(stacked, index >> bits, 0, blocks),
                one_hot(index & (base - 1), base),
            )
        for h in range(blocks):
            size = min(base, genotyped - h * base)
            block = add_parts(total[h * ROWS_EACH : (h + 1) * ROWS_EACH])
            placed_ref[:, h * base : h * base + size] = block[:, :size]

    new_m[...] = jnp.zeros_like(new_m)
    new_m[:traits] = scal[...] * res[...] + conjugacy_ref[:traits, 0:1] * direction[...]
    total_ref[...] += dot_t(new_m[...].astype(BF16), genotypes[...])

    @pl.when(step == pl.num_programs(0) - 1)
    def _():
        out[...] = jnp.broadcast_to((placed_ref[...] - total_ref[...])[None], out.shape)


def pedigree_kernel(
    bits,
    parents,
    new_a,
    sire,
    dam,
    pattern,
    table,
    genetic,
    base_ref,
    back_ref,
    part_ref,
    left_ref,
    matrix_ref,
):
    owners, _, base = parents.shape
    traits = genetic.shape[0]
    patterns = table.shape[1]
    animals = new_a.shape[1]
    load_matrix(genetic, matrix_ref)
    for h in range(0, owners, 2):
        left_ref[h * ROWS_EACH : (h + 2) * ROWS_EACH, :] = jnp.concatenate(
            [parts_of(parents[h]), parts_of(parents[h + 1])], axis=0
        ).astype(BF16)
    values = table[...]
    high_part = values.astype(BF16).astype(F32)
    rest = values - high_part
    middle_part = rest.astype(BF16).astype(F32)
    record_table = jnp.concatenate([high_part, middle_part, rest - middle_part], axis=0).astype(
        BF16
    )
    group = min(8, owners)
    groups = owners // group

    def over_groups(body):
        for g in range(groups):
            body(g)

    gathered_ref = base_ref
    width = 1024
    back_ref[...] = jnp.zeros_like(back_ref)
    part = jnp.zeros((PAD, LANES), F32)
    for start in range(0, animals, width):
        window = slice(start, start + width)
        new = new_a[:, window]
        sire_index, dam_index = sire[:, window], dam[:, window]
        sire_high, dam_high = sire_index >> bits, dam_index >> bits
        sire_hot = one_hot(sire_index & (base - 1), base)
        dam_hot = one_hot(dam_index & (base - 1), base)
        gathered_ref[:, window] = jnp.zeros((PAD, width), F32)

        def gather(g):
            left = left_ref[pl.ds(g * group * ROWS_EACH, group * ROWS_EACH), :]
            gathered_ref[:, window] += select_blocks(
                dot(left, sire_hot), sire_high, g * group, group
            ) + select_blocks(dot(left, dam_hot), dam_high, g * group, group)

        over_groups(gather)
        slots = owners * base
        known = (sire_index < slots).astype(F32) + (dam_index < slots).astype(F32)
        mendel = 1.0 / (1.0 - 0.25 * known)
        difference = new - 0.5 * gathered_ref[:, window]
        sampling = mendel * difference
        genetic_term = apply_matrix(matrix_ref, sampling, traits)
        blocks = dot(record_table, one_hot(pattern[:, window], patterns))
        record = None
        size = traits * PAD
        for s in range(traits):
            row = slice(s * PAD, (s + 1) * PAD)
            block = blocks[row] + blocks[size:][row] + blocks[2 * size :][row]
            term = block * new[s : s + 1, :]
            record = term if record is None else record + term
        base_ref[:, window] = genetic_term + record
        part = part + fold(difference * genetic_term + new * record)
        stacked = parts_of(-0.5 * sampling)

        def scatter(g):
            total = dot_t(masked_blocks(stacked, sire_high, g * group, group), sire_hot) + dot_t(
                masked_blocks(stacked, dam_high, g * group, group), dam_hot
            )
            for h in range(group):
                back_ref[g * group + h] += add_parts(total[h * ROWS_EACH : (h + 1) * ROWS_EACH])

        over_groups(scatter)
    part_ref[...] = part


def deviation_kernel(
    share,
    differences,
    placed,
    genomic,
    marker_inverse,
    genotypes,
    new_m,
    back,
    part,
    deviation_ref,
    out,
    genomic_ref,
    marker_ref,
    total_ref,
):
    step = pl.program_id(0)
    traits = genomic.shape[0]
    owners = out.shape[0]
    capacity = back.shape[2]
    padded = out.shape[2] - capacity - LANES

    @pl.when(step == 0)
    def _():
        load_matrix(genomic, genomic_ref)
        load_matrix(marker_inverse, marker_ref)
        deviation = apply_matrix(genomic_ref, sums_of(differences), traits)
        deviation_ref[...] = deviation
        total_ref[...] = part[...] + fold(placed[...] * deviation)
        out[:, :, padded : padded + capacity] = back[...]

    new = new_m[...]
    terms = dot(deviation_ref[...].astype(BF16), genotypes[...])
    per_step = new.shape[1] // share
    for j in range(per_step):
        out[step * per_step + j, :, :share] = terms[:, j * share : (j + 1) * share]
    image = apply_matrix(marker_ref, new, traits)
    total_ref[...] += fold(new * (image * (1.0 / owners) - terms))

    @pl.when(step == pl.num_programs(0) - 1)
    def _():
        out[:, :, padded + capacity :] = jnp.broadcast_to(total_ref[...][None], (owners, PAD, LANES))


def spread_kernel(received, out):
    start = received.shape[2] - LANES
    tile = received[0, :, start:]
    for i in range(1, received.shape[0]):
        tile = tile + received[i, :, start:]
    out[...] = jnp.broadcast_to(tile[None], out.shape)


def image_kernel(
    bits, received, send, base_image, deviation, row_index, genetic, out, matrix_ref, table_ref
):
    owners = received.shape[0]
    base = 1 << bits
    traits = genetic.shape[0]
    animals = base_image.shape[1]
    genotyped = deviation.shape[1]
    start = received.shape[2] - LANES - base
    load_matrix(genetic, matrix_ref)
    blocks = animals // base

    def scatter(r, total):
        index = send[pl.ds(r, 1), :]
        stacked = parts_of(received[r, :, start : start + base])
        return total + dot_t(
            masked_blocks(stacked, index >> bits, 0, blocks), one_hot(index & (base - 1), base)
        )

    total = jnp.zeros((blocks * ROWS_EACH, base), F32)
    if owners <= 8:
        for r in range(owners):
            total = scatter(r, total)
    else:
        total = lax.fori_loop(0, owners, scatter, total)
    table_ref[...] = jnp.zeros_like(table_ref)
    table_ref[:, :genotyped] = deviation[...]
    places = table_ref.shape[1] // base
    table = jnp.concatenate(
        [parts_of(table_ref[:, h * base : (h + 1) * base]) for h in range(places)], axis=0
    ).astype(BF16)
    for h in range(blocks):
        window = slice(h * base, (h + 1) * base)
        index = row_index[:, window]
        gathered = add_parts(total[h * ROWS_EACH : (h + 1) * ROWS_EACH])
        genomic_term = select_blocks(
            dot(table, one_hot(index & (base - 1), base)), index >> bits, 0, places
        )
        out[:, window] = (
            base_image[:, window] + apply_matrix(matrix_ref, gathered, traits) + genomic_term
        )


def step_of(sums, curvature):
    return product_of(sums) / total_of(sums_of(curvature))


def update_kernel(
    row,
    share,
    sums,
    curvature,
    sol_a,
    res_a,
    new_a,
    image_a,
    received,
    new_share,
    res_share,
    marker_inverse,
    next_sol_a,
    next_res_a,
    out,
    matrix_ref,
):
    del row
    traits = sol_a.shape[0]
    owners = out.shape[0]
    step = step_of(sums, curvature)
    next_sol_a[...] = sol_a[...] + step * new_a[:traits]
    next_animal = res_a[...] - step * image_a[:traits]
    next_res_a[...] = next_animal
    load_matrix(marker_inverse, matrix_ref)
    terms = received[0, :, :share]
    for i in range(1, owners):
        terms = terms + received[i, :, :share]
    image = apply_matrix(matrix_ref, new_share[...], traits) - terms
    next_share = res_share[...] - step * image[:traits]
    square = next_share * next_share
    edge = share - share % LANES
    part = jnp.sum(fold(next_animal * next_animal), axis=0, keepdims=True)
    if edge:
        part = part + jnp.sum(fold(square[:, :edge]), axis=0, keepdims=True)
    if edge < share:
        rest = jnp.sum(jnp.sum(square[:, edge:], axis=1, keepdims=True), axis=0, keepdims=True)
        part = part + jnp.where(lax.broadcasted_iota(jnp.int32, (1, LANES), 1) == 0, rest, 0.0)
    norm_row = lax.broadcasted_iota(jnp.int32, (PAD, LANES), 0) == 0
    tile = jnp.where(norm_row, part, 0.0)
    padded = out.shape[2] - LANES
    for i in range(owners):
        out[i] = jnp.zeros(out.shape[1:], F32)
        out[i, :traits, :share] = next_share
        out[i, :, padded:] = tile


def marker_solution_kernel(sums, curvature, sol, new, out):
    out[...] = sol[...] + step_of(sums, curvature) * new[: sol.shape[0]]


def collect_kernel(share, received, next_res, out):
    traits = next_res.shape[0]
    padded = received.shape[2] - LANES
    tile = received[0, :, padded:]
    for i in range(received.shape[0]):
        next_res[:, i * share : (i + 1) * share] = received[i, :traits, :share]
        if i:
            tile = tile + received[i, :, padded:]
    out[...] = jnp.broadcast_to(tile[None], out.shape)


def reduction_kernel(sums, norms, out):
    out[...] = total_of(sums_of(norms)) / norm_of(sums)


def exchange(values, axes):
    return lax.all_to_all(values, axes, split_axis=0, concat_axis=0, tiled=True)


def local(
    solution_animal,
    solution_marker,
    residual_animal,
    residual_marker,
    direction_animal,
    direction_marker,
    scaling_animal,
    scaling_marker,
    previous_product,
    genotypes,
    genetic_inverse,
    genomic_inverse,
    marker_inverse,
    residual_table,
    pattern,
    sire_slot,
    dam_slot,
    genotype_row,
    send_list,
):
    traits, animals = residual_animal.shape
    markers = residual_marker.shape[1]
    genotyped = genotypes.shape[0]
    rows = lax.axis_size("rows")
    columns = lax.axis_size("mk")
    capacity = send_list.shape[3]
    bits = capacity.bit_length() - 1
    share = markers // rows
    padded = -(-share // LANES) * LANES
    chunk = share * max(1, 1536 // share)
    steps = markers // chunk
    patterns = residual_table.shape[0]
    row = lax.axis_index("rows").astype(jnp.int32).reshape(1)
    previous = previous_product.reshape(1, 1)
    send = send_list.reshape(rows, capacity)
    sire, dam = sire_slot.reshape(1, animals), dam_slot.reshape(1, animals)
    kinds, places = pattern.reshape(1, animals), genotype_row.reshape(1, animals)
    table = jnp.pad(jnp.transpose(residual_table, (2, 1, 0)), ((0, 0), (0, PAD - traits), (0, 0)))
    table = table.reshape(traits * PAD, patterns)

    sums = exchange(
        call(
            functools.partial(totals_kernel, 1.0 / rows),
            shape_of(rows * columns, PAD, LANES),
            name="totals",
        )(residual_animal, scaling_animal, residual_marker, scaling_marker),
        ("rows", "mk"),
    )
    new_animal, outgoing = call(
        functools.partial(animal_kernel, bits),
        (shape_of(PAD, animals), shape_of(rows, PAD, capacity)),
        name="animals",
    )(sums, previous, residual_animal, scaling_animal, direction_animal, send)
    parents = exchange(outgoing, "rows")

    def fixed(array):
        return pl.BlockSpec(array.shape, lambda k, n=len(array.shape): (0,) * n)

    def moving(height):
        return pl.BlockSpec((height, chunk), lambda k: (0, k))

    new_marker, placed, difference = call(
        functools.partial(predict_kernel, bits),
        (shape_of(PAD, markers), shape_of(PAD, genotyped), shape_of(columns, PAD, genotyped)),
        (pltpu.VMEM((PAD, LANES), F32), pltpu.VMEM((PAD, genotyped), F32)),
        grid=(steps,),
        in_specs=[
            fixed(sums),
            fixed(previous),
            moving(traits),
            moving(traits),
            moving(traits),
            moving(genotyped),
            fixed(new_animal),
            fixed(places),
        ],
        out_specs=(
            moving(PAD),
            fixed(shape_of(PAD, genotyped)),
            fixed(shape_of(columns, PAD, genotyped)),
        ),
        name="predict",
    )(
        sums,
        previous,
        residual_marker,
        scaling_marker,
        direction_marker,
        genotypes,
        new_animal,
        places,
    )
    differences = exchange(difference, "mk")
    base_image, back, part = call(
        functools.partial(pedigree_kernel, bits),
        (shape_of(PAD, animals), shape_of(rows, PAD, capacity), shape_of(PAD, LANES)),
        (pltpu.VMEM((rows * ROWS_EACH, capacity), BF16), pltpu.VMEM((PAD, LANES), F32)),
        name="pedigree",
    )(parents, new_animal, sire, dam, kinds, table, genetic_inverse)
    out_shape = shape_of(rows, PAD, padded + capacity + LANES)
    deviation, payload = call(
        functools.partial(deviation_kernel, share),
        (shape_of(PAD, genotyped), out_shape),
        (pltpu.VMEM((PAD, LANES), F32),) * 3,
        grid=(steps,),
        in_specs=[
            fixed(differences),
            fixed(placed),
            fixed(genomic_inverse),
            fixed(marker_inverse),
            moving(genotyped),
            moving(PAD),
            fixed(back),
            fixed(part),
        ],
        out_specs=(fixed(placed), fixed(out_shape)),
        name="deviation",
    )(differences, placed, genomic_inverse, marker_inverse, genotypes, new_marker, back, part)
    received = exchange(payload, "rows")
    curvature = exchange(
        call(spread_kernel, shape_of(columns, PAD, LANES), name="spread")(received), "mk"
    )
    table_width = -(-genotyped // capacity) * capacity
    image_animal = call(
        functools.partial(image_kernel, bits),
        shape_of(PAD, animals),
        (pltpu.VMEM((PAD, LANES), F32), pltpu.VMEM((PAD, table_width), F32)),
        name="image",
    )(received, send, base_image, deviation, places, genetic_inverse)

    if share % LANES:
        start = row[0] * share
        new_share = lax.dynamic_slice_in_dim(new_marker, start, share, 1)
        res_share = lax.dynamic_slice_in_dim(residual_marker, start, share, 1)

        def own(height):
            return pl.BlockSpec((height, share), lambda k, r: (0, 0))
    else:
        new_share, res_share = new_marker, residual_marker

        def own(height):
            return pl.BlockSpec((height, share), lambda k, r: (0, r[0]))

    def still(array):
        return pl.BlockSpec(array.shape, lambda k, r, n=len(array.shape): (0,) * n)

    out_shape = shape_of(rows, PAD, padded + LANES)
    next_solution_animal, next_residual_animal, payload = pl.pallas_call(
        lambda r, *refs: update_kernel(r, share, *refs),
        out_shape=(shape_of(traits, animals), shape_of(traits, animals), out_shape),
        grid_spec=pltpu.PrefetchScalarGridSpec(
            num_scalar_prefetch=1,
            grid=(1,),
            in_specs=[
                still(sums),
                still(curvature),
                still(solution_animal),
                still(residual_animal),
                still(new_animal),
                still(image_animal),
                still(received),
                own(PAD),
                own(traits),
                still(marker_inverse),
            ],
            out_specs=(still(solution_animal), still(solution_animal), still(out_shape)),
            scratch_shapes=[pltpu.VMEM((PAD, LANES), F32)],
        ),
        name="update",
    )(
        row,
        sums,
        curvature,
        solution_animal,
        residual_animal,
        new_animal,
        image_animal,
        received,
        new_share,
        res_share,
        marker_inverse,
    )
    gathered = exchange(payload, "rows")
    next_solution_marker = call(
        marker_solution_kernel, shape_of(traits, markers), name="marker_solution"
    )(sums, curvature, solution_marker, new_marker)
    next_residual_marker, norm = call(
        functools.partial(collect_kernel, share),
        (shape_of(traits, markers), shape_of(columns, PAD, LANES)),
        name="collect",
    )(gathered)
    reduction = call(reduction_kernel, shape_of(1, 1), name="reduction")(
        sums, exchange(norm, "mk")
    ).reshape(())
    return (
        next_solution_animal,
        next_solution_marker,
        next_residual_animal,
        next_residual_marker,
        reduction,
    )


def solution(mesh):
    animal, marker = P(None, ("rows", "mk")), P(None, "mk")
    index = P(("rows", "mk"))
    return jax.shard_map(
        local,
        mesh=mesh,
        in_specs=(
            animal,
            marker,
            animal,
            marker,
            animal,
            marker,
            animal,
            marker,
            P(),
            P("rows", "mk"),
            P(),
            P(),
            P(),
            P(),
            index,
            index,
            index,
            index,
            P("rows", "mk", None, None),
        ),
        out_specs=(animal, marker, animal, marker, P()),
        check_vma=False,
    )
```

time: 351 us -> 113 us (0.32)
  other arithmetic: 99.8 us -> 0 us
  blocking collectives: 133 us -> 37.4 us
  local copies, waits for them, and re-layouts: 65.8 us -> 3.83 us
  Pallas kernels: 0 us -> 38.8 us
  between operations: 24.7 us -> 1.35 us
  matrix products: 15 us -> 0 us
  waiting for transfers between devices: 0.02 us -> 10.3 us
  starting transfers between devices: 11.4 us -> 20.5 us
    psum x4 -> x0, blocking collectives: 133 us -> none  [the longest x1 42 us: local(): lax.psum((jnp.sum(residual_animal * search_animal) + jnp.sum(marker_share...]
    scatter-add x4 -> x0, other arithmetic: 87.6 us -> none  [the longest x2 45.9 us: local(): backward.at[:, sire_slot].add(-0.5 * sampling).at[:, dam_slot]]
    gather x8 -> x0, local copies, waits for them, and re-layouts: 54 us -> none  [the longest x2 16.3 us: local(): parents[:, dam_slot]]
    pallas_call x0 -> x11, Pallas kernels: none -> 38.8 us  [the longest x1 9.48 us: local(): call(functools.partial(predict_kernel, bits), (shape_of(PAD, markers), sh...]
    all_to_all x0 -> x2, blocking collectives: none -> 37.4 us  [exchange(): return lax.all_to_all(values, axes, split_axis=0, concat_axis=0, tiled=True)]
    dot_general x6 -> x0, matrix products: 15 us -> none  [the longest x1 6.22 us: local(): lax.dot_general(new_marker.astype(jnp.bfloat16), genotypes, (((1,), (1,))...]
    all_to_all x2 -> x5, waiting for transfers between devices: 0.01 us -> 10.3 us  [exchange(): return lax.all_to_all(values, axes, split_axis=0, concat_axis=0, tiled=True)]
    all_to_all x2 -> x5, starting transfers between devices: 11.4 us -> 20.5 us  [exchange(): return lax.all_to_all(values, axes, split_axis=0, concat_axis=0, tiled=True)]
  transfers between devices with their start and end apart: 3 -> 5, of which waited for: 0 -> 3; matrix products, arithmetic and copies ran while one was open for 46% -> 1% of each run, Pallas kernels for 0% -> 17%
where the time goes in v1:
time: 113 us; the launch traced here: 112 us
  Pallas kernels  38.8 us (34%)
  blocking collectives  37.4 us (33%)
  starting transfers between devices  20.5 us (18%)
  waiting for transfers between devices  10.3 us (9%)
  local copies, waits for them, and re-layouts  3.83 us (3%)
  between operations  1.35 us (1%)
    all_to_all x2, blocking collectives, exchange(): return lax.all_to_all(values, axes, split_axis=0, concat_axis=0, tiled=True)  37.4 us
    all_to_all x5, starting transfers between devices, exchange(): return lax.all_to_all(values, axes, split_axis=0, concat_axis=0, tiled=True)  20.5 us
    all_to_all x5, waiting for transfers between devices, exchange(): return lax.all_to_all(values, axes, split_axis=0, concat_axis=0, tiled=True)  10.3 us
    pallas_call x1, Pallas kernels, local(): call(functools.partial(predict_kernel, bits), (shape_of(PAD, markers), sh...  9.48 us
    pallas_call x1, Pallas kernels, local(): call(functools.partial(deviation_kernel, share), (shape_of(PAD, genotyped...  7.72 us
    pallas_call x1, Pallas kernels, local(): call(functools.partial(pedigree_kernel, bits), (shape_of(PAD, animals), s...  4.67 us
    unnamed x11, local copies, waits for them, and re-layouts  3.22 us
    pallas_call x1, Pallas kernels, local(): call(functools.partial(image_kernel, bits), shape_of(PAD, animals), (pltp...  2.82 us
  transfers between devices with their start and end apart: 5, of which 3 were waited for; matrix products, arithmetic and copies ran while one was open for 1% of the time, Pallas kernels for 17%

profile of v1, /device:TPU:0, one launch (start us, length us, event | category | flops | bytes accessed | tf_op | source)
XLA Modules:
  0.0 112.0 jit_solution(8762893225089050747)
XLA Ops:
  0.6 2.0 %totals.1 = f32[32,8,128]{2,1,0:T(8,128)} custom-call(f32[6,4096]{1,0:T(8,128)} %refs_3_.1, f32[6,4096]{1,0:T(8,128)} %scal.2, f32[6,12288]{1,0:T(8,128)} %refs_8_.1, f32[6,12288]{1,0:T(8,128)} %scal.3), custom_call_target="tpu_custom_call" | custom-call | tf_op jit(solution)/shard_map/totals/pallas_call | solution.py:495
  2.7 7.3 %all-to-all-start = ((f32[32,8,128]{2,1,0:T(8,128)}), f32[32,8,128]{2,1,0:T(8,128)S(1)}, u32[]{:S(2)}, u32[]{:S(2)}) async-start(f32[32,8,128]{2,1,0:T(8,128)} %totals.1), calls=%async_computation | async-start | bytes 262144 | tf_op jit(solution)/shard_map/all_to_all | solution.py:450
  10.6 7.6 %all-to-all-done.sums.refs_0_ = f32[32,8,128]{2,1,0:T(8,128)S(1)} async-done(((f32[32,8,128]{2,1,0:T(8,128)}), f32[32,8,128]{2,1,0:T(8,128)S(1)}, u32[]{:S(2)}, u32[]{:S(2)}) %all-to-all-start) | async-done | bytes 131104 | tf_op jit(solution)/shard_map/all_to_all | solution.py:450
  18.2 0.0 copy-start
  18.2 0.7 copy-done
  18.9 2.6 %animals.1 = (f32[8,4096]{1,0:T(8,128)}, f32[8,8,256]{2,1,0:T(8,128)}) custom-call(f32[32,8,128]{2,1,0:T(8,128)} %copy-done, f32[1,1]{1,0:T(1,128)} %bitcast.11.previous, f32[6,4096]{1,0:T(8,128)} %refs_3_.1, f32[6,4096]{1,0:T(8,128)} %scal.2, f32[6,4096]{1,0:T(8,128)} %direction.2, s32[8,256]{1,0:T(8,128)} %bitcast.15), custom_call_target="tpu_custom_call" | custom-call | tf_op jit(solution)/shard_map/animals/pallas_call | solution.py:502
  21.4 3.4 %all-to-all-start.2 = ((f32[8,8,256]{2,1,0:T(8,128)}), f32[8,8,256]{2,1,0:T(8,128)S(1)}, u32[]{:S(2)}, u32[]{:S(2)}) async-start(f32[8,8,256]{2,1,0:T(8,128)} %get-tuple-element.24), calls=%async_computation.2 | async-start | bytes 131072 | tf_op jit(solution)/shard_map/all_to_all | solution.py:450
  24.8 0.7 copy.25
  25.5 9.5 %predict.1 = (f32[8,12288]{1,0:T(8,128)}, f32[8,384]{1,0:T(8,128)}, f32[4,8,384]{2,1,0:T(8,128)}) custom-call(f32[32,8,128]{2,1,0:T(8,128)} %copy-done, f32[1,1]{1,0:T(1,128)} %bitcast.12.previous, f32[6,12288]{1,0:T(8,128)} %refs_8_.1, f32[6,12288]{1,0:T(8,128)} %scal.3, f32[6,12288]{1,0:T(8,128)} %direction.3, bf16[384,12288]{1,0:T(8,128)(2,1)} %genotypes.3, ...), custom_call_target="tpu_custom_call" | custom-call | tf_op jit(solution)/shard_map/predict/pallas_call | solution.py:515
  35.0 0.0 all-to-all-done.2.parents
  35.0 0.0 copy-start.1
  35.0 3.3 %all-to-all-start.1 = ((f32[4,8,384]{2,1,0:T(8,128)}), f32[4,8,384]{2,1,0:T(8,128)S(1)}, u32[]{:S(2)}, u32[]{:S(2)}) async-start(f32[4,8,384]{2,1,0:T(8,128)} %get-tuple-element.21), calls=%async_computation.1 | async-start | bytes 98304 | tf_op jit(solution)/shard_map/all_to_all | solution.py:450
  38.3 0.6 pad_bitcast_fusion.table
  38.9 0.0 copy-done.1
  38.9 4.7 %pedigree.1 = (f32[8,4096]{1,0:T(8,128)}, f32[8,8,256]{2,1,0:T(8,128)}, f32[8,128]{1,0:T(8,128)}) custom-call(f32[8,8,256]{2,1,0:T(8,128)} %copy-done.1, f32[8,4096]{1,0:T(8,128)} %get-tuple-element.20.new_a.refs_4_, s32[1,4096]{1,0:T(1,128)} %bitcast.18, s32[1,4096]{1,0:T(1,128)} %bitcast.19, s32[1,4096]{1,0:T(1,128)} %bitcast.20, ...), custom_call_target="tpu_custom_call" | custom-call | tf_op jit(solution)/shard_map/pedigree/pallas_call | solution.py:547
  43.6 0.0 all-to-all-done.1.differences
  43.6 0.0 copy-start.2
  43.6 0.6 copy-done.2
  44.2 7.7 %deviation.1 = (f32[8,384]{1,0:T(8,128)}, f32[8,8,1920]{2,1,0:T(8,128)}) custom-call(f32[4,8,384]{2,1,0:T(8,128)} %copy-done.2, f32[8,384]{1,0:T(8,128)} %get-tuple-element.22.placed, f32[6,6]{1,0:T(8,128)} %genomic.1, f32[6,6]{1,0:T(8,128)} %refs_9_.1, bf16[384,12288]{1,0:T(8,128)(2,1)} %genotypes.3, f32[8,12288]{1,0:T(8,128)} %get-tuple-element.23.new_m.refs_7_.new, ...), custom_call_target="tpu_custom_call" | custom-call | tf_op jit(solution)/shard_map/deviation/pallas_call | solution.py:554
  52.0 20.4 %all_to_all.35.received.refs_6_ = f32[8,8,1920]{2,1,0:T(8,128)} all-to-all(f32[8,8,1920]{2,1,0:T(8,128)} %get-tuple-element.27), channel_id=1, replica_groups=mesh['rows'=8,'mk'=4] {'rows'}, dimensions={0} | all-to-all | bytes 983040 | tf_op jit(solution)/shard_map/all_to_all | solution.py:450
  72.4 1.6 %spread.1 = f32[4,8,128]{2,1,0:T(8,128)} custom-call(f32[8,8,1920]{2,1,0:T(8,128)} %all_to_all.35.received.refs_6_), custom_call_target="tpu_custom_call" | custom-call | tf_op jit(solution)/shard_map/spread/pallas_call | solution.py:574
  74.1 3.3 %all-to-all-start.4 = ((f32[4,8,128]{2,1,0:T(8,128)}), f32[4,8,128]{2,1,0:T(8,128)S(1)}, u32[]{:S(2)}, u32[]{:S(2)}) async-start(f32[4,8,128]{2,1,0:T(8,128)} %spread.1), calls=%async_computation.4 | async-start | bytes 32768 | tf_op jit(solution)/shard_map/all_to_all | solution.py:450
  77.3 2.8 %image.1.refs_5_ = f32[8,4096]{1,0:T(8,128)} custom-call(f32[8,8,1920]{2,1,0:T(8,128)} %all_to_all.35.received.refs_6_, s32[8,256]{1,0:T(8,128)} %bitcast.16, f32[8,4096]{1,0:T(8,128)} %get-tuple-element.28.base_image, f32[8,384]{1,0:T(8,128)} %get-tuple-element.29.deviation, s32[1,4096]{1,0:T(1,128)} %bitcast.14, f32[6,6]{1,0:T(8,128)} %genetic.3), custom_call_target="tpu_custom_call" | custom-call | tf_op jit(solution)/shard_map/image/pallas_call | solution.py:577
  80.1 1.0 all-to-all-done.4.refs_1_.curvature
  81.1 0.0 copy-start.3
  81.1 0.6 copy-done.3
  81.7 2.4 %update.1 = (f32[6,4096]{1,0:T(8,128)}, f32[6,4096]{1,0:T(8,128)}, f32[8,8,1664]{2,1,0:T(8,128)}) custom-call(s32[1]{0:T(128)} %bitcast.r, f32[32,8,128]{2,1,0:T(8,128)} %copy-done, f32[4,8,128]{2,1,0:T(8,128)} %copy-done.3, f32[6,4096]{1,0:T(8,128)} %refs_2_.1, f32[6,4096]{1,0:T(8,128)} %refs_3_.1, f32[8,4096]{1,0:T(8,128)} %get-tuple-element.20.new_a.refs_4_, ...), custom_call_target="tpu_custom_call" | custom-call | tf_op jit(solution)/shard_map/update/pallas_call | solution.py:601
  84.1 16.9 %all_to_all.36.received = f32[8,8,1664]{2,1,0:T(8,128)} all-to-all(f32[8,8,1664]{2,1,0:T(8,128)} %get-tuple-element.32), channel_id=1, replica_groups=mesh['rows'=8,'mk'=4] {'rows'}, dimensions={0} | all-to-all | bytes 851968 | tf_op jit(solution)/shard_map/all_to_all | solution.py:450
  101.0 1.8 %collect.1 = (f32[6,12288]{1,0:T(8,128)}, f32[4,8,128]{2,1,0:T(8,128)}) custom-call(f32[8,8,1664]{2,1,0:T(8,128)} %all_to_all.36.received), custom_call_target="tpu_custom_call" | custom-call | tf_op jit(solution)/shard_map/collect/pallas_call | solution.py:640
  102.8 3.2 %all-to-all-start.6 = ((f32[4,8,128]{2,1,0:T(8,128)}), f32[4,8,128]{2,1,0:T(8,128)S(1)}, u32[]{:S(2)}, u32[]{:S(2)}) async-start(f32[4,8,128]{2,1,0:T(8,128)} %get-tuple-element.34), calls=%async_computation.6 | async-start | bytes 32768 | tf_op jit(solution)/shard_map/all_to_all | solution.py:450
  106.1 2.1 %marker_solution.1 = f32[6,12288]{1,0:T(8,128)} custom-call(f32[32,8,128]{2,1,0:T(8,128)} %copy-done, f32[4,8,128]{2,1,0:T(8,128)} %copy-done.3, f32[6,12288]{1,0:T(8,128)} %sol.1, f32[8,12288]{1,0:T(8,128)} %get-tuple-element.23.new_m.refs_7_.new), custom_call_target="tpu_custom_call" | custom-call | tf_op jit(solution)/shard_map/marker_solution/pallas_call | solution.py:637
  108.2 1.7 %all-to-all-done.6.norms = f32[4,8,128]{2,1,0:T(8,128)S(1)} async-done(((f32[4,8,128]{2,1,0:T(8,128)}), f32[4,8,128]{2,1,0:T(8,128)S(1)}, u32[]{:S(2)}, u32[]{:S(2)}) %all-to-all-start.6) | async-done | bytes 16416 | tf_op jit(solution)/shard_map/all_to_all | solution.py:450
  109.9 0.0 copy-start.4
  109.9 0.6 copy-done.4
  110.5 1.5 %reduction.1 = f32[1,1]{1,0:T(1,128)} custom-call(f32[32,8,128]{2,1,0:T(8,128)} %copy-done, f32[4,8,128]{2,1,0:T(8,128)} %copy-done.4), custom_call_target="tpu_custom_call" | custom-call | tf_op jit(solution)/shard_map/reduction/pallas_call | solution.py:645
Async XLA Ops:
  2.7 15.5 %all-to-all-start = ((f32[32,8,128]{2,1,0:T(8,128)}), f32[32,8,128]{2,1,0:T(8,128)S(1)}, u32[]{:S(2)}, u32[]{:S(2)}) async-start(f32[32,8,128]{2,1,0:T(8,128)} %totals.1), calls=%async_computation | async-start | bytes 262144 | tf_op jit(solution)/shard_map/all_to_all | solution.py:450
  18.2 0.7 copy-start
  21.4 13.6 %all-to-all-start.2 = ((f32[8,8,256]{2,1,0:T(8,128)}), f32[8,8,256]{2,1,0:T(8,128)S(1)}, u32[]{:S(2)}, u32[]{:S(2)}) async-start(f32[8,8,256]{2,1,0:T(8,128)} %get-tuple-element.24), calls=%async_computation.2 | async-start | bytes 131072 | tf_op jit(solution)/shard_map/all_to_all | solution.py:450
  35.0 3.9 %copy-start.1 = (f32[8,8,256]{2,1,0:T(8,128)}, f32[8,8,256]{2,1,0:T(8,128)S(1)}, u32[]{:S(2)}) copy-start(f32[8,8,256]{2,1,0:T(8,128)S(1)} %all-to-all-done.2.parents) | copy-start | bytes 196612
  35.0 8.6 %all-to-all-start.1 = ((f32[4,8,384]{2,1,0:T(8,128)}), f32[4,8,384]{2,1,0:T(8,128)S(1)}, u32[]{:S(2)}, u32[]{:S(2)}) async-start(f32[4,8,384]{2,1,0:T(8,128)} %get-tuple-element.21), calls=%async_computation.1 | async-start | bytes 98304 | tf_op jit(solution)/shard_map/all_to_all | solution.py:450
  43.6 0.6 copy-start.2
  74.1 7.1 %all-to-all-start.4 = ((f32[4,8,128]{2,1,0:T(8,128)}), f32[4,8,128]{2,1,0:T(8,128)S(1)}, u32[]{:S(2)}, u32[]{:S(2)}) async-start(f32[4,8,128]{2,1,0:T(8,128)} %spread.1), calls=%async_computation.4 | async-start | bytes 32768 | tf_op jit(solution)/shard_map/all_to_all | solution.py:450
  81.1 0.6 copy-start.3
  102.8 7.1 %all-to-all-start.6 = ((f32[4,8,128]{2,1,0:T(8,128)}), f32[4,8,128]{2,1,0:T(8,128)S(1)}, u32[]{:S(2)}, u32[]{:S(2)}) async-start(f32[4,8,128]{2,1,0:T(8,128)} %get-tuple-element.34), calls=%async_computation.6 | async-start | bytes 32768 | tf_op jit(solution)/shard_map/all_to_all | solution.py:450
  109.9 0.6 copy-start.4

commit v2 on v1

v2 whole, which is shorter than its diff:
```python
import functools

import jax
import jax.numpy as jnp
from jax import lax
from jax.experimental import pallas as pl
from jax.experimental.pallas import tpu as pltpu
from jax.sharding import PartitionSpec as P

F32 = jnp.float32
BF16 = jnp.bfloat16
PAD = 8
LANES = 128


def shape_of(*dims, dtype=F32):
    return jax.ShapeDtypeStruct(dims, dtype)


def call(kernel, out_shape, scratch=(), **options):
    return pl.pallas_call(kernel, out_shape=out_shape, scratch_shapes=list(scratch), **options)


def parts_of(values):
    high = values.astype(BF16).astype(F32)
    rest = values - high
    middle = rest.astype(BF16).astype(F32)
    return jnp.concatenate([high, middle, rest - middle], axis=0)


def add_parts(stacked):
    return stacked[:PAD] + stacked[PAD : 2 * PAD] + stacked[2 * PAD :]


ROWS_EACH = 3 * PAD


def one_hot(low, base):
    wanted = lax.broadcasted_iota(jnp.int32, (base, low.shape[1]), 0)
    return jnp.where(wanted == low, 1.0, 0.0).astype(BF16)


def dot(left, right):
    return lax.dot_general(left, right, (((1,), (0,)), ((), ())), preferred_element_type=F32)


def dot_t(left, right):
    return lax.dot_general(left, right, (((1,), (1,)), ((), ())), preferred_element_type=F32)


def select_blocks(products, high, first, count):
    total = None
    for h in range(count):
        block = add_parts(products[h * ROWS_EACH : (h + 1) * ROWS_EACH])
        block = jnp.where(high == first + h, block, 0.0)
        total = block if total is None else total + block
    return total


def masked_blocks(stacked, high, first, count):
    return jnp.concatenate(
        [jnp.where(high == first + h, stacked, 0.0) for h in range(count)], axis=0
    ).astype(BF16)


def fold(values):
    total = values[:, :LANES]
    for start in range(LANES, values.shape[1], LANES):
        total = total + values[:, start : start + LANES]
    return total


def load_matrix(matrix_ref, padded_ref):
    padded_ref[...] = jnp.zeros_like(padded_ref)
    size = matrix_ref.shape[0]
    padded_ref[:size, :size] = matrix_ref[...]


def apply_matrix(padded_ref, values, count):
    total = None
    for s in range(count):
        term = padded_ref[:, s : s + 1] * values[s : s + 1, :]
        total = term if total is None else total + term
    return total


def sums_of(received_ref):
    tile = received_ref[0]
    for i in range(1, received_ref.shape[0]):
        tile = tile + received_ref[i]
    return tile


def product_of(sums_ref):
    return jnp.sum(sums_of(sums_ref)[0:1], axis=1, keepdims=True)


def norm_of(sums_ref):
    return jnp.sum(sums_of(sums_ref)[1:2], axis=1, keepdims=True)


def two_sum(left, right):
    total = left + right
    back = total - left
    return total, (left - (total - back)) + (right - back)


def halves(values):
    scaled = values * 4097.0
    high = scaled - (scaled - values)
    return high, values - high


def two_product(left, left_halves, right, right_halves):
    product = left * right
    (lh, ll), (rh, rl) = left_halves, right_halves
    return product, ((lh * rh - product) + lh * rl + ll * rh) + ll * rl


def exact_sums(pairs):
    columns = []
    for left, right in pairs:
        lh, rh = halves(left), halves(right)
        for a, ah, b, bh in ((left, lh, left, lh), (left, lh, right, rh), (right, rh, right, rh)):
            columns.append(two_product(a, ah, b, bh))
    results = []
    for kind in range(3):
        total = error = None
        for product, rounding in columns[kind::3]:
            for start in range(0, product.shape[1], LANES):
                window = slice(start, start + LANES)
                if total is None:
                    total, error = product[:, window], rounding[:, window]
                else:
                    total, extra = two_sum(total, product[:, window])
                    error = error + (extra + rounding[:, window])
        row, rest = total[0:1], error[0:1]
        for t in range(1, total.shape[0]):
            row, extra = two_sum(row, total[t : t + 1])
            rest = rest + (extra + error[t : t + 1])
        results += [row, rest]
    return results


def rows_tile(rows):
    place = lax.broadcasted_iota(jnp.int32, (PAD, LANES), 0)
    tile = jnp.zeros((PAD, LANES), F32)
    for k, row in enumerate(rows):
        tile = jnp.where(place == k, row, tile)
    return tile


def exact_tile(tiles):
    total = tiles[0]
    error = jnp.zeros_like(total)
    for tile in tiles[1:]:
        total, extra = two_sum(total, tile)
        error = error + extra
    place = lax.broadcasted_iota(jnp.int32, (PAD, LANES), 0)
    errors = (place == 2) | (place == 4) | (place == 6)
    return total + jnp.where(errors, pltpu.roll(error, 1, 0), 0.0)


def is_packed(traits, share):
    return traits == 6 and share % (4 * LANES) == 0


def packed_width(traits, share):
    return share * 3 // 4 if is_packed(traits, share) else -(-share // LANES) * LANES


def spare_pieces(traits, share):
    main, rest = share * 3 // 4, share // 4
    return [
        (t, main, rest, traits + t // 3, t % 3 * rest)
        for t in range(traits if is_packed(traits, share) else 0)
    ]


def pack(out, i, values, traits, share):
    if not is_packed(traits, share):
        out[i, :, :share] = values
        return
    main = share * 3 // 4
    out[i, :traits, :main] = values[:traits, :main]
    for t, start, width, row, column in spare_pieces(traits, share):
        out[i, row : row + 1, column : column + width] = values[t : t + 1, start : start + width]


def totals_kernel(marker_weight, res_a, scal_a, res_m, scal_m, out, token):
    def pair(res_ref, scal_ref):
        res = res_ref[...]
        square = res * res
        return (
            jnp.sum(fold(square * scal_ref[...]), axis=0, keepdims=True),
            jnp.sum(fold(square), axis=0, keepdims=True),
        )

    product_a, norm_a = pair(res_a, scal_a)
    product_m, norm_m = pair(res_m, scal_m)
    tile = rows_tile([product_a + marker_weight * product_m, norm_a + marker_weight * norm_m])
    out[...] = jnp.broadcast_to(tile[None], out.shape)
    token[...] = tile


def prepare_kernel(
    bits,
    genotyped,
    token,
    res,
    scal,
    direction,
    send,
    row_index,
    search_out,
    direction_out,
    search_placed,
    direction_placed,
    search_ref,
    direction_ref,
):
    del token
    traits, animals = res.shape
    base = 1 << bits
    blocks = animals // base
    search_ref[...] = jnp.zeros_like(search_ref)
    direction_ref[...] = jnp.zeros_like(direction_ref)
    search_ref[:traits] = scal[...] * res[...]
    direction_ref[:traits] = direction[...]
    table = jnp.concatenate(
        [
            parts_of(ref[:, h * base : (h + 1) * base])
            for ref in (search_ref, direction_ref)
            for h in range(blocks)
        ],
        axis=0,
    ).astype(BF16)
    size = blocks * ROWS_EACH

    def one(r):
        index = send[pl.ds(r, 1), :]
        products = dot(table, one_hot(index & (base - 1), base))
        search_out[r] = select_blocks(products[:size], index >> bits, 0, blocks)
        direction_out[r] = select_blocks(products[size:], index >> bits, 0, blocks)

    if send.shape[0] <= 8:
        for r in range(send.shape[0]):
            one(r)
    else:
        pl.loop(0, send.shape[0])(one)

    blocks = -(-genotyped // base)
    width = 1024
    total = jnp.zeros((blocks * 2 * ROWS_EACH, base), F32)
    for start in range(0, animals, width):
        window = slice(start, start + width)
        index = row_index[:, window]
        stacked = jnp.concatenate(
            [parts_of(search_ref[:, window]), parts_of(direction_ref[:, window])], axis=0
        )
        total = total + dot_t(
            masked_blocks(stacked, index >> bits, 0, blocks), one_hot(index & (base - 1), base)
        )
    for h in range(blocks):
        size = min(base, genotyped - h * base)
        for k, out in enumerate((search_placed, direction_placed)):
            start = (2 * h + k) * ROWS_EACH
            block = add_parts(total[start : start + ROWS_EACH])
            out[:, h * base : h * base + size] = block[:, :size]


def animal_kernel(sums, previous, res, scal, direction, search_out, direction_out, new_ref, out):
    traits = res.shape[0]
    conjugacy = product_of(sums) / previous[...]
    new_ref[...] = jnp.zeros_like(new_ref)
    new_ref[:traits] = scal[...] * res[...] + conjugacy * direction[...]
    out[...] = search_out[...] + conjugacy.reshape(1, 1, 1) * direction_out[...]


def chunk_copies(genotypes, buffer, semaphores):
    width = buffer.shape[2]
    return [
        pltpu.make_async_copy(
            genotypes.at[:, i * width : (i + 1) * width], buffer.at[i], semaphores.at[i]
        )
        for i in range(buffer.shape[0])
    ]


def predict_kernel(
    sums,
    previous,
    res,
    scal,
    direction,
    genotypes,
    search_placed,
    direction_placed,
    new_m,
    out,
    buffer,
    semaphores,
):
    copies = chunk_copies(genotypes, buffer, semaphores)
    for copy in copies:
        copy.start()
    traits = res.shape[0]
    conjugacy = product_of(sums) / previous[...]
    difference = search_placed[...] + conjugacy * direction_placed[...]
    new_m[...] = jnp.zeros_like(new_m)
    new_m[:traits] = scal[...] * res[...] + conjugacy * direction[...]
    width = buffer.shape[2]
    total = None
    for i, copy in enumerate(copies):
        new = new_m[:, i * width : (i + 1) * width].astype(BF16)
        copy.wait()
        term = dot_t(new, buffer[i])
        total = term if total is None else total + term
    out[...] = jnp.broadcast_to((difference - total)[None], out.shape)


def pedigree_kernel(bits, parents, new_a, sire, dam, sampling_ref, back_ref, left_ref):
    owners, _, base = parents.shape
    animals = new_a.shape[1]
    for h in range(0, owners, 2):
        left_ref[h * ROWS_EACH : (h + 2) * ROWS_EACH, :] = jnp.concatenate(
            [parts_of(parents[h]), parts_of(parents[h + 1])], axis=0
        ).astype(BF16)
    group = min(8, owners)
    groups = owners // group
    width = 1024
    slots = owners * base
    back_ref[...] = jnp.zeros_like(back_ref)
    for start in range(0, animals, width):
        window = slice(start, start + width)
        sire_index, dam_index = sire[:, window], dam[:, window]
        sire_high, dam_high = sire_index >> bits, dam_index >> bits
        sire_hot = one_hot(sire_index & (base - 1), base)
        dam_hot = one_hot(dam_index & (base - 1), base)
        gathered = jnp.zeros((PAD, width), F32)
        for g in range(groups):
            left = left_ref[g * group * ROWS_EACH : (g + 1) * group * ROWS_EACH, :]
            gathered = gathered + (
                select_blocks(dot(left, sire_hot), sire_high, g * group, group)
                + select_blocks(dot(left, dam_hot), dam_high, g * group, group)
            )
        known = (sire_index < slots).astype(F32) + (dam_index < slots).astype(F32)
        mendel = 1.0 / (1.0 - 0.25 * known)
        sampling = mendel * (new_a[:, window] - 0.5 * gathered)
        sampling_ref[:, window] = sampling
        stacked = parts_of(-0.5 * sampling)
        for g in range(groups):
            total = dot_t(masked_blocks(stacked, sire_high, g * group, group), sire_hot) + dot_t(
                masked_blocks(stacked, dam_high, g * group, group), dam_hot
            )
            for h in range(group):
                back_ref[g * group + h] += add_parts(total[h * ROWS_EACH : (h + 1) * ROWS_EACH])


def deviation_kernel(
    share,
    traits,
    differences,
    genomic,
    genotypes,
    back,
    deviation_ref,
    out,
    genomic_ref,
    buffer,
    semaphores,
):
    copies = chunk_copies(genotypes, buffer, semaphores)
    for copy in copies:
        copy.start()
    load_matrix(genomic, genomic_ref)
    deviation = apply_matrix(genomic_ref, sums_of(differences), traits)
    deviation_ref[...] = deviation
    rounded = deviation.astype(BF16)
    start = out.shape[2] - back.shape[2]
    out[:, :, start:] = back[...]
    per_chunk = buffer.shape[2] // share
    for i, copy in enumerate(copies):
        copy.wait()
        terms = dot(rounded, buffer[i])
        for j in range(per_chunk):
            pack(out, i * per_chunk + j, terms[:, j * share : (j + 1) * share], traits, share)


def record_kernel(token, sampling, new_a, pattern, table, genetic, out, matrix_ref):
    del token
    traits = genetic.shape[0]
    patterns = table.shape[1]
    load_matrix(genetic, matrix_ref)
    values = table[...]
    high = values.astype(BF16).astype(F32)
    rest = values - high
    middle = rest.astype(BF16).astype(F32)
    stacked = jnp.concatenate([high, middle, rest - middle], axis=0).astype(BF16)
    width = 1024
    size = traits * PAD
    for start in range(0, new_a.shape[1], width):
        window = slice(start, start + width)
        new = new_a[:, window]
        blocks = dot(stacked, one_hot(pattern[:, window], patterns))
        total = apply_matrix(matrix_ref, sampling[:, window], traits)
        for s in range(traits):
            row = slice(s * PAD, (s + 1) * PAD)
            block = blocks[row] + blocks[size:][row] + blocks[2 * size :][row]
            total = total + block * new[s : s + 1, :]
        out[:, window] = total


def image_kernel(
    bits,
    share,
    row,
    received,
    send,
    base_image,
    deviation,
    row_index,
    genetic,
    marker_inverse,
    new_a,
    res_a,
    new_share,
    res_share,
    image_a,
    out,
    matrix_ref,
    marker_ref,
    table_ref,
    terms_ref,
    res_ref,
):
    del row
    owners = received.shape[0]
    base = 1 << bits
    traits = genetic.shape[0]
    animals = base_image.shape[1]
    genotyped = deviation.shape[1]
    width = packed_width(traits, share)
    load_matrix(genetic, matrix_ref)
    load_matrix(marker_inverse, marker_ref)
    blocks = animals // base

    def scatter(r, total):
        index = send[pl.ds(r, 1), :]
        stacked = parts_of(received[r, :, width:])
        return total + dot_t(
            masked_blocks(stacked, index >> bits, 0, blocks), one_hot(index & (base - 1), base)
        )

    total = jnp.zeros((blocks * ROWS_EACH, base), F32)
    if owners <= 8:
        for r in range(owners):
            total = scatter(r, total)
    else:
        total = lax.fori_loop(0, owners, scatter, total)
    table_ref[...] = jnp.zeros_like(table_ref)
    table_ref[:, :genotyped] = deviation[...]
    places = table_ref.shape[1] // base
    table = jnp.concatenate(
        [parts_of(table_ref[:, h * base : (h + 1) * base]) for h in range(places)], axis=0
    ).astype(BF16)
    for h in range(blocks):
        window = slice(h * base, (h + 1) * base)
        index = row_index[:, window]
        gathered = add_parts(total[h * ROWS_EACH : (h + 1) * ROWS_EACH])
        genomic_term = select_blocks(
            dot(table, one_hot(index & (base - 1), base)), index >> bits, 0, places
        )
        image_a[:, window] = (
            base_image[:, window] + apply_matrix(matrix_ref, gathered, traits) + genomic_term
        )

    summed = received[0, :, :width]
    for i in range(1, owners):
        summed = summed + received[i, :, :width]
    terms_ref[...] = jnp.zeros_like(terms_ref)
    res_ref[...] = jnp.zeros_like(res_ref)
    res_ref[:traits, :share] = res_share[...]
    if is_packed(traits, share):
        main = share * 3 // 4
        terms_ref[:traits, :main] = summed[:traits, :main]
        for t, start, size, place, column in spare_pieces(traits, share):
            terms_ref[t : t + 1, start : start + size] = summed[
                place : place + 1, column : column + size
            ]
    else:
        terms_ref[:, :width] = summed
    new = new_share[...]
    image = apply_matrix(marker_ref, new, traits) - terms_ref[:, :share]
    terms_ref[:, :share] = image
    curvature = fold(new_a[...] * image_a[...])
    if share % LANES == 0:
        curvature = curvature + fold(new * image)
        curvature = jnp.sum(curvature, axis=0, keepdims=True)
    else:
        rest = jnp.sum(jnp.sum(new * image, axis=1, keepdims=True), axis=0, keepdims=True)
        first = lax.broadcasted_iota(jnp.int32, (1, LANES), 1) == 0
        curvature = jnp.sum(curvature, axis=0, keepdims=True) + jnp.where(first, rest, 0.0)
    tile = rows_tile(
        [curvature]
        + exact_sums(
            [
                (res_a[...], image_a[:traits]),
                (res_ref[:traits], terms_ref[:traits]),
            ]
        )
    )
    for i in range(owners):
        if not is_packed(traits, share):
            out[i] = jnp.zeros(out.shape[1:], F32)
        pack(out, i, image, traits, share)
        out[i, :, width:] = tile


def spread_kernel(received, out):
    start = received.shape[2] - LANES
    tile = exact_tile([received[i, :, start:] for i in range(received.shape[0])])
    out[...] = jnp.broadcast_to(tile[None], out.shape)


def final_kernel(
    share,
    sums,
    tiles,
    sol_a,
    res_a,
    new_a,
    image_a,
    sol_m,
    res_m,
    new_m,
    gathered,
    next_sol_a,
    next_sol_m,
    next_res_a,
    next_res_m,
    reduction,
):
    traits = sol_a.shape[0]
    tile = exact_tile([tiles[i] for i in range(tiles.shape[0])])
    step = product_of(sums) / jnp.sum(tile[0:1], axis=1, keepdims=True)
    next_sol_a[...] = sol_a[...] + step * new_a[:traits]
    next_res_a[...] = res_a[...] - step * image_a[:traits]
    next_sol_m[...] = sol_m[...] + step * new_m[:traits]
    for i in range(gathered.shape[0]):
        left = i * share
        if is_packed(traits, share):
            main = share * 3 // 4
            window = slice(left, left + main)
            next_res_m[:, window] = res_m[:, window] - step * gathered[i, :traits, :main]
            for t, start, size, place, column in spare_pieces(traits, share):
                window = slice(left + start, left + start + size)
                next_res_m[t : t + 1, window] = (
                    res_m[t : t + 1, window]
                    - step * gathered[i, place : place + 1, column : column + size]
                )
        else:
            window = slice(left, left + share)
            next_res_m[:, window] = res_m[:, window] - step * gathered[i, :traits, :share]

    step_row = jnp.broadcast_to(step, (1, LANES))
    step_halves = halves(step_row)

    def times_step(total, error):
        product, rounding = two_product(total, halves(total), step_row, step_halves)
        return product, rounding + error * step_row

    cross, cross_error = times_step(tile[3:4], tile[4:5])
    square, square_error = times_step(*times_step(tile[5:6], tile[6:7]))
    total, first = two_sum(tile[1:2], -2.0 * cross)
    total, second = two_sum(total, square)
    norm = total + (first + second + tile[2:3] - 2.0 * cross_error + square_error)
    reduction[...] = jnp.sum(norm, axis=1, keepdims=True) / norm_of(sums)


def exchange(values, axes):
    return lax.all_to_all(values, axes, split_axis=0, concat_axis=0, tiled=True)


def local(
    solution_animal,
    solution_marker,
    residual_animal,
    residual_marker,
    direction_animal,
    direction_marker,
    scaling_animal,
    scaling_marker,
    previous_product,
    genotypes,
    genetic_inverse,
    genomic_inverse,
    marker_inverse,
    residual_table,
    pattern,
    sire_slot,
    dam_slot,
    genotype_row,
    send_list,
):
    traits, animals = residual_animal.shape
    markers = residual_marker.shape[1]
    genotyped = genotypes.shape[0]
    rows = lax.axis_size("rows")
    columns = lax.axis_size("mk")
    capacity = send_list.shape[3]
    bits = capacity.bit_length() - 1
    share = markers // rows
    patterns = residual_table.shape[0]
    row = lax.axis_index("rows").astype(jnp.int32).reshape(1)
    previous = previous_product.reshape(1, 1)
    send = send_list.reshape(rows, capacity)
    sire, dam = sire_slot.reshape(1, animals), dam_slot.reshape(1, animals)
    kinds, places = pattern.reshape(1, animals), genotype_row.reshape(1, animals)
    table = jnp.pad(jnp.transpose(residual_table, (2, 1, 0)), ((0, 0), (0, PAD - traits), (0, 0)))
    table = table.reshape(traits * PAD, patterns)

    animal_block = shape_of(PAD, animals)
    slot_block = shape_of(rows, PAD, capacity)
    tile = shape_of(PAD, LANES)
    local_sums, token = call(
        functools.partial(totals_kernel, 1.0 / rows),
        (shape_of(rows * columns, PAD, LANES), tile),
        name="totals",
    )(residual_animal, scaling_animal, residual_marker, scaling_marker)
    sums = exchange(local_sums, ("rows", "mk"))
    search_out, direction_out, search_placed, direction_placed = call(
        functools.partial(prepare_kernel, bits, genotyped),
        (slot_block, slot_block, shape_of(PAD, genotyped), shape_of(PAD, genotyped)),
        (pltpu.VMEM((PAD, animals), F32), pltpu.VMEM((PAD, animals), F32)),
        name="prepare",
    )(token, residual_animal, scaling_animal, direction_animal, send, places)
    sums, table = lax.optimization_barrier((sums, table))
    new_animal, outgoing = call(animal_kernel, (animal_block, slot_block), name="animals")(
        sums,
        previous,
        residual_animal,
        scaling_animal,
        direction_animal,
        search_out,
        direction_out,
    )
    parents = exchange(outgoing, "rows")

    def whole(count):
        return [pl.BlockSpec(memory_space=pltpu.VMEM)] * count

    off_chip = [pl.BlockSpec(memory_space=pl.ANY)]
    chunk = 2 * share * max(1, 1536 // share)
    new_marker, difference = call(
        predict_kernel,
        (shape_of(PAD, markers), shape_of(columns, PAD, genotyped)),
        (
            pltpu.VMEM((markers // chunk, genotyped, chunk), BF16),
            pltpu.SemaphoreType.DMA((markers // chunk,)),
        ),
        in_specs=whole(5) + off_chip + whole(2),
        name="predict",
    )(
        sums,
        previous,
        residual_marker,
        scaling_marker,
        direction_marker,
        genotypes,
        search_placed,
        direction_placed,
    )
    differences = exchange(difference, "mk")
    sampling, back = call(
        functools.partial(pedigree_kernel, bits),
        (animal_block, slot_block),
        (pltpu.VMEM((rows * ROWS_EACH, capacity), BF16),),
        name="pedigree",
    )(parents, new_animal, sire, dam)
    chunk = share * max(1, 1536 // share)
    width = packed_width(traits, share)
    deviation, payload = call(
        functools.partial(deviation_kernel, share, traits),
        (shape_of(PAD, genotyped), shape_of(rows, PAD, width + capacity)),
        (
            pltpu.VMEM((PAD, LANES), F32),
            pltpu.VMEM((markers // chunk, genotyped, chunk), BF16),
            pltpu.SemaphoreType.DMA((markers // chunk,)),
        ),
        in_specs=whole(2) + off_chip + whole(1),
        name="deviation",
    )(differences, genomic_inverse, genotypes, back)
    received = exchange(payload, "rows")
    base_image = call(record_kernel, animal_block, (pltpu.VMEM((PAD, LANES), F32),), name="record")(
        deviation, sampling, new_animal, kinds, table, genetic_inverse
    )

    if share % LANES:
        start = row[0] * share
        new_share = lax.dynamic_slice_in_dim(new_marker, start, share, 1)
        res_share = lax.dynamic_slice_in_dim(residual_marker, start, share, 1)

        def own(height):
            return pl.BlockSpec((height, share), lambda k, r: (0, 0))
    else:
        new_share, res_share = new_marker, residual_marker

        def own(height):
            return pl.BlockSpec((height, share), lambda k, r: (0, r[0]))

    def still(array):
        return pl.BlockSpec(array.shape, lambda k, r, n=len(array.shape): (0,) * n)

    out_shape = shape_of(rows, PAD, width + LANES)
    full = -(-share // LANES) * LANES
    inputs = (
        received,
        send,
        base_image,
        deviation,
        places,
        genetic_inverse,
        marker_inverse,
        new_animal,
        residual_animal,
    )
    image_animal, payload = pl.pallas_call(
        functools.partial(image_kernel, bits, share),
        out_shape=(animal_block, out_shape),
        grid_spec=pltpu.PrefetchScalarGridSpec(
            num_scalar_prefetch=1,
            grid=(1,),
            in_specs=[still(array) for array in inputs] + [own(PAD), own(traits)],
            out_specs=(still(animal_block), still(out_shape)),
            scratch_shapes=[
                pltpu.VMEM((PAD, LANES), F32),
                pltpu.VMEM((PAD, LANES), F32),
                pltpu.VMEM((PAD, -(-genotyped // capacity) * capacity), F32),
                pltpu.VMEM((PAD, full), F32),
                pltpu.VMEM((PAD, full), F32),
            ],
        ),
        name="image",
    )(row, *inputs, new_share, res_share)
    gathered = exchange(payload, "rows")
    tiles = exchange(
        call(spread_kernel, shape_of(columns, PAD, LANES), name="spread")(gathered), "mk"
    )
    *outputs, reduction = call(
        functools.partial(final_kernel, share),
        (
            shape_of(traits, animals),
            shape_of(traits, markers),
            shape_of(traits, animals),
            shape_of(traits, markers),
            shape_of(1, 1),
        ),
        name="final",
    )(
        sums,
        tiles,
        solution_animal,
        residual_animal,
        new_animal,
        image_animal,
        solution_marker,
        residual_marker,
        new_marker,
        gathered,
    )
    return (*outputs, reduction.reshape(()))


def solution(mesh):
    animal, marker = P(None, ("rows", "mk")), P(None, "mk")
    index = P(("rows", "mk"))
    return jax.shard_map(
        local,
        mesh=mesh,
        in_specs=(
            animal,
            marker,
            animal,
            marker,
            animal,
            marker,
            animal,
            marker,
            P(),
            P("rows", "mk"),
            P(),
            P(),
            P(),
            P(),
            index,
            index,
            index,
            index,
            P("rows", "mk", None, None),
        ),
        out_specs=(animal, marker, animal, marker, P()),
        check_vma=False,
    )
```

time: 113 us -> 95.7 us (0.85)
  blocking collectives: 37.4 us -> 22.6 us
  Pallas kernels: 38.8 us -> 35.1 us
  waiting for transfers between devices: 10.3 us -> 12.4 us
    all_to_all x2, blocking collectives: 37.4 us -> 22.6 us  [exchange(): return lax.all_to_all(values, axes, split_axis=0, concat_axis=0, tiled=True)]
    pallas_call x11 -> x10, Pallas kernels: 38.8 us -> 35.1 us  [the longest x1 7.69 us: local(): call(predict_kernel, (shape_of(PAD, markers), shape_of(columns, PAD, geno...]
    all_to_all x5 -> x4, waiting for transfers between devices: 10.3 us -> 12.4 us  [exchange(): return lax.all_to_all(values, axes, split_axis=0, concat_axis=0, tiled=True)]
    all_to_all x5 -> x4, starting transfers between devices: 20.5 us -> 19.9 us  [exchange(): return lax.all_to_all(values, axes, split_axis=0, concat_axis=0, tiled=True)]
    unnamed x11 -> x9, local copies, waits for them, and re-layouts: 3.22 us -> 2.75 us
  transfers between devices with their start and end apart: 5 -> 4, of which waited for: 3 -> 2; matrix products, arithmetic and copies ran while one was open for 1% -> 1% of each run, Pallas kernels for 17% -> 19%
where the time goes in v2:
time: 95.7 us; the launch traced here: 94.8 us
  Pallas kernels  35.1 us (37%)
  blocking collectives  22.6 us (24%)
  starting transfers between devices  19.9 us (21%)
  waiting for transfers between devices  12.4 us (13%)
  local copies, waits for them, and re-layouts  3.35 us (4%)
  between operations  1.35 us (1%)
    all_to_all x2, blocking collectives, exchange(): return lax.all_to_all(values, axes, split_axis=0, concat_axis=0, tiled=True)  22.6 us
    all_to_all x4, starting transfers between devices, exchange(): return lax.all_to_all(values, axes, split_axis=0, concat_axis=0, tiled=True)  19.9 us
    all_to_all x4, waiting for transfers between devices, exchange(): return lax.all_to_all(values, axes, split_axis=0, concat_axis=0, tiled=True)  12.4 us
    pallas_call x1, Pallas kernels, local(): call(predict_kernel, (shape_of(PAD, markers), shape_of(columns, PAD, geno...  7.69 us
    pallas_call x1, Pallas kernels, local(): call(functools.partial(deviation_kernel, share, traits), (shape_of(PAD, g...  5.7 us
    pallas_call x1, Pallas kernels, local(): call(functools.partial(pedigree_kernel, bits), (animal_block, slot_block)...  4.57 us
    pallas_call x1, Pallas kernels, local(): pl.pallas_call(functools.partial(image_kernel, bits, share), out_shape=(a...  3.46 us
    pallas_call x1, Pallas kernels, local(): call(functools.partial(prepare_kernel, bits, genotyped), (slot_block, slo...  3.27 us
  transfers between devices with their start and end apart: 4, of which 2 were waited for; matrix products, arithmetic and copies ran while one was open for 1% of the time, Pallas kernels for 19%

profile of v2, /device:TPU:0, one launch (start us, length us, event | category | flops | bytes accessed | tf_op | source)
XLA Modules:
  0.0 94.8 jit_solution(16441530455895816041)
XLA Ops:
  0.6 2.0 %totals.1 = (f32[32,8,128]{2,1,0:T(8,128)}, f32[8,128]{1,0:T(8,128)}) custom-call(f32[6,4096]{1,0:T(8,128)} %res_a.5, f32[6,4096]{1,0:T(8,128)} %scal.5, f32[6,12288]{1,0:T(8,128)} %res_m.3, f32[6,12288]{1,0:T(8,128)} %scal.4), custom_call_target="tpu_custom_call" | custom-call | tf_op jit(solution)/shard_map/totals/pallas_call | solution.py:626
  2.7 7.3 %all-to-all-start = ((f32[32,8,128]{2,1,0:T(8,128)}), f32[32,8,128]{2,1,0:T(8,128)S(1)}, u32[]{:S(2)}, u32[]{:S(2)}) async-start(f32[32,8,128]{2,1,0:T(8,128)} %get-tuple-element.28), calls=%async_computation | async-start | bytes 262144 | tf_op jit(solution)/shard_map/all_to_all | solution.py:582
  10.6 0.7 copy.25
  11.4 3.3 %prepare.1 = (f32[8,8,256]{2,1,0:T(8,128)}, f32[8,8,256]{2,1,0:T(8,128)}, f32[8,384]{1,0:T(8,128)}, f32[8,384]{1,0:T(8,128)}) custom-call(f32[8,128]{1,0:T(8,128)} %get-tuple-element.30.token, f32[6,4096]{1,0:T(8,128)} %res_a.5, f32[6,4096]{1,0:T(8,128)} %scal.5, f32[6,4096]{1,0:T(8,128)} %direction.5, s32[8,256]{1,0:T(8,128)} %bitcast.15, s32[1,4096]{1,0:T(1,128)} %bitcast.13), custom_call_target="tpu_custom_call" | custom-call | tf_op jit(solution)/shard_map/prepare/pallas_call | solution.py:632
  14.7 0.6 pad_bitcast_fusion.table
  15.3 2.9 %all-to-all-done.sums = f32[32,8,128]{2,1,0:T(8,128)S(1)} async-done(((f32[32,8,128]{2,1,0:T(8,128)}), f32[32,8,128]{2,1,0:T(8,128)S(1)}, u32[]{:S(2)}, u32[]{:S(2)}) %all-to-all-start) | async-done | bytes 131104 | tf_op jit(solution)/shard_map/all_to_all | solution.py:582
  18.2 0.0 copy-start
  18.2 0.6 copy-done
  18.8 1.9 %animals.1 = (f32[8,4096]{1,0:T(8,128)}, f32[8,8,256]{2,1,0:T(8,128)}) custom-call(f32[32,8,128]{2,1,0:T(8,128)} %copy-done, f32[1,1]{1,0:T(1,128)} %bitcast.12.previous, f32[6,4096]{1,0:T(8,128)} %res_a.5, f32[6,4096]{1,0:T(8,128)} %scal.5, f32[6,4096]{1,0:T(8,128)} %direction.5, f32[8,8,256]{2,1,0:T(8,128)} %get-tuple-element.34.search_out, ...), custom_call_target="tpu_custom_call" | custom-call | tf_op jit(solution)/shard_map/animals/pallas_call | solution.py:639
  20.8 3.4 %all-to-all-start.2 = ((f32[8,8,256]{2,1,0:T(8,128)}), f32[8,8,256]{2,1,0:T(8,128)S(1)}, u32[]{:S(2)}, u32[]{:S(2)}) async-start(f32[8,8,256]{2,1,0:T(8,128)} %get-tuple-element.36), calls=%async_computation.2 | async-start | bytes 131072 | tf_op jit(solution)/shard_map/all_to_all | solution.py:582
  24.1 7.7 %predict.1 = (f32[8,12288]{1,0:T(8,128)}, f32[4,8,384]{2,1,0:T(8,128)}) custom-call(f32[32,8,128]{2,1,0:T(8,128)} %copy-done, f32[1,1]{1,0:T(1,128)} %bitcast.11.previous, f32[6,12288]{1,0:T(8,128)} %res_m.3, f32[6,12288]{1,0:T(8,128)} %scal.4, f32[6,12288]{1,0:T(8,128)} %direction.4, bf16[384,12288]{1,0:T(8,128)(2,1)} %genotypes.3, ...), custom_call_target="tpu_custom_call" | custom-call | tf_op jit(solution)/shard_map/predict/pallas_call | solution.py:655
  31.8 0.0 all-to-all-done.2.parents
  31.9 0.0 copy-start.2
  31.9 3.3 %all-to-all-start.1 = ((f32[4,8,384]{2,1,0:T(8,128)}), f32[4,8,384]{2,1,0:T(8,128)S(1)}, u32[]{:S(2)}, u32[]{:S(2)}) async-start(f32[4,8,384]{2,1,0:T(8,128)} %get-tuple-element.33), calls=%async_computation.1 | async-start | bytes 98304 | tf_op jit(solution)/shard_map/all_to_all | solution.py:582
  35.2 0.0 copy-done.2
  35.2 4.6 %pedigree.1 = (f32[8,4096]{1,0:T(8,128)}, f32[8,8,256]{2,1,0:T(8,128)}) custom-call(f32[8,8,256]{2,1,0:T(8,128)} %copy-done.2, f32[8,4096]{1,0:T(8,128)} %get-tuple-element.37.new_a, s32[1,4096]{1,0:T(1,128)} %bitcast.19, s32[1,4096]{1,0:T(1,128)} %bitcast.20), custom_call_target="tpu_custom_call" | custom-call | tf_op jit(solution)/shard_map/pedigree/pallas_call | solution.py:675
  39.7 0.0 all-to-all-done.1.differences
  39.7 0.0 copy-start.3
  39.7 0.6 copy-done.3
  40.4 5.7 %deviation.1 = (f32[8,384]{1,0:T(8,128)}, f32[8,8,1408]{2,1,0:T(8,128)}) custom-call(f32[4,8,384]{2,1,0:T(8,128)} %copy-done.3, f32[6,6]{1,0:T(8,128)} %genomic.1, bf16[384,12288]{1,0:T(8,128)(2,1)} %genotypes.3, f32[8,8,256]{2,1,0:T(8,128)} %get-tuple-element.38.back), custom_call_target="tpu_custom_call" | custom-call | tf_op jit(solution)/shard_map/deviation/pallas_call | solution.py:683
  46.1 5.9 %all-to-all-start.3 = ((f32[8,8,1408]{2,1,0:T(8,128)}), f32[8,8,1408]{2,1,0:T(8,128)S(1)}, u32[]{:S(2)}, u32[]{:S(2)}) async-start(f32[8,8,1408]{2,1,0:T(8,128)} %get-tuple-element.39), calls=%async_computation.3 | async-start | bytes 720896 | tf_op jit(solution)/shard_map/all_to_all | solution.py:582
  52.0 2.1 %record.1.base_image = f32[8,4096]{1,0:T(8,128)} custom-call(f32[8,384]{1,0:T(8,128)} %get-tuple-element.40.token.deviation, f32[8,4096]{1,0:T(8,128)} %get-tuple-element.41.sampling, f32[8,4096]{1,0:T(8,128)} %get-tuple-element.37.new_a, s32[1,4096]{1,0:T(1,128)} %bitcast.18, f32[48,64]{1,0:T(8,128)} %pad_bitcast_fusion.table, f32[6,6]{1,0:T(8,128)} %genetic.3), custom_call_target="tpu_custom_call" | custom-call | tf_op jit(solution)/shard_map/record/pallas_call | solution.py:695
  54.1 9.5 %all-to-all-done.3.received = f32[8,8,1408]{2,1,0:T(8,128)S(1)} async-done(((f32[8,8,1408]{2,1,0:T(8,128)}), f32[8,8,1408]{2,1,0:T(8,128)S(1)}, u32[]{:S(2)}, u32[]{:S(2)}) %all-to-all-start.3) | async-done | bytes 360480 | tf_op jit(solution)/shard_map/all_to_all | solution.py:582
  63.6 0.0 copy-start.1
  63.6 0.7 copy-done.1
  64.3 3.5 %image.1 = (f32[8,4096]{1,0:T(8,128)}, f32[8,8,1280]{2,1,0:T(8,128)}) custom-call(s32[1]{0:T(128)} %bitcast.2.row, f32[8,8,1408]{2,1,0:T(8,128)} %copy-done.1, s32[8,256]{1,0:T(8,128)} %bitcast.16, f32[8,4096]{1,0:T(8,128)} %record.1.base_image, f32[8,384]{1,0:T(8,128)} %get-tuple-element.40.token.deviation, s32[1,4096]{1,0:T(1,128)} %bitcast.14, ...), custom_call_target="tpu_custom_call" | custom-call | tf_op jit(solution)/shard_map/image/pallas_call | solution.py:728
  67.8 14.9 %all_to_all.30.received.gathered = f32[8,8,1280]{2,1,0:T(8,128)} all-to-all(f32[8,8,1280]{2,1,0:T(8,128)} %get-tuple-element.44), channel_id=1, replica_groups=mesh['rows'=8,'mk'=4] {'rows'}, dimensions={0} | all-to-all | bytes 655360 | tf_op jit(solution)/shard_map/all_to_all | solution.py:582
  82.7 1.6 %spread.1 = f32[4,8,128]{2,1,0:T(8,128)} custom-call(f32[8,8,1280]{2,1,0:T(8,128)} %all_to_all.30.received.gathered), custom_call_target="tpu_custom_call" | custom-call | tf_op jit(solution)/shard_map/spread/pallas_call | solution.py:748
  84.3 7.8 %all_to_all.31.tiles = f32[4,8,128]{2,1,0:T(8,128)} all-to-all(f32[4,8,128]{2,1,0:T(8,128)} %spread.1), channel_id=1, replica_groups=mesh['rows'=8,'mk'=4] {'mk'}, dimensions={0} | all-to-all | bytes 32768 | tf_op jit(solution)/shard_map/all_to_all | solution.py:582
  92.1 2.7 %final.1 = (f32[6,4096]{1,0:T(8,128)}, f32[6,12288]{1,0:T(8,128)}, f32[6,4096]{1,0:T(8,128)}, f32[6,12288]{1,0:T(8,128)}, f32[1,1]{1,0:T(1,128)}) custom-call(f32[32,8,128]{2,1,0:T(8,128)} %copy-done, f32[4,8,128]{2,1,0:T(8,128)} %all_to_all.31.tiles, f32[6,4096]{1,0:T(8,128)} %sol_a.1, f32[6,4096]{1,0:T(8,128)} %res_a.5, ...), custom_call_target="tpu_custom_call" | custom-call | tf_op jit(solution)/shard_map/final/pallas_call | solution.py:750
Async XLA Ops:
  2.7 15.5 %all-to-all-start = ((f32[32,8,128]{2,1,0:T(8,128)}), f32[32,8,128]{2,1,0:T(8,128)S(1)}, u32[]{:S(2)}, u32[]{:S(2)}) async-start(f32[32,8,128]{2,1,0:T(8,128)} %get-tuple-element.28), calls=%async_computation | async-start | bytes 262144 | tf_op jit(solution)/shard_map/all_to_all | solution.py:582
  18.2 0.6 copy-start
  20.8 11.1 %all-to-all-start.2 = ((f32[8,8,256]{2,1,0:T(8,128)}), f32[8,8,256]{2,1,0:T(8,128)S(1)}, u32[]{:S(2)}, u32[]{:S(2)}) async-start(f32[8,8,256]{2,1,0:T(8,128)} %get-tuple-element.36), calls=%async_computation.2 | async-start | bytes 131072 | tf_op jit(solution)/shard_map/all_to_all | solution.py:582
  31.9 3.3 %copy-start.2 = (f32[8,8,256]{2,1,0:T(8,128)}, f32[8,8,256]{2,1,0:T(8,128)S(1)}, u32[]{:S(2)}) copy-start(f32[8,8,256]{2,1,0:T(8,128)S(1)} %all-to-all-done.2.parents) | copy-start | bytes 196612
  31.9 7.9 %all-to-all-start.1 = ((f32[4,8,384]{2,1,0:T(8,128)}), f32[4,8,384]{2,1,0:T(8,128)S(1)}, u32[]{:S(2)}, u32[]{:S(2)}) async-start(f32[4,8,384]{2,1,0:T(8,128)} %get-tuple-element.33), calls=%async_computation.1 | async-start | bytes 98304 | tf_op jit(solution)/shard_map/all_to_all | solution.py:582
  39.7 0.6 copy-start.3
  46.1 17.5 %all-to-all-start.3 = ((f32[8,8,1408]{2,1,0:T(8,128)}), f32[8,8,1408]{2,1,0:T(8,128)S(1)}, u32[]{:S(2)}, u32[]{:S(2)}) async-start(f32[8,8,1408]{2,1,0:T(8,128)} %get-tuple-element.39), calls=%async_computation.3 | async-start | bytes 720896 | tf_op jit(solution)/shard_map/all_to_all | solution.py:582
  63.6 0.7 copy-start.1

commit v3 on v2

--- a/solution.py
+++ b/solution.py
@@ -17,8 +17,17 @@
     return jax.ShapeDtypeStruct(dims, dtype)
 
 
+LIMIT = pltpu.CompilerParams(vmem_limit_bytes=24 << 20)
+
+
 def call(kernel, out_shape, scratch=(), **options):
-    return pl.pallas_call(kernel, out_shape=out_shape, scratch_shapes=list(scratch), **options)
+    return pl.pallas_call(
+        kernel,
+        out_shape=out_shape,
+        scratch_shapes=list(scratch),
+        compiler_params=LIMIT,
+        **options,
+    )
 
 
 def parts_of(values):
@@ -212,12 +221,17 @@
     direction,
     send,
     row_index,
+    res_m,
+    scal_m,
+    direction_m,
     search_out,
     direction_out,
     search_placed,
     direction_placed,
     search_ref,
     direction_ref,
+    search_m,
+    direction_m8,
 ):
     del token
     traits, animals = res.shape
@@ -267,31 +281,35 @@
             start = (2 * h + k) * ROWS_EACH
             block = add_parts(total[start : start + ROWS_EACH])
             out[:, h * base : h * base + size] = block[:, :size]
-
-
-def animal_kernel(sums, previous, res, scal, direction, search_out, direction_out, new_ref, out):
-    traits = res.shape[0]
+    search_m[...] = jnp.zeros_like(search_m)
+    direction_m8[...] = jnp.zeros_like(direction_m8)
+    search_m[:traits] = scal_m[...] * res_m[...]
+    direction_m8[:traits] = direction_m[...]
+
+
+def animal_kernel(sums, previous, search, direction, search_out, direction_out, new_ref, out):
     conjugacy = product_of(sums) / previous[...]
-    new_ref[...] = jnp.zeros_like(new_ref)
-    new_ref[:traits] = scal[...] * res[...] + conjugacy * direction[...]
+    new_ref[...] = search[...] + conjugacy * direction[...]
     out[...] = search_out[...] + conjugacy.reshape(1, 1, 1) * direction_out[...]
 
 
 def chunk_copies(genotypes, buffer, semaphores):
     width = buffer.shape[2]
-    return [
+    copies = [
         pltpu.make_async_copy(
             genotypes.at[:, i * width : (i + 1) * width], buffer.at[i], semaphores.at[i]
         )
         for i in range(buffer.shape[0])
     ]
+    for copy in copies:
+        copy.start()
+    return copies
 
 
 def predict_kernel(
     sums,
     previous,
-    res,
-    scal,
+    search,
     direction,
     genotypes,
     search_placed,
@@ -302,21 +320,15 @@
     semaphores,
 ):
     copies = chunk_copies(genotypes, buffer, semaphores)
-    for copy in copies:
-        copy.start()
-    traits = res.shape[0]
     conjugacy = product_of(sums) / previous[...]
-    difference = search_placed[...] + conjugacy * direction_placed[...]
-    new_m[...] = jnp.zeros_like(new_m)
-    new_m[:traits] = scal[...] * res[...] + conjugacy * direction[...]
+    new_m[...] = search[...] + conjugacy * direction[...]
+    total = search_placed[...] + conjugacy * direction_placed[...]
     width = buffer.shape[2]
-    total = None
     for i, copy in enumerate(copies):
         new = new_m[:, i * width : (i + 1) * width].astype(BF16)
         copy.wait()
-        term = dot_t(new, buffer[i])
-        total = term if total is None else total + term
-    out[...] = jnp.broadcast_to((difference - total)[None], out.shape)
+        total = total - dot_t(new, buffer[i])
+    out[...] = total
 
 
 def pedigree_kernel(bits, parents, new_a, sire, dam, sampling_ref, back_ref, left_ref):
@@ -357,7 +369,11 @@
                 back_ref[g * group + h] += add_parts(total[h * ROWS_EACH : (h + 1) * ROWS_EACH])
 
 
-def deviation_kernel(
+def deviation_kernel(share, traits, columns, *refs):
+    deviation_body(share, traits, refs[:columns], *refs[columns:])
+
+
+def deviation_body(
     share,
     traits,
     differences,
@@ -371,10 +387,11 @@
     semaphores,
 ):
     copies = chunk_copies(genotypes, buffer, semaphores)
-    for copy in copies:
-        copy.start()
     load_matrix(genomic, genomic_ref)
-    deviation = apply_matrix(genomic_ref, sums_of(differences), traits)
+    difference = differences[0][...]
+    for other in differences[1:]:
+        difference = difference + other[...]
+    deviation = apply_matrix(genomic_ref, difference, traits)
     deviation_ref[...] = deviation
     rounded = deviation.astype(BF16)
     start = out.shape[2] - back.shape[2]
@@ -520,10 +537,20 @@
 def spread_kernel(received, out):
     start = received.shape[2] - LANES
     tile = exact_tile([received[i, :, start:] for i in range(received.shape[0])])
-    out[...] = jnp.broadcast_to(tile[None], out.shape)
+    out[...] = tile
 
 
 def final_kernel(
+    share,
+    columns,
+    sums,
+    *refs,
+):
+    tiles = refs[:columns]
+    final_body(share, sums, tiles, *refs[columns:])
+
+
+def final_body(
     share,
     sums,
     tiles,
@@ -542,7 +569,7 @@
     reduction,
 ):
     traits = sol_a.shape[0]
-    tile = exact_tile([tiles[i] for i in range(tiles.shape[0])])
+    tile = exact_tile([ref[...] for ref in tiles])
     step = product_of(sums) / jnp.sum(tile[0:1], axis=1, keepdims=True)
     next_sol_a[...] = sol_a[...] + step * new_a[:traits]
     next_res_a[...] = res_a[...] - step * image_a[:traits]
@@ -580,6 +607,14 @@
 
 def exchange(values, axes):
     return lax.all_to_all(values, axes, split_axis=0, concat_axis=0, tiled=True)
+
+
+def copies_of(values, axis):
+    size = lax.axis_size(axis)
+    return [values] + [
+        lax.ppermute(values, axis, [(i, (i + k) % size) for i in range(size)])
+        for k in range(1, size)
+    ]
 
 
 def local(
@@ -617,8 +652,8 @@
     send = send_list.reshape(rows, capacity)
     sire, dam = sire_slot.reshape(1, animals), dam_slot.reshape(1, animals)
     kinds, places = pattern.reshape(1, animals), genotype_row.reshape(1, animals)
-    table = jnp.pad(jnp.transpose(residual_table, (2, 1, 0)), ((0, 0), (0, PAD - traits), (0, 0)))
-    table = table.reshape(traits * PAD, patterns)
+    def hbm(*arrays):
+        return [pltpu.with_memory_space_constraint(array, pltpu.HBM) for array in arrays]
 
     animal_block = shape_of(PAD, animals)
     slot_block = shape_of(rows, PAD, capacity)
@@ -627,71 +662,78 @@
         functools.partial(totals_kernel, 1.0 / rows),
         (shape_of(rows * columns, PAD, LANES), tile),
         name="totals",
-    )(residual_animal, scaling_animal, residual_marker, scaling_marker)
+    )(*hbm(residual_animal, scaling_animal, residual_marker, scaling_marker))
     sums = exchange(local_sums, ("rows", "mk"))
-    search_out, direction_out, search_placed, direction_placed = call(
-        functools.partial(prepare_kernel, bits, genotyped),
-        (slot_block, slot_block, shape_of(PAD, genotyped), shape_of(PAD, genotyped)),
-        (pltpu.VMEM((PAD, animals), F32), pltpu.VMEM((PAD, animals), F32)),
-        name="prepare",
-    )(token, residual_animal, scaling_animal, direction_animal, send, places)
-    sums, table = lax.optimization_barrier((sums, table))
-    new_animal, outgoing = call(animal_kernel, (animal_block, slot_block), name="animals")(
-        sums,
-        previous,
-        residual_animal,
-        scaling_animal,
-        direction_animal,
+    in_vmem, in_hbm = pl.BlockSpec(memory_space=pltpu.VMEM), pl.BlockSpec(memory_space=pl.ANY)
+
+    placed_block, marker_block = shape_of(PAD, genotyped), shape_of(PAD, markers)
+    (
         search_out,
         direction_out,
+        search_placed,
+        direction_placed,
+        search_animal,
+        padded_direction,
+        search_marker,
+        padded_marker,
+    ) = call(
+        functools.partial(prepare_kernel, bits, genotyped),
+        (slot_block, slot_block, placed_block, placed_block)
+        + (animal_block, animal_block, marker_block, marker_block),
+        name="prepare",
+    )(
+        token,
+        *hbm(residual_animal, scaling_animal, direction_animal, send, places),
+        *hbm(residual_marker, scaling_marker, direction_marker),
+    )
+    new_animal, outgoing = call(animal_kernel, (animal_block, slot_block), name="animals")(
+        sums, previous, search_animal, padded_direction, search_out, direction_out
     )
     parents = exchange(outgoing, "rows")
 
-    def whole(count):
-        return [pl.BlockSpec(memory_space=pltpu.VMEM)] * count
-
-    off_chip = [pl.BlockSpec(memory_space=pl.ANY)]
-    chunk = 2 * share * max(1, 1536 // share)
+    (genotypes,) = hbm(genotypes)
+
+    def chunks(width):
+        return (
+            pltpu.VMEM((markers // width, genotyped, width), BF16),
+            pltpu.SemaphoreType.DMA((markers // width,)),
+        )
+
+    chunk = share * max(1, 1536 // share)
     new_marker, difference = call(
         predict_kernel,
-        (shape_of(PAD, markers), shape_of(columns, PAD, genotyped)),
-        (
-            pltpu.VMEM((markers // chunk, genotyped, chunk), BF16),
-            pltpu.SemaphoreType.DMA((markers // chunk,)),
-        ),
-        in_specs=whole(5) + off_chip + whole(2),
+        (marker_block, placed_block),
+        chunks(2 * chunk),
+        in_specs=[in_vmem] * 4 + [in_hbm] + [in_vmem] * 2,
         name="predict",
     )(
         sums,
         previous,
-        residual_marker,
-        scaling_marker,
-        direction_marker,
+        search_marker,
+        padded_marker,
         genotypes,
         search_placed,
         direction_placed,
     )
-    differences = exchange(difference, "mk")
+    differences = copies_of(difference, "mk")
     sampling, back = call(
         functools.partial(pedigree_kernel, bits),
         (animal_block, slot_block),
         (pltpu.VMEM((rows * ROWS_EACH, capacity), BF16),),
         name="pedigree",
     )(parents, new_animal, sire, dam)
-    chunk = share * max(1, 1536 // share)
     width = packed_width(traits, share)
     deviation, payload = call(
-        functools.partial(deviation_kernel, share, traits),
-        (shape_of(PAD, genotyped), shape_of(rows, PAD, width + capacity)),
-        (
-            pltpu.VMEM((PAD, LANES), F32),
-            pltpu.VMEM((markers // chunk, genotyped, chunk), BF16),
-            pltpu.SemaphoreType.DMA((markers // chunk,)),
-        ),
-        in_specs=whole(2) + off_chip + whole(1),
+        functools.partial(deviation_kernel, share, traits, columns),
+        (placed_block, shape_of(rows, PAD, width + capacity)),
+        (pltpu.VMEM((PAD, LANES), F32), *chunks(chunk)),
+        in_specs=[in_vmem] * (columns + 1) + [in_hbm, in_vmem],
         name="deviation",
-    )(differences, genomic_inverse, genotypes, back)
+    )(*differences, genomic_inverse, genotypes, back)
     received = exchange(payload, "rows")
+    residual_table, deviation = lax.optimization_barrier((residual_table, deviation))
+    table = jnp.pad(jnp.transpose(residual_table, (2, 1, 0)), ((0, 0), (0, PAD - traits), (0, 0)))
+    table = table.reshape(traits * PAD, patterns)
     base_image = call(record_kernel, animal_block, (pltpu.VMEM((PAD, LANES), F32),), name="record")(
         deviation, sampling, new_animal, kinds, table, genetic_inverse
     )
@@ -741,14 +783,13 @@
                 pltpu.VMEM((PAD, full), F32),
             ],
         ),
+        compiler_params=LIMIT,
         name="image",
     )(row, *inputs, new_share, res_share)
     gathered = exchange(payload, "rows")
-    tiles = exchange(
-        call(spread_kernel, shape_of(columns, PAD, LANES), name="spread")(gathered), "mk"
-    )
+    tiles = copies_of(call(spread_kernel, tile, name="spread")(gathered), "mk")
     *outputs, reduction = call(
-        functools.partial(final_kernel, share),
+        functools.partial(final_kernel, share, columns),
         (
             shape_of(traits, animals),
             shape_of(traits, markers),
@@ -759,7 +800,7 @@
         name="final",
     )(
         sums,
-        tiles,
+        *tiles,
         solution_animal,
         residual_animal,
         new_animal,

time: 95.7 us -> 77.5 us (0.81)
  Pallas kernels: 35.1 us -> 22.5 us
  blocking collectives: 22.6 us -> 14.6 us
  waiting for transfers between devices: 12.4 us -> 18.6 us
  local copies, waits for them, and re-layouts: 3.35 us -> 0.09 us
    all_to_all x2 -> x1, blocking collectives: 22.6 us -> 14.6 us  [exchange(): return lax.all_to_all(values, axes, split_axis=0, concat_axis=0, tiled=True)]
    pallas_call x4, Pallas kernels: 17.7 us -> 11.5 us  [the longest x1 5.5 us: local(): call(predict_kernel, (marker_block, placed_block), chunks(2 * chunk), in_...]
    all_to_all x4 -> x3, starting transfers between devices: 19.9 us -> 16.3 us  [exchange(): return lax.all_to_all(values, axes, split_axis=0, concat_axis=0, tiled=True)]
    ppermute x0 -> x6, starting transfers between devices: none -> 3.53 us  [copies_of(): lax.ppermute(values, axis, [(i, (i + k) % size) for i in range(size)])]
    all_to_all x4 -> x3, waiting for transfers between devices: 12.4 us -> 15.6 us  [exchange(): return lax.all_to_all(values, axes, split_axis=0, concat_axis=0, tiled=True)]
    ppermute x0 -> x6, waiting for transfers between devices: none -> 2.93 us  [copies_of(): lax.ppermute(values, axis, [(i, (i + k) % size) for i in range(size)])]
    unnamed x9 -> x27, local copies, waits for them, and re-layouts: 2.75 us -> 0.08 us
    pallas_call x1, Pallas kernels: 3.46 us -> 1.54 us  [local(): pl.pallas_call(functools.partial(image_kernel, bits, share), out_shape=(a...]
  transfers between devices with their start and end apart: 4 -> 9, of which waited for: 2 -> 4; matrix products, arithmetic and copies ran while one was open for 1% -> 0% of each run, Pallas kernels for 19% -> 16%
where the time goes in v3:
time: 77.5 us; the launch traced here: 77.1 us
  Pallas kernels  22.5 us (29%)
  starting transfers between devices  19.9 us (26%)
  waiting for transfers between devices  18.6 us (24%)
  blocking collectives  14.6 us (19%)
  between operations  1.54 us (2%)
    all_to_all x3, starting transfers between devices, exchange(): return lax.all_to_all(values, axes, split_axis=0, concat_axis=0, tiled=True)  16.3 us
    all_to_all x3, waiting for transfers between devices, exchange(): return lax.all_to_all(values, axes, split_axis=0, concat_axis=0, tiled=True)  15.6 us
    all_to_all x1, blocking collectives, exchange(): return lax.all_to_all(values, axes, split_axis=0, concat_axis=0, tiled=True)  14.6 us
    pallas_call x1, Pallas kernels, local(): call(predict_kernel, (marker_block, placed_block), chunks(2 * chunk), in_...  5.5 us
    pallas_call x1, Pallas kernels, local(): call(functools.partial(deviation_kernel, share, traits, columns), (placed...  4.81 us
    ppermute x6, starting transfers between devices, copies_of(): lax.ppermute(values, axis, [(i, (i + k) % size) for i in range(size)])  3.53 us
    pallas_call x1, Pallas kernels, local(): call(functools.partial(prepare_kernel, bits, genotyped), (slot_block, slo...  3.15 us
    pallas_call x1, Pallas kernels, local(): call(functools.partial(pedigree_kernel, bits), (animal_block, slot_block)...  3.03 us
  transfers between devices with their start and end apart: 9, of which 4 were waited for; matrix products, arithmetic and copies ran while one was open for 0% of the time, Pallas kernels for 16%

profile of v3, /device:TPU:0, one launch (start us, length us, event | category | flops | bytes accessed | tf_op | source)
XLA Modules:
  0.0 77.1 jit_solution(14566076865219569324)
XLA Ops:
  0.6 0.0 copy-start.9
  0.6 0.0 copy-start.8
  0.7 0.0 copy-start.10
  0.7 2.0 %totals.1 = (f32[32,8,128]{2,1,0:T(8,128)}, f32[8,128]{1,0:T(8,128)S(1)}) custom-call(f32[6,4096]{1,0:T(8,128)} %refs_5_.3, f32[6,4096]{1,0:T(8,128)} %scal.1, f32[6,12288]{1,0:T(8,128)} %refs_9_.1, f32[6,12288]{1,0:T(8,128)} %scal_m.3), custom_call_target="tpu_custom_call" | custom-call | tf_op jit(solution)/shard_map/totals/pallas_call | solution.py:661
  2.7 7.3 %all-to-all-start = ((f32[32,8,128]{2,1,0:T(8,128)}), f32[32,8,128]{2,1,0:T(8,128)S(1)}, u32[]{:S(2)}, u32[]{:S(2)}) async-start(f32[32,8,128]{2,1,0:T(8,128)} %get-tuple-element.32), calls=%async_computation | async-start | bytes 262144 | tf_op jit(solution)/shard_map/all_to_all | solution.py:609
  10.7 3.1 %prepare.1 = (f32[8,8,256]{2,1,0:T(8,128)S(1)}, f32[8,8,256]{2,1,0:T(8,128)S(1)}, f32[8,384]{1,0:T(8,128)S(1)}, f32[8,384]{1,0:T(8,128)S(1)}, f32[8,4096]{1,0:T(...) custom-call(f32[8,128]{1,0:T(8,128)S(1)} %get-tuple-element.33.token, ...), custom_call_target="tpu_custom_call" | custom-call | tf_op jit(solution)/shard_map/prepare/pallas_call | solution.py:679
  13.8 4.4 %all-to-all-done.sums = f32[32,8,128]{2,1,0:T(8,128)S(1)} async-done(((f32[32,8,128]{2,1,0:T(8,128)}), f32[32,8,128]{2,1,0:T(8,128)S(1)}, u32[]{:S(2)}, u32[]{:S(2)}) %all-to-all-start) | async-done | bytes 131104 | tf_op jit(solution)/shard_map/all_to_all | solution.py:609
  18.2 0.8 %animals.1 = (f32[8,4096]{1,0:T(8,128)S(1)}, f32[8,8,256]{2,1,0:T(8,128)}) custom-call(f32[32,8,128]{2,1,0:T(8,128)S(1)} %all-to-all-done.sums, f32[1,1]{1,0:T(1,128)} %bitcast.12.previous, f32[8,4096]{1,0:T(8,128)S(1)} %get-tuple-element.39.search, f32[8,4096]{1,0:T(8,128)S(1)} %get-tuple-element.40.direction, ...), custom_call_target="tpu_custom_call" | custom-call | tf_op jit(solution)/shard_map/animals/pallas_call | solution.py:689
  19.0 3.4 %all-to-all-start.1 = ((f32[8,8,256]{2,1,0:T(8,128)}), f32[8,8,256]{2,1,0:T(8,128)S(1)}, u32[]{:S(2)}, u32[]{:S(2)}) async-start(f32[8,8,256]{2,1,0:T(8,128)} %get-tuple-element.43), calls=%async_computation.1 | async-start | bytes 131072 | tf_op jit(solution)/shard_map/all_to_all | solution.py:609
  22.4 0.0 copy-start.12
  22.4 0.0 copy-start.6
  22.4 0.0 copy-start.7
  22.4 0.0 copy-start
  22.4 0.0 copy-start.1
  22.5 0.0 copy-start.4
  22.5 0.0 copy-start.5
  22.5 0.0 copy-start.11
  22.5 0.0 copy-start.2
  22.5 0.0 copy-start.3
  22.5 5.5 %predict.1 = (f32[8,12288]{1,0:T(8,128)S(1)}, f32[8,384]{1,0:T(8,128)S(1)}) custom-call(f32[32,8,128]{2,1,0:T(8,128)S(1)} %all-to-all-done.sums, f32[1,1]{1,0:T(1,128)} %bitcast.11.previous, f32[8,12288]{1,0:T(8,128)S(1)} %get-tuple-element.34.search, f32[8,12288]{1,0:T(8,128)S(1)} %get-tuple-element.35.direction, bf16[384,12288]{1,0:T(8,128)(2,1)} %refs_5_.2, ...), custom_call_target="tpu_custom_call" | custom-call | tf_op jit(solution)/shard_map/predict/pallas_call | solution.py:703
  28.0 0.2 collective-permute-start.2
  28.2 1.7 %collective-permute-start.1 = (f32[8,384]{1,0:T(8,128)S(1)}, f32[8,384]{1,0:T(8,128)S(1)}, u32[]{:S(2)}, u32[]{:S(2)}) collective-permute-start(f32[8,384]{1,0:T(8,128)S(1)} %get-tuple-element.38.refs_0_), channel_id=1, source_target_pairs={{0,2},{1,3},{2,0},{3,1},{4,6},{5,7},{6,4},{7,5},{8,10},{9,11},{10,... | collective-permute-start | bytes 36872 | tf_op jit(solution)/shard_map/ppermute | solution.py:615
  29.9 0.0 collective-permute-start
  29.9 0.0 all-to-all-done.1.parents
  29.9 0.0 copy-done.9
  29.9 0.0 copy-done.8
  29.9 3.0 %pedigree.1 = (f32[8,4096]{1,0:T(8,128)S(1)}, f32[8,8,256]{2,1,0:T(8,128)S(1)}) custom-call(f32[8,8,256]{2,1,0:T(8,128)S(1)} %all-to-all-done.1.parents, f32[8,4096]{1,0:T(8,128)S(1)} %get-tuple-element.44.new_a.refs_6_, s32[1,4096]{1,0:T(1,128)S(1)} %bitcast.18, s32[1,4096]{1,0:T(1,128)S(1)} %bitcast.19), custom_call_target="tpu_custom_call" | custom-call | tf_op jit(solution)/shard_map/pedigree/pallas_call | solution.py:719
  33.0 0.0 collective-permute-done.2.refs_3_
  33.0 0.0 collective-permute-done.1.refs_2_
  33.0 0.0 collective-permute-done.refs_1_
  33.0 0.0 copy-done.10
  33.0 4.8 %deviation.1 = (f32[8,384]{1,0:T(8,128)S(1)}, f32[8,8,1408]{2,1,0:T(8,128)}) custom-call(f32[8,384]{1,0:T(8,128)S(1)} %get-tuple-element.38.refs_0_, f32[8,384]{1,0:T(8,128)S(1)} %collective-permute-done.refs_1_, f32[8,384]{1,0:T(8,128)S(1)} %collective-permute-done.1.refs_2_, f32[8,384]{1,0:T(8,128)S(1)} %collective-permute-done.2.refs_3_, ...), custom_call_target="tpu_custom_call" | custom-call | tf_op jit(solution)/shard_map/deviation/pallas_call | solution.py:726
  37.9 5.7 %all-to-all-start.2 = ((f32[8,8,1408]{2,1,0:T(8,128)}), f32[8,8,1408]{2,1,0:T(8,128)S(1)}, u32[]{:S(2)}, u32[]{:S(2)}) async-start(f32[8,8,1408]{2,1,0:T(8,128)} %get-tuple-element.46), calls=%async_computation.2 | async-start | bytes 720896 | tf_op jit(solution)/shard_map/all_to_all | solution.py:609
  43.5 0.0 copy-done.12
  43.6 0.0 copy-done.6
  43.6 0.0 copy-done.7
  43.6 0.5 record.1.base_image
  44.0 11.2 %all-to-all-done.2.received = f32[8,8,1408]{2,1,0:T(8,128)S(1)} async-done(((f32[8,8,1408]{2,1,0:T(8,128)}), f32[8,8,1408]{2,1,0:T(8,128)S(1)}, u32[]{:S(2)}, u32[]{:S(2)}) %all-to-all-start.2) | async-done | bytes 360480 | tf_op jit(solution)/shard_map/all_to_all | solution.py:609
  55.3 0.0 copy-done.4
  55.3 1.5 %image.1 = (f32[8,4096]{1,0:T(8,128)S(1)}, f32[8,8,1280]{2,1,0:T(8,128)S(1)}) custom-call(s32[1]{0:T(128)} %bitcast.row, f32[8,8,1408]{2,1,0:T(8,128)S(1)} %all-to-all-done.2.received, s32[8,256]{1,0:T(8,128)S(1)} %bitcast.16, f32[8,4096]{1,0:T(8,128)S(1)} %record.1.base_image, f32[8,384]{1,0:T(8,128)S(1)} %get-tuple-element.48.token.deviation, ...), custom_call_target="tpu_custom_call" | custom-call | tf_op jit(solution)/shard_map/image/pallas_call | solution.py:770
  56.9 14.6 %all_to_all.20.received.refs_11_ = f32[8,8,1280]{2,1,0:T(8,128)S(1)} all-to-all(f32[8,8,1280]{2,1,0:T(8,128)S(1)} %get-tuple-element.52), channel_id=1, replica_groups=mesh['rows'=8,'mk'=4] {'rows'}, dimensions={0} | all-to-all | bytes 655360 | tf_op jit(solution)/shard_map/all_to_all | solution.py:609
  71.4 0.1 collective-permute-start.5
  71.5 1.4 %collective-permute-start.4 = (f32[8,128]{1,0:T(8,128)S(1)}, f32[8,128]{1,0:T(8,128)S(1)}, u32[]{:S(2)}, u32[]{:S(2)}) collective-permute-start(f32[8,128]{1,0:T(8,128)S(1)} %spread.1.refs_0_), channel_id=1, source_target_pairs={{0,2},{1,3},{2,0},{3,1},{4,6},{5,7},{6,4},{7,5},{8,10},{9,11},{10,... | collective-permute-start | bytes 12296 | tf_op jit(solution)/shard_map/ppermute | solution.py:615
  72.9 0.2 collective-permute-start.3
  73.1 0.0 collective-permute-done.5.refs_3_
  73.1 2.1 %collective-permute-done.4.refs_2_ = f32[8,128]{1,0:T(8,128)S(1)} collective-permute-done((f32[8,128]{1,0:T(8,128)S(1)}, f32[8,128]{1,0:T(8,128)S(1)}, u32[]{:S(2)}, u32[]{:S(2)}) %collective-permute-start.4) | collective-permute-done | bytes 4128 | tf_op jit(solution)/shard_map/ppermute | solution.py:615
  75.2 0.8 %collective-permute-done.3.refs_1_ = f32[8,128]{1,0:T(8,128)S(1)} collective-permute-done((f32[8,128]{1,0:T(8,128)S(1)}, f32[8,128]{1,0:T(8,128)S(1)}, u32[]{:S(2)}, u32[]{:S(2)}) %collective-permute-start.3) | collective-permute-done | bytes 4128 | tf_op jit(solution)/shard_map/ppermute | solution.py:615
  76.0 1.1 %final.1 = (f32[6,4096]{1,0:T(8,128)}, f32[6,12288]{1,0:T(8,128)}, f32[6,4096]{1,0:T(8,128)}, f32[6,12288]{1,0:T(8,128)}, f32[1,1]{1,0:T(1,128)}) custom-call(f32[32,8,128]{2,1,0:T(8,128)S(1)} %all-to-all-done.sums, f32[8,128]{1,0:T(8,128)S(1)} %spread.1.refs_0_, f32[8,128]{1,0:T(8,128)S(1)} %collective-permute-done.3.refs_1_, ...), custom_call_target="tpu_custom_call" | custom-call | tf_op jit(solution)/shard_map/final/pallas_call | solution.py:791
  (9 shorter events, 0.0 us)
Async XLA Ops:
  0.6 29.3 %copy-start.9 = (s32[4096]{0:T(1024)S(1)}, s32[4096]{0:T(1024)}, u32[]{:S(2)}) copy-start(s32[4096]{0:T(1024)} %param.35) | copy-start | bytes 49156
  0.6 29.3 %copy-start.8 = (s32[4096]{0:T(1024)S(1)}, s32[4096]{0:T(1024)}, u32[]{:S(2)}) copy-start(s32[4096]{0:T(1024)} %param.34) | copy-start | bytes 49156
  0.7 32.4 %copy-start.10 = (f32[6,6]{1,0:T(8,128)S(1)}, f32[6,6]{1,0:T(8,128)}, u32[]{:S(2)}) copy-start(f32[6,6]{1,0:T(8,128)} %refs_4_.2) | copy-start | bytes 436
  2.7 15.5 %all-to-all-start = ((f32[32,8,128]{2,1,0:T(8,128)}), f32[32,8,128]{2,1,0:T(8,128)S(1)}, u32[]{:S(2)}, u32[]{:S(2)}) async-start(f32[32,8,128]{2,1,0:T(8,128)} %get-tuple-element.32), calls=%async_computation | async-start | bytes 262144 | tf_op jit(solution)/shard_map/all_to_all | solution.py:609
  19.0 10.9 %all-to-all-start.1 = ((f32[8,8,256]{2,1,0:T(8,128)}), f32[8,8,256]{2,1,0:T(8,128)S(1)}, u32[]{:S(2)}, u32[]{:S(2)}) async-start(f32[8,8,256]{2,1,0:T(8,128)} %get-tuple-element.43), calls=%async_computation.1 | async-start | bytes 131072 | tf_op jit(solution)/shard_map/all_to_all | solution.py:609
  22.4 21.1 %copy-start.12 = (f32[64,6,6]{0,2,1:T(8,128)S(1)}, f32[64,6,6]{0,2,1:T(8,128)}, u32[]{:S(2)}) copy-start(f32[64,6,6]{0,2,1:T(8,128)} %param.32) | copy-start | bytes 27652
  22.4 21.2 %copy-start.6 = (f32[6,6]{1,0:T(8,128)S(1)}, f32[6,6]{1,0:T(8,128)}, u32[]{:S(2)}) copy-start(f32[6,6]{1,0:T(8,128)} %genetic.3) | copy-start | bytes 436
  22.4 21.2 %copy-start.7 = (s32[4096]{0:T(1024)S(1)}, s32[4096]{0:T(1024)}, u32[]{:S(2)}) copy-start(s32[4096]{0:T(1024)} %param.33) | copy-start | bytes 49156
  22.4 32.9 %copy-start = (f32[6,12288]{1,0:T(8,128)S(1)}, f32[6,12288]{1,0:T(8,128)}, u32[]{:S(2)}) copy-start(f32[6,12288]{1,0:T(8,128)} %refs_9_.1) | copy-start | bytes 884740
  22.4 32.8 %copy-start.1 = (f32[6,4096]{1,0:T(8,128)S(1)}, f32[6,4096]{1,0:T(8,128)}, u32[]{:S(2)}) copy-start(f32[6,4096]{1,0:T(8,128)} %refs_5_.3) | copy-start | bytes 294916
  22.5 32.8 %copy-start.4 = (s32[4096]{0:T(1024)S(1)}, s32[4096]{0:T(1024)}, u32[]{:S(2)}) copy-start(s32[4096]{0:T(1024)} %param.36) | copy-start | bytes 49156
  22.5 32.8 %copy-start.5 = (s32[1,1,8,256]{3,2,1,0:T(8,128)S(1)}, s32[1,1,8,256]{3,2,1,0:T(8,128)}, u32[]{:S(2)}) copy-start(s32[1,1,8,256]{3,2,1,0:T(8,128)} %param.37) | copy-start | bytes 24580
  22.5 32.8 %copy-start.11 = (f32[6,6]{1,0:T(8,128)S(1)}, f32[6,6]{1,0:T(8,128)}, u32[]{:S(2)}) copy-start(f32[6,6]{1,0:T(8,128)} %marker_inverse.1) | copy-start | bytes 436
  22.5 53.5 %copy-start.2 = (f32[6,12288]{1,0:T(8,128)S(1)}, f32[6,12288]{1,0:T(8,128)}, u32[]{:S(2)}) copy-start(f32[6,12288]{1,0:T(8,128)} %refs_8_.1) | copy-start | bytes 884740
  22.5 53.5 %copy-start.3 = (f32[6,4096]{1,0:T(8,128)S(1)}, f32[6,4096]{1,0:T(8,128)}, u32[]{:S(2)}) copy-start(f32[6,4096]{1,0:T(8,128)} %refs_4_.3) | copy-start | bytes 294916
  28.0 5.0 %collective-permute-start.2 = (f32[8,384]{1,0:T(8,128)S(1)}, f32[8,384]{1,0:T(8,128)S(1)}, u32[]{:S(2)}, u32[]{:S(2)}) collective-permute-start(f32[8,384]{1,0:T(8,128)S(1)} %get-tuple-element.38.refs_0_), channel_id=1, source_target_pairs={{0,3},{1,0},{2,1},{3,2},{4,7},{5,4},{6,5},{7,6},{8,11},{9,8},{10,9... | collective-permute-start | bytes 36872 | tf_op jit(solution)/shard_map/ppermute | solution.py:615
  28.2 4.8 %collective-permute-start.1 = (f32[8,384]{1,0:T(8,128)S(1)}, f32[8,384]{1,0:T(8,128)S(1)}, u32[]{:S(2)}, u32[]{:S(2)}) collective-permute-start(f32[8,384]{1,0:T(8,128)S(1)} %get-tuple-element.38.refs_0_), channel_id=1, source_target_pairs={{0,2},{1,3},{2,0},{3,1},{4,6},{5,7},{6,4},{7,5},{8,10},{9,11},{10,... | collective-permute-start | bytes 36872 | tf_op jit(solution)/shard_map/ppermute | solution.py:615
  29.9 3.1 %collective-permute-start = (f32[8,384]{1,0:T(8,128)S(1)}, f32[8,384]{1,0:T(8,128)S(1)}, u32[]{:S(2)}, u32[]{:S(2)}) collective-permute-start(f32[8,384]{1,0:T(8,128)S(1)} %get-tuple-element.38.refs_0_), channel_id=1, source_target_pairs={{0,1},{1,2},{2,3},{3,0},{4,5},{5,6},{6,7},{7,4},{8,9},{9,10},{10,1... | collective-permute-start | bytes 36872 | tf_op jit(solution)/shard_map/ppermute | solution.py:615
  37.9 17.4 %all-to-all-start.2 = ((f32[8,8,1408]{2,1,0:T(8,128)}), f32[8,8,1408]{2,1,0:T(8,128)S(1)}, u32[]{:S(2)}, u32[]{:S(2)}) async-start(f32[8,8,1408]{2,1,0:T(8,128)} %get-tuple-element.46), calls=%async_computation.2 | async-start | bytes 720896 | tf_op jit(solution)/shard_map/all_to_all | solution.py:609
  71.4 1.6 %collective-permute-start.5 = (f32[8,128]{1,0:T(8,128)S(1)}, f32[8,128]{1,0:T(8,128)S(1)}, u32[]{:S(2)}, u32[]{:S(2)}) collective-permute-start(f32[8,128]{1,0:T(8,128)S(1)} %spread.1.refs_0_), channel_id=1, source_target_pairs={{0,3},{1,0},{2,1},{3,2},{4,7},{5,4},{6,5},{7,6},{8,11},{9,8},{10,9... | collective-permute-start | bytes 12296 | tf_op jit(solution)/shard_map/ppermute | solution.py:615
  71.5 3.7 %collective-permute-start.4 = (f32[8,128]{1,0:T(8,128)S(1)}, f32[8,128]{1,0:T(8,128)S(1)}, u32[]{:S(2)}, u32[]{:S(2)}) collective-permute-start(f32[8,128]{1,0:T(8,128)S(1)} %spread.1.refs_0_), channel_id=1, source_target_pairs={{0,2},{1,3},{2,0},{3,1},{4,6},{5,7},{6,4},{7,5},{8,10},{9,11},{10,... | collective-permute-start | bytes 12296 | tf_op jit(solution)/shard_map/ppermute | solution.py:615
  72.9 3.0 %collective-permute-start.3 = (f32[8,128]{1,0:T(8,128)S(1)}, f32[8,128]{1,0:T(8,128)S(1)}, u32[]{:S(2)}, u32[]{:S(2)}) collective-permute-start(f32[8,128]{1,0:T(8,128)S(1)} %spread.1.refs_0_), channel_id=1, source_target_pairs={{0,1},{1,2},{2,3},{3,0},{4,5},{5,6},{6,7},{7,4},{8,9},{9,10},{10,1... | collective-permute-start | bytes 12296 | tf_op jit(solution)/shard_map/ppermute | solution.py:615

commit v4 on v3

--- a/solution.py
+++ b/solution.py
@@ -45,8 +45,10 @@
 
 
 def one_hot(low, base):
-    wanted = lax.broadcasted_iota(jnp.int32, (base, low.shape[1]), 0)
-    return jnp.where(wanted == low, 1.0, 0.0).astype(BF16)
+    wanted = lax.broadcasted_iota(jnp.int32, (base, LANES), 0).astype(F32).astype(BF16)
+    wanted = jnp.concatenate([wanted] * (low.shape[1] // LANES), axis=1)
+    found = wanted == low.astype(F32).astype(BF16)
+    return jnp.where(found, jnp.ones((), BF16), jnp.zeros((), BF16))
 
 
 def dot(left, right):
@@ -66,10 +68,27 @@
     return total
 
 
-def masked_blocks(stacked, high, first, count):
-    return jnp.concatenate(
-        [jnp.where(high == first + h, stacked, 0.0) for h in range(count)], axis=0
-    ).astype(BF16)
+def doubled_parts(values):
+    stacked = parts_of(values)
+    parts = [stacked[p * PAD : (p + 1) * PAD] for p in range(3)]
+    return [jnp.concatenate([part, part], axis=0).astype(BF16) for part in parts]
+
+
+def masked_blocks(parts, high, first, count):
+    half = lax.broadcasted_iota(jnp.int32, (2 * PAD, LANES), 0) // PAD
+    half = half.astype(F32).astype(BF16)
+    half = jnp.concatenate([half] * (high.shape[1] // LANES), axis=1)
+    tiles = []
+    for pair in range(0, count, 2):
+        found = half == (high - (first + pair)).astype(F32).astype(BF16)
+        tiles += [jnp.where(found, part, jnp.zeros((), BF16)) for part in parts]
+    return jnp.concatenate(tiles, axis=0)
+
+
+def block_of(total, h, kinds=1, kind=0):
+    start = (h // 2 * kinds + kind) * 3 * 2 * PAD + h % 2 * PAD
+    rows = [total[start + p * 2 * PAD : start + p * 2 * PAD + PAD] for p in range(3)]
+    return rows[0] + rows[1] + rows[2]
 
 
 def fold(values):
@@ -263,24 +282,20 @@
     else:
         pl.loop(0, send.shape[0])(one)
 
-    blocks = -(-genotyped // base)
+    blocks = -(-genotyped // (2 * base)) * 2
     width = 1024
     total = jnp.zeros((blocks * 2 * ROWS_EACH, base), F32)
     for start in range(0, animals, width):
         window = slice(start, start + width)
         index = row_index[:, window]
-        stacked = jnp.concatenate(
-            [parts_of(search_ref[:, window]), parts_of(direction_ref[:, window])], axis=0
+        parts = doubled_parts(search_ref[:, window]) + doubled_parts(direction_ref[:, window])
+        total = total + dot_t(
+            masked_blocks(parts, index >> bits, 0, blocks), one_hot(index & (base - 1), base)
         )
-        total = total + dot_t(
-            masked_blocks(stacked, index >> bits, 0, blocks), one_hot(index & (base - 1), base)
-        )
-    for h in range(blocks):
+    for h in range(-(-genotyped // base)):
         size = min(base, genotyped - h * base)
         for k, out in enumerate((search_placed, direction_placed)):
-            start = (2 * h + k) * ROWS_EACH
-            block = add_parts(total[start : start + ROWS_EACH])
-            out[:, h * base : h * base + size] = block[:, :size]
+            out[:, h * base : h * base + size] = block_of(total, h, 2, k)[:, :size]
     search_m[...] = jnp.zeros_like(search_m)
     direction_m8[...] = jnp.zeros_like(direction_m8)
     search_m[:traits] = scal_m[...] * res_m[...]
@@ -360,13 +375,13 @@
         mendel = 1.0 / (1.0 - 0.25 * known)
         sampling = mendel * (new_a[:, window] - 0.5 * gathered)
         sampling_ref[:, window] = sampling
-        stacked = parts_of(-0.5 * sampling)
+        parts = doubled_parts(-0.5 * sampling)
         for g in range(groups):
-            total = dot_t(masked_blocks(stacked, sire_high, g * group, group), sire_hot) + dot_t(
-                masked_blocks(stacked, dam_high, g * group, group), dam_hot
+            total = dot_t(masked_blocks(parts, sire_high, g * group, group), sire_hot) + dot_t(
+                masked_blocks(parts, dam_high, g * group, group), dam_hot
             )
             for h in range(group):
-                back_ref[g * group + h] += add_parts(total[h * ROWS_EACH : (h + 1) * ROWS_EACH])
+                back_ref[g * group + h] += block_of(total, h)
 
 
 def deviation_kernel(share, traits, columns, *refs):
@@ -464,9 +479,9 @@
 
     def scatter(r, total):
         index = send[pl.ds(r, 1), :]
-        stacked = parts_of(received[r, :, width:])
+        parts = doubled_parts(received[r, :, width:])
         return total + dot_t(
-            masked_blocks(stacked, index >> bits, 0, blocks), one_hot(index & (base - 1), base)
+            masked_blocks(parts, index >> bits, 0, blocks), one_hot(index & (base - 1), base)
         )
 
     total = jnp.zeros((blocks * ROWS_EACH, base), F32)
@@ -484,7 +499,7 @@
     for h in range(blocks):
         window = slice(h * base, (h + 1) * base)
         index = row_index[:, window]
-        gathered = add_parts(total[h * ROWS_EACH : (h + 1) * ROWS_EACH])
+        gathered = block_of(total, h)
         genomic_term = select_blocks(
             dot(table, one_hot(index & (base - 1), base)), index >> bits, 0, places
         )
@@ -612,7 +627,7 @@
 def copies_of(values, axis):
     size = lax.axis_size(axis)
     return [values] + [
-        lax.ppermute(values, axis, [(i, (i + k) % size) for i in range(size)])
+        lax.ppermute(values, axis, [(i, i ^ k) for i in range(size)])
         for k in range(1, size)
     ]
 

time: 77.5 us -> 76.7 us (0.990)
  waiting for transfers between devices: 18.6 us -> 17.1 us
    ppermute x6, waiting for transfers between devices: 2.93 us -> 1.84 us  [copies_of(): lax.ppermute(values, axis, [(i, i ^ k) for i in range(size)])]
where the time goes in v4:
time: 76.7 us; the launch traced here: 76.3 us
  Pallas kernels  22.6 us (29%)
  starting transfers between devices  20.5 us (27%)
  waiting for transfers between devices  17.1 us (22%)
  blocking collectives  14.5 us (19%)
  between operations  1.55 us (2%)
    all_to_all x3, starting transfers between devices, exchange(): return lax.all_to_all(values, axes, split_axis=0, concat_axis=0, tiled=True)  16.6 us
    all_to_all x3, waiting for transfers between devices, exchange(): return lax.all_to_all(values, axes, split_axis=0, concat_axis=0, tiled=True)  15.3 us
    all_to_all x1, blocking collectives, exchange(): return lax.all_to_all(values, axes, split_axis=0, concat_axis=0, tiled=True)  14.5 us
    pallas_call x1, Pallas kernels, local(): call(predict_kernel, (marker_block, placed_block), chunks(2 * chunk), in_...  5.5 us
    pallas_call x1, Pallas kernels, local(): call(functools.partial(deviation_kernel, share, traits, columns), (placed...  4.81 us
    ppermute x6, starting transfers between devices, copies_of(): lax.ppermute(values, axis, [(i, i ^ k) for i in range(size)])  3.85 us
    pallas_call x1, Pallas kernels, local(): call(functools.partial(prepare_kernel, bits, genotyped), (slot_block, slo...  3.12 us
    pallas_call x1, Pallas kernels, local(): call(functools.partial(pedigree_kernel, bits), (animal_block, slot_block)...  3.06 us
  transfers between devices with their start and end apart: 9, of which 4 were waited for; matrix products, arithmetic and copies ran while one was open for 0% of the time, Pallas kernels for 16%

profile of v4, /device:TPU:0, one launch (start us, length us, event | category | flops | bytes accessed | tf_op | source)
XLA Modules:
  0.0 76.3 jit_solution(14498713295761952267)
XLA Ops:
  0.6 0.0 copy-start.9
  0.6 0.0 copy-start.8
  0.7 0.0 copy-start.10
  0.7 2.0 %totals.1 = (f32[32,8,128]{2,1,0:T(8,128)}, f32[8,128]{1,0:T(8,128)S(1)}) custom-call(f32[6,4096]{1,0:T(8,128)} %refs_5_.3, f32[6,4096]{1,0:T(8,128)} %scal.1, f32[6,12288]{1,0:T(8,128)} %refs_9_.1, f32[6,12288]{1,0:T(8,128)} %scal_m.3), custom_call_target="tpu_custom_call" | custom-call | tf_op jit(solution)/shard_map/totals/pallas_call | solution.py:676
  2.7 7.3 %all-to-all-start = ((f32[32,8,128]{2,1,0:T(8,128)}), f32[32,8,128]{2,1,0:T(8,128)S(1)}, u32[]{:S(2)}, u32[]{:S(2)}) async-start(f32[32,8,128]{2,1,0:T(8,128)} %get-tuple-element.32), calls=%async_computation | async-start | bytes 262144 | tf_op jit(solution)/shard_map/all_to_all | solution.py:624
  10.7 3.1 %prepare.1 = (f32[8,8,256]{2,1,0:T(8,128)S(1)}, f32[8,8,256]{2,1,0:T(8,128)S(1)}, f32[8,384]{1,0:T(8,128)S(1)}, f32[8,384]{1,0:T(8,128)S(1)}, f32[8,4096]{1,0:T(...) custom-call(f32[8,128]{1,0:T(8,128)S(1)} %get-tuple-element.33.token, ...), custom_call_target="tpu_custom_call" | custom-call | tf_op jit(solution)/shard_map/prepare/pallas_call | solution.py:694
  13.8 4.4 %all-to-all-done.sums = f32[32,8,128]{2,1,0:T(8,128)S(1)} async-done(((f32[32,8,128]{2,1,0:T(8,128)}), f32[32,8,128]{2,1,0:T(8,128)S(1)}, u32[]{:S(2)}, u32[]{:S(2)}) %all-to-all-start) | async-done | bytes 131104 | tf_op jit(solution)/shard_map/all_to_all | solution.py:624
  18.2 0.8 %animals.1 = (f32[8,4096]{1,0:T(8,128)S(1)}, f32[8,8,256]{2,1,0:T(8,128)}) custom-call(f32[32,8,128]{2,1,0:T(8,128)S(1)} %all-to-all-done.sums, f32[1,1]{1,0:T(1,128)} %bitcast.12.previous, f32[8,4096]{1,0:T(8,128)S(1)} %get-tuple-element.39.search, f32[8,4096]{1,0:T(8,128)S(1)} %get-tuple-element.40.direction, ...), custom_call_target="tpu_custom_call" | custom-call | tf_op jit(solution)/shard_map/animals/pallas_call | solution.py:704
  19.0 3.4 %all-to-all-start.1 = ((f32[8,8,256]{2,1,0:T(8,128)}), f32[8,8,256]{2,1,0:T(8,128)S(1)}, u32[]{:S(2)}, u32[]{:S(2)}) async-start(f32[8,8,256]{2,1,0:T(8,128)} %get-tuple-element.43), calls=%async_computation.1 | async-start | bytes 131072 | tf_op jit(solution)/shard_map/all_to_all | solution.py:624
  22.4 0.0 copy-start.12
  22.4 0.0 copy-start.6
  22.4 0.0 copy-start.7
  22.4 0.0 copy-start
  22.4 0.0 copy-start.1
  22.5 0.0 copy-start.4
  22.5 0.0 copy-start.5
  22.5 0.0 copy-start.11
  22.5 0.0 copy-start.2
  22.5 0.0 copy-start.3
  22.5 5.5 %predict.1 = (f32[8,12288]{1,0:T(8,128)S(1)}, f32[8,384]{1,0:T(8,128)S(1)}) custom-call(f32[32,8,128]{2,1,0:T(8,128)S(1)} %all-to-all-done.sums, f32[1,1]{1,0:T(1,128)} %bitcast.11.previous, f32[8,12288]{1,0:T(8,128)S(1)} %get-tuple-element.34.search, f32[8,12288]{1,0:T(8,128)S(1)} %get-tuple-element.35.direction, bf16[384,12288]{1,0:T(8,128)(2,1)} %refs_5_.2, ...), custom_call_target="tpu_custom_call" | custom-call | tf_op jit(solution)/shard_map/predict/pallas_call | solution.py:718
  28.0 0.2 collective-permute-start.2
  28.3 1.7 %collective-permute-start.1 = (f32[8,384]{1,0:T(8,128)S(1)}, f32[8,384]{1,0:T(8,128)S(1)}, u32[]{:S(2)}, u32[]{:S(2)}) collective-permute-start(f32[8,384]{1,0:T(8,128)S(1)} %get-tuple-element.38.refs_0_), channel_id=1, source_target_pairs={{0,2},{1,3},{2,0},{3,1},{4,6},{5,7},{6,4},{7,5},{8,10},{9,11},{10,... | collective-permute-start | bytes 36872 | tf_op jit(solution)/shard_map/ppermute | solution.py:630
  29.9 0.0 collective-permute-start
  30.0 0.0 all-to-all-done.1.parents
  30.0 0.0 copy-done.9
  30.0 0.0 copy-done.8
  30.0 3.1 %pedigree.1 = (f32[8,4096]{1,0:T(8,128)S(1)}, f32[8,8,256]{2,1,0:T(8,128)S(1)}) custom-call(f32[8,8,256]{2,1,0:T(8,128)S(1)} %all-to-all-done.1.parents, f32[8,4096]{1,0:T(8,128)S(1)} %get-tuple-element.44.new_a.refs_6_, s32[1,4096]{1,0:T(1,128)S(1)} %bitcast.18, s32[1,4096]{1,0:T(1,128)S(1)} %bitcast.19), custom_call_target="tpu_custom_call" | custom-call | tf_op jit(solution)/shard_map/pedigree/pallas_call | solution.py:734
  33.0 0.0 collective-permute-done.2.refs_3_
  33.0 0.0 collective-permute-done.1.refs_2_
  33.1 0.0 collective-permute-done.refs_1_
  33.1 0.0 copy-done.10
  33.1 4.8 %deviation.1 = (f32[8,384]{1,0:T(8,128)S(1)}, f32[8,8,1408]{2,1,0:T(8,128)}) custom-call(f32[8,384]{1,0:T(8,128)S(1)} %get-tuple-element.38.refs_0_, f32[8,384]{1,0:T(8,128)S(1)} %collective-permute-done.refs_1_, f32[8,384]{1,0:T(8,128)S(1)} %collective-permute-done.1.refs_2_, f32[8,384]{1,0:T(8,128)S(1)} %collective-permute-done.2.refs_3_, ...), custom_call_target="tpu_custom_call" | custom-call | tf_op jit(solution)/shard_map/deviation/pallas_call | solution.py:741
  37.9 5.9 %all-to-all-start.2 = ((f32[8,8,1408]{2,1,0:T(8,128)}), f32[8,8,1408]{2,1,0:T(8,128)S(1)}, u32[]{:S(2)}, u32[]{:S(2)}) async-start(f32[8,8,1408]{2,1,0:T(8,128)} %get-tuple-element.46), calls=%async_computation.2 | async-start | bytes 720896 | tf_op jit(solution)/shard_map/all_to_all | solution.py:624
  43.9 0.0 copy-done.6
  43.9 0.0 copy-done.7
  43.9 0.5 record.1.base_image
  44.4 10.8 %all-to-all-done.2.received = f32[8,8,1408]{2,1,0:T(8,128)S(1)} async-done(((f32[8,8,1408]{2,1,0:T(8,128)}), f32[8,8,1408]{2,1,0:T(8,128)S(1)}, u32[]{:S(2)}, u32[]{:S(2)}) %all-to-all-start.2) | async-done | bytes 360480 | tf_op jit(solution)/shard_map/all_to_all | solution.py:624
  55.2 0.0 copy-done.5
  55.2 0.0 copy-done.11
  55.2 1.6 %image.1 = (f32[8,4096]{1,0:T(8,128)S(1)}, f32[8,8,1280]{2,1,0:T(8,128)S(1)}) custom-call(s32[1]{0:T(128)} %bitcast.row, f32[8,8,1408]{2,1,0:T(8,128)S(1)} %all-to-all-done.2.received, s32[8,256]{1,0:T(8,128)S(1)} %bitcast.16, f32[8,4096]{1,0:T(8,128)S(1)} %record.1.base_image, f32[8,384]{1,0:T(8,128)S(1)} %get-tuple-element.48.token.deviation, ...), custom_call_target="tpu_custom_call" | custom-call | tf_op jit(solution)/shard_map/image/pallas_call | solution.py:785
  56.8 14.5 %all_to_all.20.received.refs_11_ = f32[8,8,1280]{2,1,0:T(8,128)S(1)} all-to-all(f32[8,8,1280]{2,1,0:T(8,128)S(1)} %get-tuple-element.52), channel_id=1, replica_groups=mesh['rows'=8,'mk'=4] {'rows'}, dimensions={0} | all-to-all | bytes 655360 | tf_op jit(solution)/shard_map/all_to_all | solution.py:624
  71.4 0.1 collective-permute-start.5
  71.5 0.6 collective-permute-start.4
  72.1 1.2 %collective-permute-start.3 = (f32[8,128]{1,0:T(8,128)S(1)}, f32[8,128]{1,0:T(8,128)S(1)}, u32[]{:S(2)}, u32[]{:S(2)}) collective-permute-start(f32[8,128]{1,0:T(8,128)S(1)} %spread.1.refs_0_), channel_id=1, source_target_pairs={{0,1},{1,0},{2,3},{3,2},{4,5},{5,4},{6,7},{7,6},{8,9},{9,8},{10,11... | collective-permute-start | bytes 12296 | tf_op jit(solution)/shard_map/ppermute | solution.py:630
  73.3 1.2 %collective-permute-done.5.refs_3_ = f32[8,128]{1,0:T(8,128)S(1)} collective-permute-done((f32[8,128]{1,0:T(8,128)S(1)}, f32[8,128]{1,0:T(8,128)S(1)}, u32[]{:S(2)}, u32[]{:S(2)}) %collective-permute-start.5) | collective-permute-done | bytes 4128 | tf_op jit(solution)/shard_map/ppermute | solution.py:630
  74.5 0.7 collective-permute-done.4.refs_2_
  75.1 0.0 collective-permute-done.3.refs_1_
  75.2 1.1 %final.1 = (f32[6,4096]{1,0:T(8,128)}, f32[6,12288]{1,0:T(8,128)}, f32[6,4096]{1,0:T(8,128)}, f32[6,12288]{1,0:T(8,128)}, f32[1,1]{1,0:T(1,128)}) custom-call(f32[32,8,128]{2,1,0:T(8,128)S(1)} %all-to-all-done.sums, f32[8,128]{1,0:T(8,128)S(1)} %spread.1.refs_0_, f32[8,128]{1,0:T(8,128)S(1)} %collective-permute-done.3.refs_1_, ...), custom_call_target="tpu_custom_call" | custom-call | tf_op jit(solution)/shard_map/final/pallas_call | solution.py:806
  (9 shorter events, 0.0 us)
Async XLA Ops:
  0.6 29.3 %copy-start.9 = (s32[4096]{0:T(1024)S(1)}, s32[4096]{0:T(1024)}, u32[]{:S(2)}) copy-start(s32[4096]{0:T(1024)} %param.35) | copy-start | bytes 49156
  0.6 29.3 %copy-start.8 = (s32[4096]{0:T(1024)S(1)}, s32[4096]{0:T(1024)}, u32[]{:S(2)}) copy-start(s32[4096]{0:T(1024)} %param.34) | copy-start | bytes 49156
  0.7 32.4 %copy-start.10 = (f32[6,6]{1,0:T(8,128)S(1)}, f32[6,6]{1,0:T(8,128)}, u32[]{:S(2)}) copy-start(f32[6,6]{1,0:T(8,128)} %refs_4_.2) | copy-start | bytes 436
  2.7 15.5 %all-to-all-start = ((f32[32,8,128]{2,1,0:T(8,128)}), f32[32,8,128]{2,1,0:T(8,128)S(1)}, u32[]{:S(2)}, u32[]{:S(2)}) async-start(f32[32,8,128]{2,1,0:T(8,128)} %get-tuple-element.32), calls=%async_computation | async-start | bytes 262144 | tf_op jit(solution)/shard_map/all_to_all | solution.py:624
  19.0 10.9 %all-to-all-start.1 = ((f32[8,8,256]{2,1,0:T(8,128)}), f32[8,8,256]{2,1,0:T(8,128)S(1)}, u32[]{:S(2)}, u32[]{:S(2)}) async-start(f32[8,8,256]{2,1,0:T(8,128)} %get-tuple-element.43), calls=%async_computation.1 | async-start | bytes 131072 | tf_op jit(solution)/shard_map/all_to_all | solution.py:624
  22.4 21.5 %copy-start.12 = (f32[64,6,6]{0,2,1:T(8,128)S(1)}, f32[64,6,6]{0,2,1:T(8,128)}, u32[]{:S(2)}) copy-start(f32[64,6,6]{0,2,1:T(8,128)} %param.32) | copy-start | bytes 27652
  22.4 21.5 %copy-start.6 = (f32[6,6]{1,0:T(8,128)S(1)}, f32[6,6]{1,0:T(8,128)}, u32[]{:S(2)}) copy-start(f32[6,6]{1,0:T(8,128)} %genetic.3) | copy-start | bytes 436
  22.4 21.5 %copy-start.7 = (s32[4096]{0:T(1024)S(1)}, s32[4096]{0:T(1024)}, u32[]{:S(2)}) copy-start(s32[4096]{0:T(1024)} %param.33) | copy-start | bytes 49156
  22.4 32.8 %copy-start = (f32[6,12288]{1,0:T(8,128)S(1)}, f32[6,12288]{1,0:T(8,128)}, u32[]{:S(2)}) copy-start(f32[6,12288]{1,0:T(8,128)} %refs_9_.1) | copy-start | bytes 884740
  22.4 32.8 %copy-start.1 = (f32[6,4096]{1,0:T(8,128)S(1)}, f32[6,4096]{1,0:T(8,128)}, u32[]{:S(2)}) copy-start(f32[6,4096]{1,0:T(8,128)} %refs_5_.3) | copy-start | bytes 294916
  22.5 32.8 %copy-start.4 = (s32[4096]{0:T(1024)S(1)}, s32[4096]{0:T(1024)}, u32[]{:S(2)}) copy-start(s32[4096]{0:T(1024)} %param.36) | copy-start | bytes 49156
  22.5 32.7 %copy-start.5 = (s32[1,1,8,256]{3,2,1,0:T(8,128)S(1)}, s32[1,1,8,256]{3,2,1,0:T(8,128)}, u32[]{:S(2)}) copy-start(s32[1,1,8,256]{3,2,1,0:T(8,128)} %param.37) | copy-start | bytes 24580
  22.5 32.7 %copy-start.11 = (f32[6,6]{1,0:T(8,128)S(1)}, f32[6,6]{1,0:T(8,128)}, u32[]{:S(2)}) copy-start(f32[6,6]{1,0:T(8,128)} %marker_inverse.1) | copy-start | bytes 436
  22.5 52.7 %copy-start.2 = (f32[6,12288]{1,0:T(8,128)S(1)}, f32[6,12288]{1,0:T(8,128)}, u32[]{:S(2)}) copy-start(f32[6,12288]{1,0:T(8,128)} %refs_8_.1) | copy-start | bytes 884740
  22.5 52.6 %copy-start.3 = (f32[6,4096]{1,0:T(8,128)S(1)}, f32[6,4096]{1,0:T(8,128)}, u32[]{:S(2)}) copy-start(f32[6,4096]{1,0:T(8,128)} %refs_4_.3) | copy-start | bytes 294916
  28.0 5.0 %collective-permute-start.2 = (f32[8,384]{1,0:T(8,128)S(1)}, f32[8,384]{1,0:T(8,128)S(1)}, u32[]{:S(2)}, u32[]{:S(2)}) collective-permute-start(f32[8,384]{1,0:T(8,128)S(1)} %get-tuple-element.38.refs_0_), channel_id=1, source_target_pairs={{0,3},{1,2},{2,1},{3,0},{4,7},{5,6},{6,5},{7,4},{8,11},{9,10},{10,... | collective-permute-start | bytes 36872 | tf_op jit(solution)/shard_map/ppermute | solution.py:630
  28.3 4.8 %collective-permute-start.1 = (f32[8,384]{1,0:T(8,128)S(1)}, f32[8,384]{1,0:T(8,128)S(1)}, u32[]{:S(2)}, u32[]{:S(2)}) collective-permute-start(f32[8,384]{1,0:T(8,128)S(1)} %get-tuple-element.38.refs_0_), channel_id=1, source_target_pairs={{0,2},{1,3},{2,0},{3,1},{4,6},{5,7},{6,4},{7,5},{8,10},{9,11},{10,... | collective-permute-start | bytes 36872 | tf_op jit(solution)/shard_map/ppermute | solution.py:630
  29.9 3.1 %collective-permute-start = (f32[8,384]{1,0:T(8,128)S(1)}, f32[8,384]{1,0:T(8,128)S(1)}, u32[]{:S(2)}, u32[]{:S(2)}) collective-permute-start(f32[8,384]{1,0:T(8,128)S(1)} %get-tuple-element.38.refs_0_), channel_id=1, source_target_pairs={{0,1},{1,0},{2,3},{3,2},{4,5},{5,4},{6,7},{7,6},{8,9},{9,8},{10,11... | collective-permute-start | bytes 36872 | tf_op jit(solution)/shard_map/ppermute | solution.py:630
  37.9 17.3 %all-to-all-start.2 = ((f32[8,8,1408]{2,1,0:T(8,128)}), f32[8,8,1408]{2,1,0:T(8,128)S(1)}, u32[]{:S(2)}, u32[]{:S(2)}) async-start(f32[8,8,1408]{2,1,0:T(8,128)} %get-tuple-element.46), calls=%async_computation.2 | async-start | bytes 720896 | tf_op jit(solution)/shard_map/all_to_all | solution.py:624
  71.4 3.1 %collective-permute-start.5 = (f32[8,128]{1,0:T(8,128)S(1)}, f32[8,128]{1,0:T(8,128)S(1)}, u32[]{:S(2)}, u32[]{:S(2)}) collective-permute-start(f32[8,128]{1,0:T(8,128)S(1)} %spread.1.refs_0_), channel_id=1, source_target_pairs={{0,3},{1,2},{2,1},{3,0},{4,7},{5,6},{6,5},{7,4},{8,11},{9,10},{10,... | collective-permute-start | bytes 12296 | tf_op jit(solution)/shard_map/ppermute | solution.py:630
  71.5 3.7 %collective-permute-start.4 = (f32[8,128]{1,0:T(8,128)S(1)}, f32[8,128]{1,0:T(8,128)S(1)}, u32[]{:S(2)}, u32[]{:S(2)}) collective-permute-start(f32[8,128]{1,0:T(8,128)S(1)} %spread.1.refs_0_), channel_id=1, source_target_pairs={{0,2},{1,3},{2,0},{3,1},{4,6},{5,7},{6,4},{7,5},{8,10},{9,11},{10,... | collective-permute-start | bytes 12296 | tf_op jit(solution)/shard_map/ppermute | solution.py:630
  72.1 3.0 %collective-permute-start.3 = (f32[8,128]{1,0:T(8,128)S(1)}, f32[8,128]{1,0:T(8,128)S(1)}, u32[]{:S(2)}, u32[]{:S(2)}) collective-permute-start(f32[8,128]{1,0:T(8,128)S(1)} %spread.1.refs_0_), channel_id=1, source_target_pairs={{0,1},{1,0},{2,3},{3,2},{4,5},{5,4},{6,7},{7,6},{8,9},{9,8},{10,11... | collective-permute-start | bytes 12296 | tf_op jit(solution)/shard_map/ppermute | solution.py:630

commit v5 on v4

--- a/solution.py
+++ b/solution.py
@@ -17,6 +17,7 @@
     return jax.ShapeDtypeStruct(dims, dtype)
 
 
+KEPT = 128
 LIMIT = pltpu.CompilerParams(vmem_limit_bytes=24 << 20)
 
 
@@ -310,9 +311,10 @@
 
 def chunk_copies(genotypes, buffer, semaphores):
     width = buffer.shape[2]
+    first = genotypes.shape[0] - buffer.shape[1]
     copies = [
         pltpu.make_async_copy(
-            genotypes.at[:, i * width : (i + 1) * width], buffer.at[i], semaphores.at[i]
+            genotypes.at[first:, i * width : (i + 1) * width], buffer.at[i], semaphores.at[i]
         )
         for i in range(buffer.shape[0])
     ]
@@ -346,7 +348,21 @@
     out[...] = total
 
 
-def pedigree_kernel(bits, parents, new_a, sire, dam, sampling_ref, back_ref, left_ref):
+def pedigree_kernel(
+    bits,
+    parents,
+    new_a,
+    sire,
+    dam,
+    genotypes,
+    sampling_ref,
+    back_ref,
+    resident,
+    left_ref,
+    semaphore,
+):
+    copy = pltpu.make_async_copy(genotypes.at[: resident.shape[0]], resident, semaphore)
+    copy.start()
     owners, _, base = parents.shape
     animals = new_a.shape[1]
     for h in range(0, owners, 2):
@@ -382,6 +398,7 @@
             )
             for h in range(group):
                 back_ref[g * group + h] += block_of(total, h)
+    copy.wait()
 
 
 def deviation_kernel(share, traits, columns, *refs):
@@ -393,6 +410,7 @@
     traits,
     differences,
     genomic,
+    resident,
     genotypes,
     back,
     deviation_ref,
@@ -412,16 +430,37 @@
     start = out.shape[2] - back.shape[2]
     out[:, :, start:] = back[...]
     per_chunk = buffer.shape[2] // share
+    first = resident.shape[0]
     for i, copy in enumerate(copies):
+        width = buffer.shape[2]
+        terms = dot(rounded[:, :first], resident[:, i * width : (i + 1) * width])
         copy.wait()
-        terms = dot(rounded, buffer[i])
+        terms = terms + dot(rounded[:, first:], buffer[i])
         for j in range(per_chunk):
             pack(out, i * per_chunk + j, terms[:, j * share : (j + 1) * share], traits, share)
 
 
-def record_kernel(token, sampling, new_a, pattern, table, genetic, out, matrix_ref):
-    del token
+def record_kernel(
+    bits,
+    deviation,
+    sampling,
+    new_a,
+    pattern,
+    row_index,
+    table,
+    genetic,
+    out,
+    matrix_ref,
+    table_ref,
+):
     traits = genetic.shape[0]
+    base = 1 << bits
+    table_ref[...] = jnp.zeros_like(table_ref)
+    table_ref[:, : deviation.shape[1]] = deviation[...]
+    places = table_ref.shape[1] // base
+    genomic = jnp.concatenate(
+        [parts_of(table_ref[:, h * base : (h + 1) * base]) for h in range(places)], axis=0
+    ).astype(BF16)
     patterns = table.shape[1]
     load_matrix(genetic, matrix_ref)
     values = table[...]
@@ -440,7 +479,9 @@
             row = slice(s * PAD, (s + 1) * PAD)
             block = blocks[row] + blocks[size:][row] + blocks[2 * size :][row]
             total = total + block * new[s : s + 1, :]
-        out[:, window] = total
+        index = row_index[:, window]
+        products = dot(genomic, one_hot(index & (base - 1), base))
+        out[:, window] = total + select_blocks(products, index >> bits, 0, places)
 
 
 def image_kernel(
@@ -450,8 +491,6 @@
     received,
     send,
     base_image,
-    deviation,
-    row_index,
     genetic,
     marker_inverse,
     new_a,
@@ -462,7 +501,6 @@
     out,
     matrix_ref,
     marker_ref,
-    table_ref,
     terms_ref,
     res_ref,
 ):
@@ -471,7 +509,6 @@
     base = 1 << bits
     traits = genetic.shape[0]
     animals = base_image.shape[1]
-    genotyped = deviation.shape[1]
     width = packed_width(traits, share)
     load_matrix(genetic, matrix_ref)
     load_matrix(marker_inverse, marker_ref)
@@ -490,22 +527,10 @@
             total = scatter(r, total)
     else:
         total = lax.fori_loop(0, owners, scatter, total)
-    table_ref[...] = jnp.zeros_like(table_ref)
-    table_ref[:, :genotyped] = deviation[...]
-    places = table_ref.shape[1] // base
-    table = jnp.concatenate(
-        [parts_of(table_ref[:, h * base : (h + 1) * base]) for h in range(places)], axis=0
-    ).astype(BF16)
     for h in range(blocks):
         window = slice(h * base, (h + 1) * base)
-        index = row_index[:, window]
         gathered = block_of(total, h)
-        genomic_term = select_blocks(
-            dot(table, one_hot(index & (base - 1), base)), index >> bits, 0, places
-        )
-        image_a[:, window] = (
-            base_image[:, window] + apply_matrix(matrix_ref, gathered, traits) + genomic_term
-        )
+        image_a[:, window] = base_image[:, window] + apply_matrix(matrix_ref, gathered, traits)
 
     summed = received[0, :, :width]
     for i in range(1, owners):
@@ -708,9 +733,9 @@
 
     (genotypes,) = hbm(genotypes)
 
-    def chunks(width):
+    def chunks(width, kept):
         return (
-            pltpu.VMEM((markers // width, genotyped, width), BF16),
+            pltpu.VMEM((markers // width, genotyped - kept, width), BF16),
             pltpu.SemaphoreType.DMA((markers // width,)),
         )
 
@@ -718,7 +743,7 @@
     new_marker, difference = call(
         predict_kernel,
         (marker_block, placed_block),
-        chunks(2 * chunk),
+        chunks(2 * chunk, 0),
         in_specs=[in_vmem] * 4 + [in_hbm] + [in_vmem] * 2,
         name="predict",
     )(
@@ -731,27 +756,34 @@
         direction_placed,
     )
     differences = copies_of(difference, "mk")
-    sampling, back = call(
+    sampling, back, resident = call(
         functools.partial(pedigree_kernel, bits),
-        (animal_block, slot_block),
-        (pltpu.VMEM((rows * ROWS_EACH, capacity), BF16),),
+        (animal_block, slot_block, pltpu.VMEM((KEPT, markers), BF16)),
+        (pltpu.VMEM((rows * ROWS_EACH, capacity), BF16), pltpu.SemaphoreType.DMA),
+        in_specs=[in_vmem] * 4 + [in_hbm],
         name="pedigree",
-    )(parents, new_animal, sire, dam)
+    )(parents, new_animal, sire, dam, genotypes)
     width = packed_width(traits, share)
     deviation, payload = call(
         functools.partial(deviation_kernel, share, traits, columns),
         (placed_block, shape_of(rows, PAD, width + capacity)),
-        (pltpu.VMEM((PAD, LANES), F32), *chunks(chunk)),
-        in_specs=[in_vmem] * (columns + 1) + [in_hbm, in_vmem],
+        (pltpu.VMEM((PAD, LANES), F32), *chunks(chunk, KEPT)),
+        in_specs=[in_vmem] * (columns + 2) + [in_hbm, in_vmem],
         name="deviation",
-    )(*differences, genomic_inverse, genotypes, back)
+    )(*differences, genomic_inverse, resident, genotypes, back)
     received = exchange(payload, "rows")
     residual_table, deviation = lax.optimization_barrier((residual_table, deviation))
     table = jnp.pad(jnp.transpose(residual_table, (2, 1, 0)), ((0, 0), (0, PAD - traits), (0, 0)))
     table = table.reshape(traits * PAD, patterns)
-    base_image = call(record_kernel, animal_block, (pltpu.VMEM((PAD, LANES), F32),), name="record")(
-        deviation, sampling, new_animal, kinds, table, genetic_inverse
-    )
+    base_image = call(
+        functools.partial(record_kernel, bits),
+        animal_block,
+        (
+            pltpu.VMEM((PAD, LANES), F32),
+            pltpu.VMEM((PAD, -(-genotyped // capacity) * capacity), F32),
+        ),
+        name="record",
+    )(deviation, sampling, new_animal, kinds, places, table, genetic_inverse)
 
     if share % LANES:
         start = row[0] * share
@@ -775,8 +807,6 @@
         received,
         send,
         base_image,
-        deviation,
-        places,
         genetic_inverse,
         marker_inverse,
         new_animal,
@@ -793,7 +823,6 @@
             scratch_shapes=[
                 pltpu.VMEM((PAD, LANES), F32),
                 pltpu.VMEM((PAD, LANES), F32),
-                pltpu.VMEM((PAD, -(-genotyped // capacity) * capacity), F32),
                 pltpu.VMEM((PAD, full), F32),
                 pltpu.VMEM((PAD, full), F32),
             ],

time: 76.7 us -> 75.8 us (0.988)
  no operation moved by 1% of the time
where the time goes in v5:
time: 75.8 us; the launch traced here: 75.4 us
  Pallas kernels  21.9 us (29%)
  starting transfers between devices  20.5 us (27%)
  waiting for transfers between devices  16.8 us (22%)
  blocking collectives  14.5 us (19%)
  between operations  1.55 us (2%)
    all_to_all x3, starting transfers between devices, exchange(): return lax.all_to_all(values, axes, split_axis=0, concat_axis=0, tiled=True)  16.6 us
    all_to_all x3, waiting for transfers between devices, exchange(): return lax.all_to_all(values, axes, split_axis=0, concat_axis=0, tiled=True)  15 us
    all_to_all x1, blocking collectives, exchange(): return lax.all_to_all(values, axes, split_axis=0, concat_axis=0, tiled=True)  14.5 us
    pallas_call x1, Pallas kernels, local(): call(predict_kernel, (marker_block, placed_block), chunks(2 * chunk, 0),...  5.43 us
    pallas_call x1, Pallas kernels, local(): call(functools.partial(deviation_kernel, share, traits, columns), (placed...  4.33 us
    ppermute x6, starting transfers between devices, copies_of(): lax.ppermute(values, axis, [(i, i ^ k) for i in range(size)])  3.85 us
    pallas_call x1, Pallas kernels, local(): call(functools.partial(prepare_kernel, bits, genotyped), (slot_block, slo...  3.1 us
    pallas_call x1, Pallas kernels, local(): call(functools.partial(pedigree_kernel, bits), (animal_block, slot_block,...  3.1 us
  transfers between devices with their start and end apart: 9, of which 4 were waited for; matrix products, arithmetic and copies ran while one was open for 0% of the time, Pallas kernels for 16%

profile of v5, /device:TPU:0, one launch (start us, length us, event | category | flops | bytes accessed | tf_op | source)
XLA Modules:
  0.0 75.4 jit_solution(17612078866228745816)
XLA Ops:
  0.6 0.0 copy-start.7
  0.6 0.0 copy-start.6
  0.7 2.0 %totals.1 = (f32[32,8,128]{2,1,0:T(8,128)}, f32[8,128]{1,0:T(8,128)S(1)}) custom-call(f32[6,4096]{1,0:T(8,128)} %refs_5_.1, f32[6,4096]{1,0:T(8,128)} %scal.1, f32[6,12288]{1,0:T(8,128)} %refs_9_.1, f32[6,12288]{1,0:T(8,128)} %scal_m.3), custom_call_target="tpu_custom_call" | custom-call | tf_op jit(solution)/shard_map/totals/pallas_call | solution.py:701
  2.7 7.3 %all-to-all-start = ((f32[32,8,128]{2,1,0:T(8,128)}), f32[32,8,128]{2,1,0:T(8,128)S(1)}, u32[]{:S(2)}, u32[]{:S(2)}) async-start(f32[32,8,128]{2,1,0:T(8,128)} %get-tuple-element.33), calls=%async_computation | async-start | bytes 262144 | tf_op jit(solution)/shard_map/all_to_all | solution.py:649
  10.7 3.1 %prepare.1 = (f32[8,8,256]{2,1,0:T(8,128)S(1)}, f32[8,8,256]{2,1,0:T(8,128)S(1)}, f32[8,384]{1,0:T(8,128)S(1)}, f32[8,384]{1,0:T(8,128)S(1)}, f32[8,4096]{1,0:T(...) custom-call(f32[8,128]{1,0:T(8,128)S(1)} %get-tuple-element.34.token, ...), custom_call_target="tpu_custom_call" | custom-call | tf_op jit(solution)/shard_map/prepare/pallas_call | solution.py:719
  13.8 4.4 %all-to-all-done.sums = f32[32,8,128]{2,1,0:T(8,128)S(1)} async-done(((f32[32,8,128]{2,1,0:T(8,128)}), f32[32,8,128]{2,1,0:T(8,128)S(1)}, u32[]{:S(2)}, u32[]{:S(2)}) %all-to-all-start) | async-done | bytes 131104 | tf_op jit(solution)/shard_map/all_to_all | solution.py:649
  18.2 0.8 %animals.1 = (f32[8,4096]{1,0:T(8,128)S(1)}, f32[8,8,256]{2,1,0:T(8,128)}) custom-call(f32[32,8,128]{2,1,0:T(8,128)S(1)} %all-to-all-done.sums, f32[1,1]{1,0:T(1,128)} %bitcast.12.previous, f32[8,4096]{1,0:T(8,128)S(1)} %get-tuple-element.40.search, f32[8,4096]{1,0:T(8,128)S(1)} %get-tuple-element.41.direction, ...), custom_call_target="tpu_custom_call" | custom-call | tf_op jit(solution)/shard_map/animals/pallas_call | solution.py:729
  19.0 3.4 %all-to-all-start.1 = ((f32[8,8,256]{2,1,0:T(8,128)}), f32[8,8,256]{2,1,0:T(8,128)S(1)}, u32[]{:S(2)}, u32[]{:S(2)}) async-start(f32[8,8,256]{2,1,0:T(8,128)} %get-tuple-element.44), calls=%async_computation.1 | async-start | bytes 131072 | tf_op jit(solution)/shard_map/all_to_all | solution.py:649
  22.4 0.0 copy-start.10
  22.4 5.4 %predict.1 = (f32[8,12288]{1,0:T(8,128)S(1)}, f32[8,384]{1,0:T(8,128)S(1)}) custom-call(f32[32,8,128]{2,1,0:T(8,128)S(1)} %all-to-all-done.sums, f32[1,1]{1,0:T(1,128)} %bitcast.11.previous, f32[8,12288]{1,0:T(8,128)S(1)} %get-tuple-element.35.search, f32[8,12288]{1,0:T(8,128)S(1)} %get-tuple-element.36.direction, bf16[384,12288]{1,0:T(8,128)(2,1)} %refs_6_.1, ...), custom_call_target="tpu_custom_call" | custom-call | tf_op jit(solution)/shard_map/predict/pallas_call | solution.py:743
  27.8 0.2 collective-permute-start.2
  28.1 1.7 %collective-permute-start.1 = (f32[8,384]{1,0:T(8,128)S(1)}, f32[8,384]{1,0:T(8,128)S(1)}, u32[]{:S(2)}, u32[]{:S(2)}) collective-permute-start(f32[8,384]{1,0:T(8,128)S(1)} %get-tuple-element.39.refs_0_), channel_id=1, source_target_pairs={{0,2},{1,3},{2,0},{3,1},{4,6},{5,7},{6,4},{7,5},{8,10},{9,11},{10,... | collective-permute-start | bytes 36872 | tf_op jit(solution)/shard_map/ppermute | solution.py:655
  29.7 0.0 collective-permute-start
  29.8 0.0 all-to-all-done.1.parents
  29.8 0.0 copy-done.7
  29.8 0.0 copy-done.6
  29.8 0.0 copy-start.12
  29.8 0.0 copy-start.4
  29.8 0.0 copy-start.8
  29.8 0.0 copy-start.9
  29.8 0.0 copy-start
  29.8 0.0 copy-start.1
  29.8 0.0 copy-start.5
  29.8 0.0 copy-start.11
  29.9 3.1 %pedigree.1 = (f32[8,4096]{1,0:T(8,128)S(1)}, f32[8,8,256]{2,1,0:T(8,128)S(1)}, bf16[128,12288]{1,0:T(8,128)(2,1)S(1)}) custom-call(f32[8,8,256]{2,1,0:T(8,128)S(1)} %all-to-all-done.1.parents, f32[8,4096]{1,0:T(8,128)S(1)} %get-tuple-element.45.new_a.refs_6_, s32[1,4096]{1,0:T(1,128)S(1)} %bitcast.17, s32[1,4096]{1,0:T(1,128)S(1)} %bitcast.18, ...), custom_call_target="tpu_custom_call" | custom-call | tf_op jit(solution)/shard_map/pedigree/pallas_call | solution.py:759
  33.0 0.0 copy-start.2
  33.0 0.0 copy-start.3
  33.0 0.0 collective-permute-done.2.refs_3_
  33.0 0.0 collective-permute-done.1.refs_2_
  33.0 0.0 collective-permute-done.refs_1_
  33.0 0.0 copy-done.10
  33.0 4.3 %deviation.1 = (f32[8,384]{1,0:T(8,128)S(1)}, f32[8,8,1408]{2,1,0:T(8,128)}) custom-call(f32[8,384]{1,0:T(8,128)S(1)} %get-tuple-element.39.refs_0_, f32[8,384]{1,0:T(8,128)S(1)} %collective-permute-done.refs_1_, f32[8,384]{1,0:T(8,128)S(1)} %collective-permute-done.1.refs_2_, f32[8,384]{1,0:T(8,128)S(1)} %collective-permute-done.2.refs_3_, ...), custom_call_target="tpu_custom_call" | custom-call | tf_op jit(solution)/shard_map/deviation/pallas_call | solution.py:767
  37.4 5.9 %all-to-all-start.2 = ((f32[8,8,1408]{2,1,0:T(8,128)}), f32[8,8,1408]{2,1,0:T(8,128)S(1)}, u32[]{:S(2)}, u32[]{:S(2)}) async-start(f32[8,8,1408]{2,1,0:T(8,128)} %get-tuple-element.48), calls=%async_computation.2 | async-start | bytes 720896 | tf_op jit(solution)/shard_map/all_to_all | solution.py:649
  43.3 0.0 copy-done.12
  43.4 0.0 copy-done.4
  43.4 0.7 record.1.base_image
  44.1 10.5 %all-to-all-done.2.received = f32[8,8,1408]{2,1,0:T(8,128)S(1)} async-done(((f32[8,8,1408]{2,1,0:T(8,128)}), f32[8,8,1408]{2,1,0:T(8,128)S(1)}, u32[]{:S(2)}, u32[]{:S(2)}) %all-to-all-start.2) | async-done | bytes 360480 | tf_op jit(solution)/shard_map/all_to_all | solution.py:649
  54.7 0.0 copy-done.1
  54.7 1.2 %image.1 = (f32[8,4096]{1,0:T(8,128)S(1)}, f32[8,8,1280]{2,1,0:T(8,128)S(1)}) custom-call(s32[1]{0:T(128)} %bitcast.row, f32[8,8,1408]{2,1,0:T(8,128)S(1)} %all-to-all-done.2.received, s32[8,256]{1,0:T(8,128)S(1)} %bitcast.16, f32[8,4096]{1,0:T(8,128)S(1)} %record.1.base_image, f32[6,6]{1,0:T(8,128)S(1)} %copy-done.8, f32[6,6]{1,0:T(8,128)S(1)} %copy-done.11, ...), custom_call_target="tpu_custom_call" | custom-call | tf_op jit(solution)/shard_map/image/pallas_call | solution.py:815
  55.9 14.5 %all_to_all.20.received.refs_11_ = f32[8,8,1280]{2,1,0:T(8,128)S(1)} all-to-all(f32[8,8,1280]{2,1,0:T(8,128)S(1)} %get-tuple-element.54), channel_id=1, replica_groups=mesh['rows'=8,'mk'=4] {'rows'}, dimensions={0} | all-to-all | bytes 655360 | tf_op jit(solution)/shard_map/all_to_all | solution.py:649
  70.4 0.1 collective-permute-start.5
  70.5 0.6 collective-permute-start.4
  71.1 1.2 %collective-permute-start.3 = (f32[8,128]{1,0:T(8,128)S(1)}, f32[8,128]{1,0:T(8,128)S(1)}, u32[]{:S(2)}, u32[]{:S(2)}) collective-permute-start(f32[8,128]{1,0:T(8,128)S(1)} %spread.1.refs_0_), channel_id=1, source_target_pairs={{0,1},{1,0},{2,3},{3,2},{4,5},{5,4},{6,7},{7,6},{8,9},{9,8},{10,11... | collective-permute-start | bytes 12296 | tf_op jit(solution)/shard_map/ppermute | solution.py:655
  72.4 1.2 %collective-permute-done.5.refs_3_ = f32[8,128]{1,0:T(8,128)S(1)} collective-permute-done((f32[8,128]{1,0:T(8,128)S(1)}, f32[8,128]{1,0:T(8,128)S(1)}, u32[]{:S(2)}, u32[]{:S(2)}) %collective-permute-start.5) | collective-permute-done | bytes 4128 | tf_op jit(solution)/shard_map/ppermute | solution.py:655
  73.5 0.7 collective-permute-done.4.refs_2_
  74.2 0.0 collective-permute-done.3.refs_1_
  74.2 0.0 copy-done.3
  74.2 1.1 %final.1 = (f32[6,4096]{1,0:T(8,128)}, f32[6,12288]{1,0:T(8,128)}, f32[6,4096]{1,0:T(8,128)}, f32[6,12288]{1,0:T(8,128)}, f32[1,1]{1,0:T(1,128)}) custom-call(f32[32,8,128]{2,1,0:T(8,128)S(1)} %all-to-all-done.sums, f32[8,128]{1,0:T(8,128)S(1)} %spread.1.refs_0_, f32[8,128]{1,0:T(8,128)S(1)} %collective-permute-done.3.refs_1_, ...), custom_call_target="tpu_custom_call" | custom-call | tf_op jit(solution)/shard_map/final/pallas_call | solution.py:835
  (9 shorter events, 0.0 us)
Async XLA Ops:
  0.6 29.1 %copy-start.7 = (s32[4096]{0:T(1024)S(1)}, s32[4096]{0:T(1024)}, u32[]{:S(2)}) copy-start(s32[4096]{0:T(1024)} %param.35) | copy-start | bytes 49156
  0.6 29.1 %copy-start.6 = (s32[4096]{0:T(1024)S(1)}, s32[4096]{0:T(1024)}, u32[]{:S(2)}) copy-start(s32[4096]{0:T(1024)} %param.34) | copy-start | bytes 49156
  2.7 15.5 %all-to-all-start = ((f32[32,8,128]{2,1,0:T(8,128)}), f32[32,8,128]{2,1,0:T(8,128)S(1)}, u32[]{:S(2)}, u32[]{:S(2)}) async-start(f32[32,8,128]{2,1,0:T(8,128)} %get-tuple-element.33), calls=%async_computation | async-start | bytes 262144 | tf_op jit(solution)/shard_map/all_to_all | solution.py:649
  19.0 10.7 %all-to-all-start.1 = ((f32[8,8,256]{2,1,0:T(8,128)}), f32[8,8,256]{2,1,0:T(8,128)S(1)}, u32[]{:S(2)}, u32[]{:S(2)}) async-start(f32[8,8,256]{2,1,0:T(8,128)} %get-tuple-element.44), calls=%async_computation.1 | async-start | bytes 131072 | tf_op jit(solution)/shard_map/all_to_all | solution.py:649
  22.4 10.7 %copy-start.10 = (f32[6,6]{1,0:T(8,128)S(1)}, f32[6,6]{1,0:T(8,128)}, u32[]{:S(2)}) copy-start(f32[6,6]{1,0:T(8,128)} %refs_4_.2) | copy-start | bytes 436
  27.8 5.2 %collective-permute-start.2 = (f32[8,384]{1,0:T(8,128)S(1)}, f32[8,384]{1,0:T(8,128)S(1)}, u32[]{:S(2)}, u32[]{:S(2)}) collective-permute-start(f32[8,384]{1,0:T(8,128)S(1)} %get-tuple-element.39.refs_0_), channel_id=1, source_target_pairs={{0,3},{1,2},{2,1},{3,0},{4,7},{5,6},{6,5},{7,4},{8,11},{9,10},{10,... | collective-permute-start | bytes 36872 | tf_op jit(solution)/shard_map/ppermute | solution.py:655
  28.1 5.0 %collective-permute-start.1 = (f32[8,384]{1,0:T(8,128)S(1)}, f32[8,384]{1,0:T(8,128)S(1)}, u32[]{:S(2)}, u32[]{:S(2)}) collective-permute-start(f32[8,384]{1,0:T(8,128)S(1)} %get-tuple-element.39.refs_0_), channel_id=1, source_target_pairs={{0,2},{1,3},{2,0},{3,1},{4,6},{5,7},{6,4},{7,5},{8,10},{9,11},{10,... | collective-permute-start | bytes 36872 | tf_op jit(solution)/shard_map/ppermute | solution.py:655
  29.7 3.3 %collective-permute-start = (f32[8,384]{1,0:T(8,128)S(1)}, f32[8,384]{1,0:T(8,128)S(1)}, u32[]{:S(2)}, u32[]{:S(2)}) collective-permute-start(f32[8,384]{1,0:T(8,128)S(1)} %get-tuple-element.39.refs_0_), channel_id=1, source_target_pairs={{0,1},{1,0},{2,3},{3,2},{4,5},{5,4},{6,7},{7,6},{8,9},{9,8},{10,11... | collective-permute-start | bytes 36872 | tf_op jit(solution)/shard_map/ppermute | solution.py:655
  29.8 13.6 %copy-start.12 = (f32[64,6,6]{0,2,1:T(8,128)S(1)}, f32[64,6,6]{0,2,1:T(8,128)}, u32[]{:S(2)}) copy-start(f32[64,6,6]{0,2,1:T(8,128)} %param.32) | copy-start | bytes 27652
  29.8 13.6 %copy-start.4 = (s32[4096]{0:T(1024)S(1)}, s32[4096]{0:T(1024)}, u32[]{:S(2)}) copy-start(s32[4096]{0:T(1024)} %param.36) | copy-start | bytes 49156
  29.8 13.6 %copy-start.8 = (f32[6,6]{1,0:T(8,128)S(1)}, f32[6,6]{1,0:T(8,128)}, u32[]{:S(2)}) copy-start(f32[6,6]{1,0:T(8,128)} %genetic.3) | copy-start | bytes 436
  29.8 13.6 %copy-start.9 = (s32[4096]{0:T(1024)S(1)}, s32[4096]{0:T(1024)}, u32[]{:S(2)}) copy-start(s32[4096]{0:T(1024)} %param.33) | copy-start | bytes 49156
  29.8 24.9 %copy-start = (f32[6,12288]{1,0:T(8,128)S(1)}, f32[6,12288]{1,0:T(8,128)}, u32[]{:S(2)}) copy-start(f32[6,12288]{1,0:T(8,128)} %refs_9_.1) | copy-start | bytes 884740
  29.8 24.9 %copy-start.1 = (f32[6,4096]{1,0:T(8,128)S(1)}, f32[6,4096]{1,0:T(8,128)}, u32[]{:S(2)}) copy-start(f32[6,4096]{1,0:T(8,128)} %refs_5_.1) | copy-start | bytes 294916
  29.8 24.8 %copy-start.5 = (s32[1,1,8,256]{3,2,1,0:T(8,128)S(1)}, s32[1,1,8,256]{3,2,1,0:T(8,128)}, u32[]{:S(2)}) copy-start(s32[1,1,8,256]{3,2,1,0:T(8,128)} %param.37) | copy-start | bytes 24580
  29.8 24.8 %copy-start.11 = (f32[6,6]{1,0:T(8,128)S(1)}, f32[6,6]{1,0:T(8,128)}, u32[]{:S(2)}) copy-start(f32[6,6]{1,0:T(8,128)} %marker_inverse.1) | copy-start | bytes 436
  33.0 41.2 %copy-start.2 = (f32[6,12288]{1,0:T(8,128)S(1)}, f32[6,12288]{1,0:T(8,128)}, u32[]{:S(2)}) copy-start(f32[6,12288]{1,0:T(8,128)} %refs_8_.1) | copy-start | bytes 884740
  33.0 41.2 %copy-start.3 = (f32[6,4096]{1,0:T(8,128)S(1)}, f32[6,4096]{1,0:T(8,128)}, u32[]{:S(2)}) copy-start(f32[6,4096]{1,0:T(8,128)} %refs_4_.3) | copy-start | bytes 294916
  37.4 17.3 %all-to-all-start.2 = ((f32[8,8,1408]{2,1,0:T(8,128)}), f32[8,8,1408]{2,1,0:T(8,128)S(1)}, u32[]{:S(2)}, u32[]{:S(2)}) async-start(f32[8,8,1408]{2,1,0:T(8,128)} %get-tuple-element.48), calls=%async_computation.2 | async-start | bytes 720896 | tf_op jit(solution)/shard_map/all_to_all | solution.py:649
  70.4 3.1 %collective-permute-start.5 = (f32[8,128]{1,0:T(8,128)S(1)}, f32[8,128]{1,0:T(8,128)S(1)}, u32[]{:S(2)}, u32[]{:S(2)}) collective-permute-start(f32[8,128]{1,0:T(8,128)S(1)} %spread.1.refs_0_), channel_id=1, source_target_pairs={{0,3},{1,2},{2,1},{3,0},{4,7},{5,6},{6,5},{7,4},{8,11},{9,10},{10,... | collective-permute-start | bytes 12296 | tf_op jit(solution)/shard_map/ppermute | solution.py:655
  70.5 3.7 %collective-permute-start.4 = (f32[8,128]{1,0:T(8,128)S(1)}, f32[8,128]{1,0:T(8,128)S(1)}, u32[]{:S(2)}, u32[]{:S(2)}) collective-permute-start(f32[8,128]{1,0:T(8,128)S(1)} %spread.1.refs_0_), channel_id=1, source_target_pairs={{0,2},{1,3},{2,0},{3,1},{4,6},{5,7},{6,4},{7,5},{8,10},{9,11},{10,... | collective-permute-start | bytes 12296 | tf_op jit(solution)/shard_map/ppermute | solution.py:655
  71.1 3.1 %collective-permute-start.3 = (f32[8,128]{1,0:T(8,128)S(1)}, f32[8,128]{1,0:T(8,128)S(1)}, u32[]{:S(2)}, u32[]{:S(2)}) collective-permute-start(f32[8,128]{1,0:T(8,128)S(1)} %spread.1.refs_0_), channel_id=1, source_target_pairs={{0,1},{1,0},{2,3},{3,2},{4,5},{5,4},{6,7},{7,6},{8,9},{9,8},{10,11... | collective-permute-start | bytes 12296 | tf_op jit(solution)/shard_map/ppermute | solution.py:655
